TPU v7x, 32 devices: a whole 2x2x4 slice. The times are simulated.
32 devices in a mesh: dp: 8 (over y, x, core), tensor: 4 (over z).
Axes of the slice: x: 2, y: 2, z: 4, core: 2. Of those that a mesh axis runs over, the one named last changes fastest.
Arguments:
- tokens: bfloat16 [8192, 1536], P(('dp', 'tensor')), may hold values from -6 to 6
- segments: int32 [8, 1024], P('dp'), may hold values from -1 to 17, as said below
- granularity: int32 [8], P('dp'), may hold values from 1 to 4
- norm1_gain: float32 [1536], replicated, may hold values from 0.5 to 1.5
- norm2_gain: float32 [1536], replicated, may hold values from 0.5 to 1.5
- w_query: bfloat16 [1536, 1536], P(None, 'tensor'), may hold values from -0.15625 to 0.15625
- w_key: bfloat16 [1536, 1536], P(None, 'tensor'), may hold values from -0.15625 to 0.15625
- w_value: bfloat16 [1536, 1536], P(None, 'tensor'), may hold values from -0.15625 to 0.15625
- w_out: bfloat16 [1536, 1536], P('tensor'), may hold values from -0.625 to 0.625
- w_gate: bfloat16 [1536, 6144], P(None, 'tensor'), may hold values from -0.15625 to 0.15625
- w_up: bfloat16 [1536, 6144], P(None, 'tensor'), may hold values from -0.15625 to 0.15625
- w_down: bfloat16 [6144, 1536], P('tensor'), may hold values from -0.15625 to 0.15625
- cotangent: bfloat16 [8192, 1536], P(('dp', 'tensor')), may hold values from -6 to 6
Outputs:
- output: bfloat16 [8192, 1536], P(('dp', 'tensor'))
- grad_tokens: bfloat16 [8192, 1536], P(('dp', 'tensor'))
- grad_norm1: float32 [1536], replicated
- grad_norm2: float32 [1536], replicated
- grad_query: float32 [1536, 1536], P('dp', 'tensor')
- grad_key: float32 [1536, 1536], P('dp', 'tensor')
- grad_value: float32 [1536, 1536], P('dp', 'tensor')
- grad_out: float32 [1536, 1536], P('tensor', 'dp')
- grad_gate: float32 [1536, 6144], P('dp', 'tensor')
- grad_up: float32 [1536, 6144], P('dp', 'tensor')
- grad_down: float32 [6144, 1536], P('tensor', 'dp')
Inputs may be any that keep to these rules, and one draw needn't show every extreme that they name: `segments`: in each packed sequence ids start at 0 and never fall, a document is a run of equal ids, every sequence holds exactly 18 documents, and the sequence ends in 1 to 128 padding tokens of id -1.
All inputs are finite; a program needn't handle non-finite values.
Results may differ from a plain program's by a relative error of at most 0.017.
Values may be sent and summed in bfloat16 or wider, within the bound.
A program may use at most 192 MiB of HBM per device.

v0:
```python
import jax
import jax.numpy as jnp
from jax import lax
from jax.sharding import PartitionSpec as P

HD = 128
FF = 6144


EPS = 1e-06
NEG = -1e30


def norm_rows(values, row_gain):
    factor = lax.rsqrt(jnp.mean(values * values, axis=-1, keepdims=True) + EPS)
    return (values * factor * row_gain, factor)


def norm_back(values, factor, row_gain, gradient):
    scaled = gradient * row_gain
    inner_mean = jnp.mean(scaled * values, axis=-1, keepdims=True)
    back_rows = factor * scaled - values * (factor * factor * factor) * inner_mean
    return (back_rows, jnp.sum(gradient * values * factor, axis=0))


def rope_tables(length, head_size):
    half_size = head_size // 2
    frequency = 10000.0 ** (-jnp.arange(half_size, dtype=jnp.float32) / half_size)
    angles = jnp.arange(length, dtype=jnp.float32)[:, None] * frequency[None, :]
    return (jnp.cos(angles)[:, None, :], jnp.sin(angles)[:, None, :])


def rotate(values, cosine, sine_table):
    half_size = values.shape[-1] // 2
    lower_half = values[..., :half_size]
    upper_half = values[..., half_size:]
    return jnp.concatenate(
        [
            lower_half * cosine - upper_half * sine_table,
            upper_half * cosine + lower_half * sine_table,
        ],
        axis=-1,
    )


def rotate_back(gradient, cosine, sine_table):
    half_size = gradient.shape[-1] // 2
    lower_half = gradient[..., :half_size]
    upper_half = gradient[..., half_size:]
    return jnp.concatenate(
        [
            lower_half * cosine + upper_half * sine_table,
            upper_half * cosine - lower_half * sine_table,
        ],
        axis=-1,
    )


def block_logits(query_block, keys_all, row_start, query_ids, key_ids):
    raw_scores = jnp.einsum(
        "qhd,khd->hqk", query_block, keys_all, preferred_element_type=jnp.float32
    )
    query_pos = row_start + jnp.arange(query_block.shape[0])[:, None]
    key_pos = jnp.arange(keys_all.shape[0])[None, :]
    allowed = (key_pos <= query_pos) & (query_ids[:, None] == key_ids[None, :])
    return jnp.where(allowed[None], raw_scores * query_block.shape[-1] ** (-0.5), NEG)


def attend_forward(query_rot, key_rot, value_low, seg_ids):
    seq_len = query_rot.shape[1]
    block_rows = min(512, seq_len)
    num_blocks = seq_len // block_rows

    def one_sequence(inputs):
        queries, keys_all, values_all, key_ids = inputs

        def one_block(block_index):
            row_start = block_index * block_rows
            query_block = lax.dynamic_slice_in_dim(queries, row_start, block_rows, 0)
            query_ids = lax.dynamic_slice_in_dim(key_ids, row_start, block_rows, 0)
            logits = block_logits(query_block, keys_all, row_start, query_ids, key_ids)
            row_max = jnp.max(logits, axis=-1, keepdims=True)
            expo = jnp.exp(logits - row_max)
            row_total = jnp.sum(expo, axis=-1, keepdims=True)
            weights_low = (expo / row_total).astype(jnp.bfloat16)
            attended = jnp.einsum(
                "hqk,khd->qhd", weights_low, values_all, preferred_element_type=jnp.float32
            )
            return (attended, (row_max + jnp.log(row_total))[..., 0])

        attended, log_totals = lax.map(one_block, jnp.arange(num_blocks))
        return (attended.reshape(seq_len, attended.shape[2], attended.shape[3]), log_totals)

    return lax.map(one_sequence, (query_rot, key_rot, value_low, seg_ids))


def attend_backward(query_rot, key_rot, value_low, grad_low, log_totals, seg_ids):
    seq_len = query_rot.shape[1]
    block_rows = min(512, seq_len)
    num_blocks = seq_len // block_rows

    def one_sequence(inputs):
        queries, keys_all, values_all, grads_all, totals_all, key_ids = inputs

        def one_block(carry, block_index):
            key_acc, value_acc = carry
            row_start = block_index * block_rows
            query_block = lax.dynamic_slice_in_dim(queries, row_start, block_rows, 0)
            grad_block = lax.dynamic_slice_in_dim(grads_all, row_start, block_rows, 0)
            query_ids = lax.dynamic_slice_in_dim(key_ids, row_start, block_rows, 0)
            log_block = totals_all[block_index]
            logits = block_logits(query_block, keys_all, row_start, query_ids, key_ids)
            probs = jnp.exp(logits - log_block[..., None])
            probs_low = probs.astype(jnp.bfloat16)
            grad_probs = jnp.einsum(
                "qhd,khd->hqk", grad_block, values_all, preferred_element_type=jnp.float32
            )
            delta = jnp.sum(probs * grad_probs, axis=-1, keepdims=True)
            grad_logits = (probs * (grad_probs - delta) * queries.shape[-1] ** (-0.5)).astype(
                jnp.bfloat16
            )
            grad_query = jnp.einsum(
                "hqk,khd->qhd", grad_logits, keys_all, preferred_element_type=jnp.float32
            )
            key_acc = key_acc + jnp.einsum(
                "hqk,qhd->khd", grad_logits, query_block, preferred_element_type=jnp.float32
            )
            value_acc = value_acc + jnp.einsum(
                "hqk,qhd->khd", probs_low, grad_block, preferred_element_type=jnp.float32
            )
            return ((key_acc, value_acc), grad_query)

        zero_acc = jnp.zeros(keys_all.shape, jnp.float32)
        (key_grad, value_grad), query_grad = lax.scan(
            one_block, (zero_acc, zero_acc), jnp.arange(num_blocks)
        )
        return (
            query_grad.reshape(seq_len, query_grad.shape[2], query_grad.shape[3]),
            key_grad,
            value_grad,
        )

    return lax.map(one_sequence, (query_rot, key_rot, value_low, grad_low, log_totals, seg_ids))


def contract_rows(left, right):
    return lax.dot_general(
        left, right, (((0,), (0,)), ((), ())), preferred_element_type=jnp.float32
    )


def contract_cols(left, right):
    return lax.dot_general(
        left, right, (((1,), (1,)), ((), ())), preferred_element_type=jnp.float32
    )


def on_device(
    tokens,
    segments,
    granularity,
    norm1_gain,
    norm2_gain,
    w_query,
    w_key,
    w_value,
    w_out,
    w_gate,
    w_up,
    w_down,
    cotangent,
):
    seq_count, seq_len = segments.shape
    head_size = HD
    heads_here = w_query.shape[1] // head_size
    group_rows = seq_count * seq_len
    own_rows = tokens.shape[0]
    width_here = w_gate.shape[1]
    tensor_rank = lax.axis_index("tensor")
    cosine, sine_table = rope_tables(seq_len, head_size)

    def heads_view(matrix):
        return matrix.reshape(seq_count, seq_len, heads_here, head_size)

    inputs_f = tokens.astype(jnp.float32)
    normed_one, factor_one = norm_rows(inputs_f, norm1_gain)
    rows_one = lax.all_gather(normed_one.astype(jnp.bfloat16), "tensor", axis=0, tiled=True)
    query_f = jnp.dot(rows_one, w_query, preferred_element_type=jnp.float32)
    key_f = jnp.dot(rows_one, w_key, preferred_element_type=jnp.float32)
    value_f = jnp.dot(rows_one, w_value, preferred_element_type=jnp.float32)
    query_rot = rotate(heads_view(query_f), cosine, sine_table).astype(jnp.bfloat16)
    key_rot = rotate(heads_view(key_f), cosine, sine_table).astype(jnp.bfloat16)
    value_low = heads_view(value_f).astype(jnp.bfloat16)
    attended, log_totals = attend_forward(query_rot, key_rot, value_low, segments)
    attended_low = attended.reshape(group_rows, heads_here * head_size).astype(jnp.bfloat16)
    hidden_f = inputs_f + lax.psum_scatter(
        jnp.dot(attended_low, w_out, preferred_element_type=jnp.float32),
        "tensor",
        scatter_dimension=0,
        tiled=True,
    )
    normed_two, factor_two = norm_rows(hidden_f, norm2_gain)
    rows_two = lax.all_gather(normed_two.astype(jnp.bfloat16), "tensor", axis=0, tiled=True)
    gate_f = jnp.dot(rows_two, w_gate, preferred_element_type=jnp.float32)
    up_f = jnp.dot(rows_two, w_up, preferred_element_type=jnp.float32)
    unit_ids = tensor_rank * width_here + jnp.arange(width_here)
    seq_width = FF // 8 * 2 ** (granularity - 1)
    token_width = jnp.broadcast_to(seq_width[:, None], (seq_count, seq_len)).reshape(group_rows)
    unit_mask = (unit_ids[None, :] < token_width[:, None]).astype(jnp.float32)
    sigma = jax.nn.sigmoid(gate_f)
    activated = gate_f * sigma
    inner_low = (activated * up_f * unit_mask).astype(jnp.bfloat16)
    output_f = hidden_f + lax.psum_scatter(
        jnp.dot(inner_low, w_down, preferred_element_type=jnp.float32).astype(jnp.bfloat16),
        "tensor",
        scatter_dimension=0,
        tiled=True,
    ).astype(jnp.float32)
    flat_ids = segments.reshape(group_rows)
    own_ids = lax.dynamic_slice_in_dim(flat_ids, tensor_rank * own_rows, own_rows, 0)
    grad_out_f = cotangent.astype(jnp.float32) * (own_ids >= 0).astype(jnp.float32)[:, None]
    grad_rows_two = lax.all_gather(grad_out_f.astype(jnp.bfloat16), "tensor", axis=0, tiled=True)
    grad_inner = contract_cols(grad_rows_two, w_down)
    grad_down = contract_rows(inner_low, grad_rows_two)
    grad_gate_low = (grad_inner * unit_mask * up_f * sigma * (1.0 + gate_f * (1.0 - sigma))).astype(
        jnp.bfloat16
    )
    grad_up_low = (grad_inner * unit_mask * activated).astype(jnp.bfloat16)
    grad_gate = contract_rows(rows_two, grad_gate_low)
    grad_up = contract_rows(rows_two, grad_up_low)
    grad_normed_two = lax.psum_scatter(
        contract_cols(grad_gate_low, w_gate) + contract_cols(grad_up_low, w_up),
        "tensor",
        scatter_dimension=0,
        tiled=True,
    )
    back_two, gain_two = norm_back(hidden_f, factor_two, norm2_gain, grad_normed_two)
    grad_hidden = grad_out_f + back_two
    grad_rows_one = lax.all_gather(grad_hidden.astype(jnp.bfloat16), "tensor", axis=0, tiled=True)
    grad_wout = contract_rows(attended_low, grad_rows_one)
    grad_attended = contract_cols(grad_rows_one, w_out).astype(jnp.bfloat16)
    query_grad, key_grad, value_grad = attend_backward(
        query_rot, key_rot, value_low, heads_view(grad_attended), log_totals, segments
    )
    grad_query_low = (
        rotate_back(query_grad, cosine, sine_table)
        .reshape(group_rows, heads_here * head_size)
        .astype(jnp.bfloat16)
    )
    grad_key_low = (
        rotate_back(key_grad, cosine, sine_table)
        .reshape(group_rows, heads_here * head_size)
        .astype(jnp.bfloat16)
    )
    grad_value_low = value_grad.reshape(group_rows, heads_here * head_size).astype(jnp.bfloat16)
    grad_wq = contract_rows(rows_one, grad_query_low)
    grad_wk = contract_rows(rows_one, grad_key_low)
    grad_wv = contract_rows(rows_one, grad_value_low)
    grad_normed_one = lax.psum_scatter(
        (
            contract_cols(grad_query_low, w_query)
            + contract_cols(grad_key_low, w_key)
            + contract_cols(grad_value_low, w_value)
        ).astype(jnp.bfloat16),
        "tensor",
        scatter_dimension=0,
        tiled=True,
    ).astype(jnp.float32)
    back_one, gain_one = norm_back(inputs_f, factor_one, norm1_gain, grad_normed_one)
    grad_tokens = (grad_hidden + back_one).astype(jnp.bfloat16)
    gain_one, gain_two = lax.psum((gain_one, gain_two), ("dp", "tensor"))
    weight_grads = tuple(
        (
            lax.psum_scatter(grad_wq, "dp", scatter_dimension=0, tiled=True),
            lax.psum_scatter(grad_wk, "dp", scatter_dimension=0, tiled=True),
            lax.psum_scatter(grad_wv, "dp", scatter_dimension=0, tiled=True),
            lax.psum_scatter(grad_wout, "dp", scatter_dimension=1, tiled=True),
            lax.psum_scatter(grad_gate, "dp", scatter_dimension=0, tiled=True),
            lax.psum_scatter(grad_up, "dp", scatter_dimension=0, tiled=True),
            lax.psum_scatter(grad_down, "dp", scatter_dimension=1, tiled=True),
        )
    )
    return (output_f.astype(jnp.bfloat16), grad_tokens, gain_one, gain_two) + weight_grads


def solution(mesh):
    in_specs = (
        P(("dp", "tensor"), None),
        P("dp", None),
        P("dp"),
        P(),
        P(),
        P(None, "tensor"),
        P(None, "tensor"),
        P(None, "tensor"),
        P("tensor", None),
        P(None, "tensor"),
        P(None, "tensor"),
        P("tensor", None),
        P(("dp", "tensor"), None),
    )
    out_specs = (
        P(("dp", "tensor"), None),
        P(("dp", "tensor"), None),
        P(),
        P(),
        P("dp", "tensor"),
        P("dp", "tensor"),
        P("dp", "tensor"),
        P("tensor", "dp"),
        P("dp", "tensor"),
        P("dp", "tensor"),
        P("tensor", "dp"),
    )
    return jax.shard_map(
        on_device, mesh=mesh, in_specs=in_specs, out_specs=out_specs, check_vma=False
    )
```

profile of v0, /device:TPU:0, one launch (start us, length us, event | category | flops | bytes accessed | tf_op | source)
XLA Modules:
  0.0 1253.0 jit_solution(9171922235454918241)
XLA Ops:
  14.6 63.5 %all-gather.5.cloned.1.call-done = bf16[1024,1536]{1,0:T(8,128)(2,1)} async-done(((bf16[256,1536]{1,0:T(8,128)(2,1)}), bf16[1024,1536]{1,0:T(8,128)(2,1)}) %all-gather.5.cloned.1.call-update) | async-done | bytes 3145744 | tf_op jit(solution)/shard_map/all_gather | solution.py:187
  106.0 18.4 %while.47 = (s32[]{:T(128)}, bf16[2,512,3,128]{3,1,2,0:T(8,128)(2,1)}, f32[2,3,512]{2,1,0:T(4,128)}, s32[2]{0:T(128)S(1)}, s32[1024]{0:T(1024)S(1)}, /*index=5*/...) while((s32[]{:T(128)}, ...), condition=%wide.region_4.5_spmd, body=%wide.region_1.4_spmd.sunk | while | flops 825752576 | bytes 30187836 | solution.py:91
  134.7 109.5 %reduce-scatter.12.cloned.1.call-done = f32[256,1536]{1,0:T(8,128)} async-done(((f32[1024,1536]{1,0:T(8,128)}), f32[256,1536]{1,0:T(8,128)}) %reduce-scatter.12.cloned.1.call-update) | async-done | bytes 1572880 | tf_op jit(solution)/shard_map/reduce_scatter | solution.py:196
  252.6 60.0 %all-gather.7.cloned.1.call-done = bf16[1024,1536]{1,0:T(8,128)(2,1)} async-done(((bf16[256,1536]{1,0:T(8,128)(2,1)}), bf16[1024,1536]{1,0:T(8,128)(2,1)}) %all-gather.7.cloned.1.call-update) | async-done | bytes 3145744 | tf_op jit(solution)/shard_map/all_gather | solution.py:203
  331.7 45.0 %all-gather.9.cloned.1.call-done = bf16[1024,1536]{1,0:T(8,128)(2,1)} async-done(((bf16[256,1536]{1,0:T(8,128)(2,1)}), bf16[1024,1536]{1,0:T(8,128)(2,1)}) %all-gather.9.cloned.1.call-update) | async-done | bytes 3145744 | tf_op jit(solution)/shard_map/all_gather | solution.py:222
  376.8 13.0 %multiply_convert_fusion.1 = (bf16[1024,1536]{1,0:T(8,128)(2,1)S(1)}, bf16[1024,1536]{1,0:T(8,128)(2,1)S(1)}, bf16[1024,1536]{1,0:T(8,128)(2,1)}) fusion(pred[1536]{0:T(1024)(128)(4,1)} %add_compare_fusion, f32[1024,1536]{1,0:T(8,128)} %fusion.102, f32[1024,1536]{1,0:T(8,128)} %fusion.103, bf16[1024,1536]{1,0:T(8,128)(2,1)} %all-gather.9.cloned.1.call-done, ...), kind=kOutput, calls=%fused_computation.65 | convolution fusion | flops 4858576896 | bytes 29885952 | tf_op jit(solution)/shard_map/dot_general | solution.py:153
  417.6 99.9 %reduce-scatter.16.cloned.1.call-done = f32[256,1536]{1,0:T(8,128)} async-done(((f32[1024,1536]{1,0:T(8,128)}), f32[256,1536]{1,0:T(8,128)}) %reduce-scatter.16.cloned.1.call-update) | async-done | bytes 1572880 | tf_op jit(solution)/shard_map/reduce_scatter | solution.py:231
  521.0 59.5 %reduce-scatter.14.cloned.1.call-done = bf16[256,1536]{1,0:T(8,128)(2,1)} async-done(((bf16[1024,1536]{1,0:T(8,128)(2,1)}), bf16[256,1536]{1,0:T(8,128)(2,1)}) %reduce-scatter.14.cloned.1.call-update) | async-done | bytes 786448 | tf_op jit(solution)/shard_map/reduce_scatter | solution.py:213
  585.3 63.6 %all-gather.11.cloned.1.call-done = bf16[1024,1536]{1,0:T(8,128)(2,1)} async-done(((bf16[256,1536]{1,0:T(8,128)(2,1)}), bf16[1024,1536]{1,0:T(8,128)(2,1)}) %all-gather.11.cloned.1.call-update) | async-done | bytes 3145744 | tf_op jit(solution)/shard_map/all_gather | solution.py:239
  653.1 87.2 %while.48 = (s32[]{:T(128)}, f32[1024,3,128]{0,2,1:T(8,128)}, f32[1024,3,128]{0,2,1:T(8,128)}, f32[2,512,3,128]{3,1,0,2:T(8,128)}, s32[2]{0:T(128)S(1)}, /*index...) while((s32[]{:T(128)}, f32[1024,3,128]{0,2,1:T(8,128)}, ...), condition=%wide.region_12.13_spmd.clone, body=%wide.region_10.12_spmd.clone.sunk | while | flops 2057311744 | bytes 111741272 | solution.py:134
  665.5 15.6 %bitcast_add_fusion.4 = f32[1024,3,128]{0,2,1:T(8,128)} fusion(f32[1024,3,128]{0,2,1:T(8,128)} %get-tuple-element.513, f32[3,512,1024]{2,1,0:T(8,128)} %fusion.197, f32[3,512,1024]{2,1,0:T(8,128)} %copy-done.2, f32[3,512]{1,0:T(4,128)S(1)} %dynamic-slice_bitcast_fusion.2, pred[512,1024]{1,0:T(8,128)(4,1)S(1)} %fusion.199, pred[]{:T(512)S(6)} %compare.3, ...), kind=kOutput, calls=%fused_computation.41.clone.1 | convolution fusion | flops 420743680 | bytes 29769732 | tf_op jit(solution)/shard_map/while/body/eval_jaxpr/while/body/eval_jaxpr/hqk,qhd->khd/dot_general | solution.py:125
  681.1 14.0 %fusion.200 = f32[2,512,3,128]{3,1,0,2:T(8,128)} fusion(f32[2,512,3,128]{3,1,0,2:T(8,128)} %get-tuple-element.515, s32[]{:T(128)S(6)} %copy.91, bf16[1024,3,128]{2,0,1:T(8,128)(2,1)S(1)} %get-tuple-element.535, f32[3,512,1024]{2,1,0:T(8,128)} %fusion.197, f32[3,512,1024]{2,1,0:T(8,128)} %copy-done.2, f32[3,512]{1,0:T(4,128)S(1)} %dynamic-slice_bitcast_fusion.2, ...), kind=kOutput, calls=%fused_computation.43.clone.1 | convolution fusion | flops 419957248 | bytes 27803652 | tf_op jit(solution)/shard_map/while/body/eval_jaxpr/while/body/eval_jaxpr/hqk,khd->qhd/dot_general | solution.py:122
  710.1 16.0 %bitcast_add_fusion.4 = f32[1024,3,128]{0,2,1:T(8,128)} fusion(f32[1024,3,128]{0,2,1:T(8,128)} %get-tuple-element.513, f32[3,512,1024]{2,1,0:T(8,128)} %fusion.197, f32[3,512,1024]{2,1,0:T(8,128)} %copy-done.2, f32[3,512]{1,0:T(4,128)S(1)} %dynamic-slice_bitcast_fusion.2, pred[512,1024]{1,0:T(8,128)(4,1)S(1)} %fusion.199, pred[]{:T(512)S(6)} %compare.3, ...), kind=kOutput, calls=%fused_computation.41.clone.1 | convolution fusion | flops 420743680 | bytes 29769732 | tf_op jit(solution)/shard_map/while/body/eval_jaxpr/while/body/eval_jaxpr/hqk,qhd->khd/dot_general | solution.py:125
  726.1 14.0 %fusion.200 = f32[2,512,3,128]{3,1,0,2:T(8,128)} fusion(f32[2,512,3,128]{3,1,0,2:T(8,128)} %get-tuple-element.515, s32[]{:T(128)S(6)} %copy.91, bf16[1024,3,128]{2,0,1:T(8,128)(2,1)S(1)} %get-tuple-element.535, f32[3,512,1024]{2,1,0:T(8,128)} %fusion.197, f32[3,512,1024]{2,1,0:T(8,128)} %copy-done.2, f32[3,512]{1,0:T(4,128)S(1)} %dynamic-slice_bitcast_fusion.2, ...), kind=kOutput, calls=%fused_computation.43.clone.1 | convolution fusion | flops 419957248 | bytes 27803652 | tf_op jit(solution)/shard_map/while/body/eval_jaxpr/while/body/eval_jaxpr/hqk,khd->qhd/dot_general | solution.py:122
  769.0 10.3 fusion.112
  779.4 10.0 fusion.111
  820.2 40.8 %all-reduce = (f32[1536]{0:T(1024)}, f32[1536]{0:T(1024)}) all-reduce(f32[1536]{0:T(1024)} %get-tuple-element.264, f32[1536]{0:T(1024)S(1)} %copy-done.23), channel_id=1, replica_groups=mesh['dp'=8,'tensor'=4] {'dp','tensor'}, use_global_device_ids=true, to_apply=%region_16.17 | all-reduce | flops 3072 | bytes 24576 | tf_op jit(solution)/shard_map/psum | solution.py:271
  864.3 35.0 %reduce-scatter.32.cloned.1.call-done = f32[1536,192]{0,1:T(8,128)} async-done(((f32[1536,1536]{0,1:T(8,128)}), f32[1536,192]{0,1:T(8,128)}) %reduce-scatter.32.cloned.1.call-update) | async-done | bytes 1179664 | tf_op jit(solution)/shard_map/reduce_scatter | solution.py:280
  899.2 80.4 %reduce-scatter.30.cloned.1.call-done = f32[192,1536]{1,0:T(8,128)} async-done(((f32[1536,1536]{1,0:T(8,128)}), f32[192,1536]{1,0:T(8,128)}) %reduce-scatter.30.cloned.1.call-update) | async-done | bytes 1179664 | tf_op jit(solution)/shard_map/reduce_scatter | solution.py:279
  979.7 80.6 %reduce-scatter.28.cloned.1.call-done = f32[192,1536]{1,0:T(8,128)} async-done(((f32[1536,1536]{1,0:T(8,128)}), f32[192,1536]{1,0:T(8,128)}) %reduce-scatter.28.cloned.1.call-update) | async-done | bytes 1179664 | tf_op jit(solution)/shard_map/reduce_scatter | solution.py:278
  1060.3 46.3 %reduce-scatter.26.cloned.1.call-done = f32[384,192]{0,1:T(8,128)} async-done(((f32[384,1536]{0,1:T(8,128)}), f32[384,192]{0,1:T(8,128)}) %reduce-scatter.26.cloned.1.call-update) | async-done | bytes 294928 | tf_op jit(solution)/shard_map/reduce_scatter | solution.py:277
  1106.6 46.8 %reduce-scatter.20.cloned.1.call-done = f32[192,384]{1,0:T(8,128)} async-done(((f32[1536,384]{1,0:T(8,128)}), f32[192,384]{1,0:T(8,128)}) %reduce-scatter.20.cloned.1.call-update) | async-done | bytes 294928 | tf_op jit(solution)/shard_map/reduce_scatter | solution.py:274
  1153.4 46.3 %reduce-scatter.24.cloned.1.call-done = f32[192,384]{1,0:T(8,128)} async-done(((f32[1536,384]{1,0:T(8,128)}), f32[192,384]{1,0:T(8,128)}) %reduce-scatter.24.cloned.1.call-update) | async-done | bytes 294928 | tf_op jit(solution)/shard_map/reduce_scatter | solution.py:276
  1199.7 46.6 %reduce-scatter.22.cloned.1.call-done = f32[192,384]{1,0:T(8,128)} async-done(((f32[1536,384]{1,0:T(8,128)}), f32[192,384]{1,0:T(8,128)}) %reduce-scatter.22.cloned.1.call-update) | async-done | bytes 294928 | tf_op jit(solution)/shard_map/reduce_scatter | solution.py:275
  (193 shorter events, 214.1 us)
Async XLA Ops:
  7.2 123.0 %copy-start = (bf16[384,1536]{1,0:T(8,128)(2,1)S(1)}, bf16[384,1536]{1,0:T(8,128)(2,1)}, u32[]{:S(2)}) copy-start(bf16[384,1536]{1,0:T(8,128)(2,1)} %param.25) | copy-start | bytes 3538948
  7.2 70.8 %copy-start.14 = (bf16[1536,384]{1,0:T(8,128)(2,1)S(1)}, bf16[1536,384]{1,0:T(8,128)(2,1)}, u32[]{:S(2)}) copy-start(bf16[1536,384]{1,0:T(8,128)(2,1)} %param.24) | copy-start | bytes 3538948
  7.2 70.8 %all-gather.5.cloned.1.call-start = ((), (), s32[]{:S(2)}) async-start(), calls=%async_computation.11 | async-start | bytes 3932160 | tf_op jit(solution)/shard_map/all_gather | solution.py:187
  11.7 232.6 %reduce-scatter.12.cloned.1.call-start = ((), (), s32[]{:S(2)}) async-start(), calls=%async_computation.12 | async-start | bytes 7864320 | tf_op jit(solution)/shard_map/reduce_scatter | solution.py:196
  134.7 112.6 %copy-start.22 = (f32[1536]{0:T(1024)S(1)}, f32[1536]{0:T(1024)}, u32[]{:S(2)}) copy-start(f32[1536]{0:T(1024)} %param.21) | copy-start | bytes 18436
  134.7 177.9 %all-gather.7.cloned.1.call-start = ((), (), s32[]{:S(2)}) async-start(), calls=%async_computation.13 | async-start | bytes 3932160 | tf_op jit(solution)/shard_map/all_gather | solution.py:203
  248.4 128.4 %all-gather.9.cloned.1.call-start = ((), (), s32[]{:S(2)}) async-start(), calls=%async_computation.15 | async-start | bytes 3932160 | tf_op jit(solution)/shard_map/all_gather | solution.py:222
  251.3 266.3 %reduce-scatter.16.cloned.1.call-start = ((), (), s32[]{:S(2)}) async-start(), calls=%async_computation.16 | async-start | bytes 7864320 | tf_op jit(solution)/shard_map/reduce_scatter | solution.py:231
  312.6 9.8 copy-start.26
  389.7 8.8 copy-start.27
  408.0 172.5 %reduce-scatter.14.cloned.1.call-start = ((), (), s32[]{:S(2)}) async-start(), calls=%async_computation.14 | async-start | bytes 3932160 | tf_op jit(solution)/shard_map/reduce_scatter | solution.py:213
  417.6 231.3 %all-gather.11.cloned.1.call-start = ((), (), s32[]{:S(2)}) async-start(), calls=%async_computation.17 | async-start | bytes 3932160 | tf_op jit(solution)/shard_map/all_gather | solution.py:239
  585.2 232.8 %reduce-scatter.18.cloned.1.call-start = ((), (), s32[]{:S(2)}) async-start(), calls=%async_computation.18 | async-start | bytes 3932160 | tf_op jit(solution)/shard_map/reduce_scatter | solution.py:259
  758.9 140.3 %reduce-scatter.32.cloned.1.call-start = ((), (), s32[]{:S(2)}) async-start(), calls=%async_computation.25 | async-start | bytes 10616832 | tf_op jit(solution)/shard_map/reduce_scatter | solution.py:280
  768.9 210.8 %reduce-scatter.30.cloned.1.call-start = ((), (), s32[]{:S(2)}) async-start(), calls=%async_computation.24 | async-start | bytes 10616832 | tf_op jit(solution)/shard_map/reduce_scatter | solution.py:279
  779.3 280.9 %reduce-scatter.28.cloned.1.call-start = ((), (), s32[]{:S(2)}) async-start(), calls=%async_computation.23 | async-start | bytes 10616832 | tf_op jit(solution)/shard_map/reduce_scatter | solution.py:278
  789.4 317.2 %reduce-scatter.26.cloned.1.call-start = ((), (), s32[]{:S(2)}) async-start(), calls=%async_computation.22 | async-start | bytes 2654208 | tf_op jit(solution)/shard_map/reduce_scatter | solution.py:277
  795.7 357.7 %reduce-scatter.20.cloned.1.call-start = ((), (), s32[]{:S(2)}) async-start(), calls=%async_computation.19 | async-start | bytes 2654208 | tf_op jit(solution)/shard_map/reduce_scatter | solution.py:274
  800.9 398.7 %reduce-scatter.24.cloned.1.call-start = ((), (), s32[]{:S(2)}) async-start(), calls=%async_computation.21 | async-start | bytes 2654208 | tf_op jit(solution)/shard_map/reduce_scatter | solution.py:276
  806.1 11.8 copy-start.4
  806.2 11.8 copy-start.21
  806.2 440.2 %reduce-scatter.22.cloned.1.call-start = ((), (), s32[]{:S(2)}) async-start(), calls=%async_computation.20 | async-start | bytes 2654208 | tf_op jit(solution)/shard_map/reduce_scatter | solution.py:275
  811.6 50.1 %copy-start.5 = (f32[256,1536]{1,0:T(8,128)S(1)}, f32[256,1536]{1,0:T(8,128)}, u32[]{:S(2)}) copy-start(f32[256,1536]{1,0:T(8,128)} %get-tuple-element.307) | copy-start | bytes 4718596
  811.6 434.7 %copy-start.1 = (bf16[384,1536]{1,0:T(8,128)(2,1)S(1)}, bf16[384,1536]{1,0:T(8,128)(2,1)}, u32[]{:S(2)}) copy-start(bf16[384,1536]{1,0:T(8,128)(2,1)} %param.25) | copy-start | bytes 3538948
  (26 other events, 64.3 us)
Sparse Core Ops, SparseCore 0:
  11.8 66.1 all-gather.4
  134.8 109.3 reduce-scatter.11
  248.5 64.0 all-gather.6
  314.6 62.1 all-gather.8
  408.1 109.3 reduce-scatter.15
  519.7 60.7 reduce-scatter.13
  585.3 63.5 all-gather.10
  759.0 58.8 reduce-scatter.17
  822.1 77.1 reduce-scatter.31
  903.2 76.4 reduce-scatter.29
  983.8 76.4 reduce-scatter.27
  1064.0 42.5 reduce-scatter.25
  1110.9 42.4 reduce-scatter.19
  1157.2 42.4 reduce-scatter.23
  1203.8 42.4 reduce-scatter.21
where the time goes:
time: 1260 us; the launch traced here: 1250 us
  waiting for transfers between devices  890 us (71%)
  matrix products  224 us (18%)
  other arithmetic  44.1 us (4%)
  blocking collectives  40.8 us (3%)
  local copies, waits for them, and re-layouts  31.2 us (2%)
  between operations  15.2 us (1%)
    reduce_scatter x1, waiting for transfers between devices, on_device(): lax.psum_scatter(jnp.dot(attended_low, w_out, preferred_element_type=jnp....  109 us
    reduce_scatter x1, waiting for transfers between devices, on_device(): lax.psum_scatter(contract_cols(grad_gate_low, w_gate) + contract_cols(gra...  99.9 us
    reduce_scatter x1, waiting for transfers between devices, on_device(): lax.psum_scatter(grad_gate, 'dp', scatter_dimension=0, tiled=True)  80.6 us
    reduce_scatter x1, waiting for transfers between devices, on_device(): lax.psum_scatter(grad_up, 'dp', scatter_dimension=0, tiled=True)  80.4 us
    all_gather x1, waiting for transfers between devices, on_device(): lax.all_gather(grad_hidden.astype(jnp.bfloat16), 'tensor', axis=0, tiled=...  63.6 us
    all_gather x1, waiting for transfers between devices, on_device(): lax.all_gather(normed_one.astype(jnp.bfloat16), 'tensor', axis=0, tiled=T...  63.5 us
    all_gather x1, waiting for transfers between devices, on_device(): lax.all_gather(normed_two.astype(jnp.bfloat16), 'tensor', axis=0, tiled=T...  60 us
    reduce_scatter x1, waiting for transfers between devices, on_device(): lax.psum_scatter(jnp.dot(inner_low, w_down, preferred_element_type=jnp.fl...  59.5 us
  transfers between devices with their start and end apart: 15, of which 15 were waited for; matrix products, arithmetic and copies ran while one was open for 8% of the time, Pallas kernels for 0%

commit v1 on v0

v1 whole, which is shorter than its diff:
```python
import functools

import jax
import jax.numpy as jnp
from jax import lax
from jax.experimental import pallas as pl
from jax.experimental.pallas import tpu as pltpu
from jax.sharding import PartitionSpec as P

HD = 128
FF = 6144
EPS = 1e-06
NEG = -1e30
BF = jnp.bfloat16
F32 = jnp.float32
QB = 256


def norm_factor(values):
    return lax.rsqrt(jnp.mean(values * values, axis=-1, keepdims=True) + EPS)


def norm_back(values, factor, row_gain, gradient):
    scaled = gradient * row_gain
    inner_mean = jnp.mean(scaled * values, axis=-1, keepdims=True)
    back_rows = factor * scaled - values * (factor * factor * factor) * inner_mean
    return (back_rows, jnp.sum(gradient * values * factor, axis=0))


def rope_tables(length, head_size):
    half_size = head_size // 2
    frequency = 10000.0 ** (-jnp.arange(half_size, dtype=F32) / half_size)
    angles = jnp.arange(length, dtype=F32)[:, None] * frequency[None, :]
    cosine, sine = jnp.cos(angles), jnp.sin(angles)
    return (jnp.concatenate([cosine, cosine], 1), jnp.concatenate([-sine, sine], 1))


def dot(left, right, dims=((1,), (0,))):
    return lax.dot_general(left, right, (dims, ((), ())), preferred_element_type=F32)


def attend_forward_body(q_ref, k_ref, v_ref, cos_ref, sin_ref, seg_col, seg_row, qr_ref, kr_ref, vb_ref, p_ref, o_ref):
    length = q_ref.shape[0]
    half = HD // 2
    cosine, sine = cos_ref[...], sin_ref[...]
    q, k = q_ref[...], k_ref[...]
    qr_ref[...] = (q * cosine + pltpu.roll(q, half, 1) * sine).astype(BF)
    kr_ref[...] = (k * cosine + pltpu.roll(k, half, 1) * sine).astype(BF)
    vb_ref[...] = v_ref[...].astype(BF)
    scale = HD ** (-0.5)
    for start in range(0, length, QB):
        extent = start + QB
        scores = dot(qr_ref[start:extent, :], kr_ref[:extent, :], ((1,), (1,)))
        rows = lax.broadcasted_iota(jnp.int32, (QB, extent), 0) + start
        cols = lax.broadcasted_iota(jnp.int32, (QB, extent), 1)
        allowed = (cols <= rows) & (seg_col[start:extent, :] == seg_row[:, :extent])
        logits = jnp.where(allowed, scores * scale, NEG)
        expo = jnp.exp(logits - jnp.max(logits, axis=-1, keepdims=True))
        weights = (expo / jnp.sum(expo, axis=-1, keepdims=True)).astype(BF)
        p_ref[0, start:extent, :extent] = weights
        o_ref[start:extent, :] = dot(weights, vb_ref[:extent, :]).astype(BF)


def attend_backward_body(q_ref, k_ref, v_ref, do_ref, p_ref, cos_ref, sin_ref, dq_ref, dk_ref, dv_ref, ds_ref):
    length = q_ref.shape[0]
    half = HD // 2
    scale = HD ** (-0.5)

    def unrope(grad, rows):
        return (grad * cos_ref[rows, :] - pltpu.roll(grad, half, 1) * sin_ref[rows, :]).astype(BF)

    for start in range(0, length, QB):
        extent = start + QB
        rows = slice(start, extent)
        grad_p = dot(do_ref[rows, :], v_ref[:extent, :], ((1,), (1,)))
        p = p_ref[0, rows, :extent].astype(F32)
        weighted = p * grad_p
        delta = jnp.sum(weighted, axis=-1, keepdims=True)
        ds_ref[rows, :extent] = ((weighted - p * delta) * scale).astype(BF)
        dq_ref[rows, :] = unrope(dot(ds_ref[rows, :extent], k_ref[:extent, :]), rows)
    for start in range(0, length, QB):
        rows = slice(start, start + QB)
        dk_ref[rows, :] = unrope(dot(ds_ref[start:, rows], q_ref[start:, :], ((0,), (0,))), rows)
        dv_ref[rows, :] = dot(p_ref[0, start:, rows], do_ref[start:, :], ((0,), (0,))).astype(BF)


def head_specs(length, width):
    head = pl.BlockSpec((length, HD), lambda h: (0, h))
    table = pl.BlockSpec((length, HD), lambda h: (0, 0))
    probs = pl.BlockSpec((1, length, length), lambda h: (h, 0, 0))
    array = jax.ShapeDtypeStruct((length, width), BF)
    return head, table, probs, array


def attend_forward(query, key, value, cosine, sine, seg_ids):
    length, width = query.shape
    heads = width // HD
    head, table, probs, array = head_specs(length, width)
    return pl.pallas_call(
        attend_forward_body,
        grid=(heads,),
        in_specs=[head, head, head, table, table,
                  pl.BlockSpec((length, 1), lambda h: (0, 0)), pl.BlockSpec((1, length), lambda h: (0, 0))],
        out_specs=[head, head, head, probs, head],
        out_shape=[array, array, array, jax.ShapeDtypeStruct((heads, length, length), BF), array],
        compiler_params=pltpu.CompilerParams(dimension_semantics=("arbitrary",)),
        cost_estimate=pl.CostEstimate(flops=4 * heads * length * length * HD, bytes_accessed=12 << 20, transcendentals=heads * length * length),
        name="attend_forward",
    )(query, key, value, cosine, sine, seg_ids.reshape(length, 1), seg_ids.reshape(1, length))


def attend_backward(query, key, value, grad, probs_low, cosine, sine):
    length, width = query.shape
    heads = width // HD
    head, table, probs, array = head_specs(length, width)
    return pl.pallas_call(
        attend_backward_body,
        grid=(heads,),
        in_specs=[head, head, head, head, probs, table, table],
        out_specs=[head, head, head],
        out_shape=[array, array, array],
        scratch_shapes=[pltpu.VMEM((length, length), BF)],
        compiler_params=pltpu.CompilerParams(dimension_semantics=("arbitrary",)),
        cost_estimate=pl.CostEstimate(flops=8 * heads * length * length * HD, bytes_accessed=12 << 20, transcendentals=0),
        name="attend_backward",
    )(query, key, value, grad, probs_low, cosine, sine)


def on_device(tokens, segments, granularity, norm1_gain, norm2_gain, w_query, w_key, w_value, w_out, w_gate, w_up, w_down, cotangent):
    own_rows, model = tokens.shape
    length = segments.shape[1]
    heads_width = w_query.shape[1]
    width_here = w_gate.shape[1]
    ranks = length // own_rows
    tensor_rank = lax.axis_index("tensor")
    seg_ids = segments.reshape(length)
    cosine, sine = rope_tables(length, HD)

    def own(array):
        return lax.dynamic_slice_in_dim(array, tensor_rank * own_rows, own_rows, 0)

    def scatter_rows(partial):
        return lax.psum_scatter(partial.astype(BF), "tensor", scatter_dimension=0, tiled=True).astype(F32)

    tokens_all = lax.all_gather(tokens, "tensor", axis=0, tiled=True)
    inputs_f = tokens_all.astype(F32)
    rows_one = (inputs_f * norm_factor(inputs_f) * norm1_gain).astype(BF)
    query, key, value = dot(rows_one, w_query), dot(rows_one, w_key), dot(rows_one, w_value)
    query_rot, key_rot, value_low, probs_low, attended = attend_forward(query, key, value, cosine, sine, seg_ids)
    attended_all = lax.all_gather(attended, "tensor", axis=0)
    w_out_all = lax.all_gather(w_out, "tensor", axis=0)
    hidden_f = inputs_f + lax.dot_general(
        attended_all, w_out_all, (((0, 2), (0, 1)), ((), ())), preferred_element_type=F32
    )
    rows_two = (hidden_f * norm_factor(hidden_f) * norm2_gain).astype(BF)
    gate_f = dot(rows_two, w_gate)
    up_f = dot(rows_two, w_up)
    unit_ids = tensor_rank * width_here + jnp.arange(width_here)
    unit_mask = unit_ids[None, :] < (FF // 8 * 2 ** (granularity - 1))[:, None]
    sigma = jax.nn.sigmoid(gate_f)
    activated = jnp.where(unit_mask, gate_f * sigma, 0.0)
    inner_low = (activated * up_f).astype(BF)
    hidden_own = own(hidden_f)
    output = (hidden_own + scatter_rows(dot(inner_low, w_down))).astype(BF)
    cotangent_all = lax.all_gather(cotangent, "tensor", axis=0, tiled=True)
    grad_rows = jnp.where((seg_ids >= 0)[:, None], cotangent_all, 0)
    grad_inner = dot(grad_rows, w_down, ((1,), (1,)))
    grad_gate_low = jnp.where(unit_mask, grad_inner * up_f * sigma * (1.0 + gate_f * (1.0 - sigma)), 0.0).astype(BF)
    grad_up_low = (grad_inner * activated).astype(BF)
    grad_normed_two = scatter_rows(dot(grad_gate_low, w_gate, ((1,), (1,))) + dot(grad_up_low, w_up, ((1,), (1,))))
    grad_gate = dot(rows_two, grad_gate_low, ((0,), (0,))).astype(BF)
    grad_up = dot(rows_two, grad_up_low, ((0,), (0,))).astype(BF)
    grad_down_t = dot(grad_rows, inner_low, ((0,), (0,))).astype(BF)

    def reduce_dp(partial):
        return lax.psum_scatter(partial, "dp", scatter_dimension=0, tiled=True)

    back_two, gain_two = norm_back(hidden_own, norm_factor(hidden_own), norm2_gain, grad_normed_two)
    grad_hidden = own(grad_rows).astype(F32) + back_two
    grad_hidden_low = grad_hidden.astype(BF)
    grad_attended_own = lax.dot_general(
        w_out_all, grad_hidden_low, (((2,), (1,)), ((), ())), preferred_element_type=F32
    ).astype(BF)
    grad_attended_own = jnp.transpose(grad_attended_own, (0, 2, 1))
    grad_attended = lax.all_to_all(grad_attended_own, "tensor", 0, 0).reshape(length, heads_width)
    attended_own = lax.dynamic_slice_in_dim(attended_all, tensor_rank * own_rows, own_rows, 1)
    grad_out_part = jnp.stack([dot(attended_own[r], grad_hidden_low, ((0,), (0,))) for r in range(ranks)]).astype(BF)
    grad_q, grad_k, grad_v = attend_backward(query_rot, key_rot, value_low, grad_attended, probs_low, cosine, sine)
    grad_normed_one = scatter_rows(
        dot(grad_q, w_query, ((1,), (1,))) + dot(grad_k, w_key, ((1,), (1,))) + dot(grad_v, w_value, ((1,), (1,)))
    )
    grads_qkv = reduce_dp(jnp.concatenate([dot(rows_one, g, ((0,), (0,))).astype(BF) for g in (grad_q, grad_k, grad_v)], axis=1)).astype(F32)
    inputs_own = tokens.astype(F32)
    back_one, gain_one = norm_back(inputs_own, norm_factor(inputs_own), norm1_gain, grad_normed_one)
    grad_tokens = (grad_hidden + back_one).astype(BF)
    gain_one, gain_two = lax.psum((gain_one, gain_two), ("dp", "tensor"))
    grad_out = lax.psum_scatter(grad_out_part, "dp", scatter_dimension=2, tiled=True)
    grad_out = lax.psum_scatter(grad_out, "tensor", scatter_dimension=0, tiled=True)[0].astype(F32)
    return (
        output,
        grad_tokens,
        gain_one,
        gain_two,
        grads_qkv[:, :heads_width],
        grads_qkv[:, heads_width : 2 * heads_width],
        grads_qkv[:, 2 * heads_width :],
        grad_out,
        reduce_dp(grad_gate).astype(F32),
        reduce_dp(grad_up).astype(F32),
        reduce_dp(grad_down_t).astype(F32).T,
    )


def solution(mesh):
    in_specs = (
        P(("dp", "tensor"), None), P("dp", None), P("dp"), P(), P(),
        P(None, "tensor"), P(None, "tensor"), P(None, "tensor"), P("tensor", None),
        P(None, "tensor"), P(None, "tensor"), P("tensor", None), P(("dp", "tensor"), None),
    )
    out_specs = (
        P(("dp", "tensor"), None), P(("dp", "tensor"), None), P(), P(),
        P("dp", "tensor"), P("dp", "tensor"), P("dp", "tensor"), P("tensor", "dp"),
        P("dp", "tensor"), P("dp", "tensor"), P("tensor", "dp"),
    )
    return jax.shard_map(on_device, mesh=mesh, in_specs=in_specs, out_specs=out_specs, check_vma=False)
```

time: 1260 us -> 908 us (0.72)
  waiting for transfers between devices: 890 us -> 619 us
  matrix products: 224 us -> 124 us
  Pallas kernels: 0 us -> 22.3 us
    reduce_scatter x11 -> x7, waiting for transfers between devices: 657 us -> 285 us  [the longest x3 134 us: reduce_dp(): return lax.psum_scatter(partial, 'dp', scatter_dimension=0, tiled=True)]
    dot_general x35 -> x24, matrix products: 224 us -> 124 us  [the longest x22 110 us: dot(): lax.dot_general(left, right, (dims, ((), ())), preferred_element_type=F32)]
    unnamed x15, waiting for transfers between devices: 0.24 us -> 65.4 us
    pallas_call x0 -> x2, Pallas kernels: none -> 22.3 us  [the longest x1 11.8 us: attend_forward(): pl.pallas_call(attend_forward_body, grid=(heads,), in_specs=[head, head,...]
    all_to_all x0 -> x1, waiting for transfers between devices: none -> 18.9 us  [on_device(): lax.all_to_all(grad_attended_own, 'tensor', 0, 0)]
    all_gather x4, waiting for transfers between devices: 232 us -> 250 us  [the longest x1 85.8 us: on_device(): w_out_all = lax.all_gather(w_out, 'tensor', axis=0)]
  transfers between devices with their start and end apart: 15 -> 14, of which waited for: 15 -> 14; matrix products, arithmetic and copies ran while one was open for 8% -> 12% of each run, Pallas kernels for 0% -> 2%
where the time goes in v1:
time: 908 us; the launch traced here: 899 us
  waiting for transfers between devices  619 us (68%)
  matrix products  124 us (14%)
  blocking collectives  45.4 us (5%)
  other arithmetic  35.2 us (4%)
  local copies, waits for them, and re-layouts  32.4 us (4%)
  Pallas kernels  22.3 us (2%)
  between operations  16 us (2%)
    reduce_scatter x3, waiting for transfers between devices, reduce_dp(): return lax.psum_scatter(partial, 'dp', scatter_dimension=0, tiled=True)  134 us
    reduce_scatter x3, waiting for transfers between devices, scatter_rows(): lax.psum_scatter(partial.astype(BF), 'tensor', scatter_dimension=0, tiled...  129 us
    dot_general x22, matrix products, dot(): lax.dot_general(left, right, (dims, ((), ())), preferred_element_type=F32)  110 us
    all_gather x1, waiting for transfers between devices, on_device(): w_out_all = lax.all_gather(w_out, 'tensor', axis=0)  85.8 us
    unnamed x15, waiting for transfers between devices  65.4 us
    all_gather x1, waiting for transfers between devices, on_device(): attended_all = lax.all_gather(attended, 'tensor', axis=0)  64 us
    all_gather x1, waiting for transfers between devices, on_device(): tokens_all = lax.all_gather(tokens, 'tensor', axis=0, tiled=True)  61.3 us
    psum x1, blocking collectives, on_device(): gain_one, gain_two = lax.psum((gain_one, gain_two), ('dp', 'tensor'))  45.4 us
  transfers between devices with their start and end apart: 14, of which 14 were waited for; matrix products, arithmetic and copies ran while one was open for 12% of the time, Pallas kernels for 2%

profile of v1, /device:TPU:0, one launch (start us, length us, event | category | flops | bytes accessed | tf_op | source)
XLA Modules:
  0.0 899.3 jit_solution(13768139343140778026)
XLA Ops:
  14.5 61.3 %all-gather.7.cloned.1.call-done = bf16[1024,1536]{1,0:T(8,128)(2,1)} async-done(((bf16[256,1536]{1,0:T(8,128)(2,1)}), bf16[1024,1536]{1,0:T(8,128)(2,1)}) %all-gather.7.cloned.1.call-update) | async-done | bytes 3145744 | tf_op jit(solution)/shard_map/all_gather | solution.py:145
  87.7 11.8 %attend_forward.1 = (bf16[1024,384]{1,0:T(8,128)(2,1)}, bf16[1024,384]{1,0:T(8,128)(2,1)}, bf16[1024,384]{1,0:T(8,128)(2,1)}, bf16[3,1024,1024]{2,1,0:T(8,128)(2,1)}, bf16[1024,384]{1,0:T(8,128)(2,1)}) custom-call(f32[1024,384]{1,0:T(8,128)} %fusion.40.q_ref, f32[1024,384]{1,0:T(8,128)} %fusion.38.k_ref, f32[1024,384]{1,0:T(8,128)} %fusion.36.v_ref, ...), custom_call_target="tpu_custom_call" | custom-call | flops 1610612736 | bytes 12582912 | tf_op jit(solution)/shard_map/attend_forward/pallas_call | solution.py:99
  100.7 38.8 %all-gather.9.cloned.1.call-done = bf16[1024,1536]{1,0:T(8,128)(2,1)} async-done(((bf16[256,1536]{1,0:T(8,128)(2,1)}), bf16[1024,1536]{1,0:T(8,128)(2,1)}) %all-gather.9.cloned.1.call-update) | async-done | bytes 3145744 | tf_op jit(solution)/shard_map/all_gather | solution.py:165
  143.4 85.8 %all-gather.13.cloned.1.call-done = bf16[1536,1536]{1,0:T(8,128)(2,1)} async-done(((bf16[384,1536]{1,0:T(8,128)(2,1)}), bf16[1536,1536]{1,0:T(8,128)(2,1)}) %all-gather.13.cloned.1.call-update) | async-done | bytes 4718608 | tf_op jit(solution)/shard_map/all_gather | solution.py:151
  229.3 64.0 %all-gather.11.cloned.1.call-done = bf16[4096,384]{1,0:T(8,128)(2,1)} async-done(((bf16[1024,384]{1,0:T(8,128)(2,1)}), bf16[4096,384]{1,0:T(8,128)(2,1)}) %all-gather.11.cloned.1.call-update) | async-done | bytes 3145744 | tf_op jit(solution)/shard_map/all_gather | solution.py:150
  293.2 8.9 multiply_reduce_fusion
  319.3 14.1 %multiply_convert_fusion = (bf16[1024,1536]{1,0:T(8,128)(2,1)}, bf16[1024,1536]{1,0:T(8,128)(2,1)}, bf16[1024,1536]{1,0:T(8,128)(2,1)}) fusion(f32[1024,1536]{1,0:T(8,128)} %fusion.43, pred[1536]{0:T(1024)(128)(4,1)S(1)} %add_compare_fusion, f32[1024,1536]{1,0:T(8,128)} %fusion.44, bf16[1024,1536]{1,0:T(8,128)(2,1)S(1)} %copy-done.3, ...), kind=kOutput, calls=%fused_computation.11 | convolution fusion | flops 4858576896 | bytes 29885952 | tf_op jit(solution)/shard_map/dot_general | solution.py:39
  349.0 57.4 %reduce-scatter.13.cloned.1.call-done = bf16[256,1536]{1,0:T(8,128)(2,1)} async-done(((bf16[1024,1536]{1,0:T(8,128)(2,1)}), bf16[256,1536]{1,0:T(8,128)(2,1)}) %reduce-scatter.13.cloned.1.call-update) | async-done | bytes 786448 | tf_op jit(solution)/shard_map/reduce_scatter | solution.py:143
  419.0 8.5 copy.39
  427.6 9.3 %convolution_convert_fusion.2 = bf16[1536,1536]{1,0:T(8,128)(2,1)} fusion(bf16[1024,1536]{1,0:T(8,128)(2,1)} %copy-done.5, bf16[1024,1536]{1,0:T(8,128)(2,1)} %get-tuple-element.78), kind=kOutput, calls=%fused_computation.5 | convolution fusion | flops 4834197504 | bytes 11010048 | tf_op jit(solution)/shard_map/dot_general | solution.py:39
  437.0 9.3 %convolution_convert_fusion.1 = bf16[1536,1536]{1,0:T(8,128)(2,1)} fusion(bf16[1024,1536]{1,0:T(8,128)(2,1)} %copy-done.5, bf16[1024,1536]{1,0:T(8,128)(2,1)} %get-tuple-element.77), kind=kOutput, calls=%fused_computation.4 | convolution fusion | flops 4834197504 | bytes 11010048 | tf_op jit(solution)/shard_map/dot_general | solution.py:39
  446.4 9.6 %convolution_convert_fusion = bf16[1536,1536]{1,0:T(8,128)(2,1)} fusion(bf16[1024,1536]{1,0:T(8,128)(2,1)} %broadcast_select_fusion, bf16[1024,1536]{1,0:T(8,128)(2,1)} %get-tuple-element.79), kind=kOutput, calls=%fused_computation.3 | convolution fusion | flops 4834197504 | bytes 11010048 | tf_op jit(solution)/shard_map/dot_general | solution.py:39
  465.6 18.9 %all-to-all-done = bf16[4,256,384]{2,1,0:T(8,128)(2,1)S(1)} async-done(((bf16[4,256,384]{2,1,0:T(8,128)(2,1)}), bf16[4,256,384]{2,1,0:T(8,128)(2,1)S(1)}, u32[]{:S(2)}, u32[]{:S(2)}) %all-to-all-start) | async-done | bytes 786464 | tf_op jit(solution)/shard_map/all_to_all | solution.py:185
  485.4 10.6 %attend_backward.1 = (bf16[1024,384]{1,0:T(8,128)(2,1)}, bf16[1024,384]{1,0:T(8,128)(2,1)}, bf16[1024,384]{1,0:T(8,128)(2,1)}) custom-call(bf16[1024,384]{1,0:T(8,128)(2,1)} %get-tuple-element.20.q_ref, bf16[1024,384]{1,0:T(8,128)(2,1)} %get-tuple-element.21.k_ref, bf16[1024,384]{1,0:T(8,128)(2,1)} %get-tuple-element.22.v_ref, bf16[1024,384]{1,0:T(8,128)(2,1)} %bitcast.76, ...), custom_call_target="tpu_custom_call" | custom-call | flops 3221225472 | bytes 12582912 | tf_op jit(solution)/shard_map/attend_backward/pallas_call | solution.py:116
  499.6 14.9 %all-reduce.4.cloned.1.call-done = bf16[4,384,1536]{1,0,2:T(4,128)(2,1)} async-done(((bf16[4,384,1536]{1,0,2:T(4,128)(2,1)}), bf16[4,384,1536]{1,0,2:T(4,128)(2,1)}) %all-reduce.4.cloned.1.call-update) | async-done | bytes 4718608
  538.6 9.5 %convolution_convert_fusion.3 = bf16[1024,1536]{1,0:T(8,128)(2,1)} fusion(bf16[1024,1536]{1,0:T(8,128)(2,1)} %get-tuple-element.79, bf16[1536,1536]{1,0:T(8,128)(2,1)} %param.24), kind=kOutput, calls=%fused_computation.19 | convolution fusion | flops 4833411072 | bytes 11010048 | tf_op jit(solution)/shard_map/dot_general | solution.py:39
  549.5 22.9 %reduce-scatter.19.cloned.1.call-done = bf16[192,1536]{1,0:T(8,128)(2,1)} async-done(((bf16[1536,1536]{1,0:T(8,128)(2,1)}), bf16[192,1536]{1,0:T(8,128)(2,1)}) %reduce-scatter.19.cloned.1.call-update) | async-done | bytes 589840 | tf_op jit(solution)/shard_map/reduce_scatter | solution.py:176
  574.6 55.2 %reduce-scatter.21.cloned.1.call-done = bf16[192,1536]{1,0:T(8,128)(2,1)} async-done(((bf16[1536,1536]{1,0:T(8,128)(2,1)}), bf16[192,1536]{1,0:T(8,128)(2,1)}) %reduce-scatter.21.cloned.1.call-update) | async-done | bytes 589840 | tf_op jit(solution)/shard_map/reduce_scatter | solution.py:176
  632.0 55.5 %reduce-scatter.23.cloned.1.call-done = bf16[192,1536]{1,0:T(8,128)(2,1)} async-done(((bf16[1536,1536]{1,0:T(8,128)(2,1)}), bf16[192,1536]{1,0:T(8,128)(2,1)}) %reduce-scatter.23.cloned.1.call-update) | async-done | bytes 589840 | tf_op jit(solution)/shard_map/reduce_scatter | solution.py:176
  689.7 22.5 %reduce-scatter.17.cloned.1.call-done = bf16[1,384,192]{1,2,0:T(8,128)(2,1)} async-done(((bf16[4,384,192]{1,2,0:T(8,128)(2,1)}), bf16[1,384,192]{1,2,0:T(8,128)(2,1)}) %reduce-scatter.17.cloned.1.call-update) | async-done | bytes 147472 | tf_op jit(solution)/shard_map/reduce_scatter | solution.py:198
  713.9 48.3 %reduce-scatter.25.cloned.1.call-done = bf16[192,1152]{1,0:T(8,128)(2,1)} async-done(((bf16[1536,1152]{1,0:T(8,128)(2,1)}), bf16[192,1152]{1,0:T(8,128)(2,1)}) %reduce-scatter.25.cloned.1.call-update) | async-done | bytes 442384
  770.1 54.5 %reduce-scatter.15.cloned.1.call-done = bf16[256,1536]{1,0:T(8,128)(2,1)} async-done(((bf16[1024,1536]{1,0:T(8,128)(2,1)}), bf16[256,1536]{1,0:T(8,128)(2,1)}) %reduce-scatter.15.cloned.1.call-update) | async-done | bytes 786448 | tf_op jit(solution)/shard_map/reduce_scatter | solution.py:143
  826.2 45.4 %all-reduce.1 = (f32[1536]{0:T(1024)}, f32[1536]{0:T(1024)}) all-reduce(f32[1536]{0:T(1024)S(1)} %get-tuple-element.73, f32[1536]{0:T(1024)S(1)} %get-tuple-element.71), channel_id=1, replica_groups=mesh['dp'=8,'tensor'=4] {'dp','tensor'}, use_global_device_ids=true, to_apply=%region_10.11 | all-reduce | flops 3072 | bytes 24576 | tf_op jit(solution)/shard_map/psum | solution.py:196
  871.6 16.7 %reduce-scatter.11.cloned.1.call-done = bf16[256,1536]{1,0:T(8,128)(2,1)} async-done(((bf16[1024,1536]{1,0:T(8,128)(2,1)}), bf16[256,1536]{1,0:T(8,128)(2,1)}) %reduce-scatter.11.cloned.1.call-update) | async-done | bytes 786448 | tf_op jit(solution)/shard_map/reduce_scatter | solution.py:143
  (133 shorter events, 129.4 us)
Async XLA Ops:
  7.2 77.5 %copy-start = (bf16[1536,384]{1,0:T(8,128)(2,1)S(1)}, bf16[1536,384]{1,0:T(8,128)(2,1)}, u32[]{:S(2)}) copy-start(bf16[1536,384]{1,0:T(8,128)(2,1)} %param.18) | copy-start | bytes 3538948
  7.2 68.6 %all-gather.7.cloned.1.call-start = ((), (), s32[]{:S(2)}) async-start(), calls=%async_computation.9 | async-start | bytes 3932160 | tf_op jit(solution)/shard_map/all_gather | solution.py:145
  7.9 131.7 %all-gather.9.cloned.1.call-start = ((), (), s32[]{:S(2)}) async-start(), calls=%async_computation.11 | async-start | bytes 3932160 | tf_op jit(solution)/shard_map/all_gather | solution.py:165
  8.7 220.6 %all-gather.13.cloned.1.call-start = ((), (), s32[]{:S(2)}) async-start(), calls=%async_computation.19 | async-start | bytes 5898240 | tf_op jit(solution)/shard_map/all_gather | solution.py:151
  9.4 283.8 %all-gather.11.cloned.1.call-start = ((), (), s32[]{:S(2)}) async-start(), calls=%async_computation.18 | async-start | bytes 3932160 | tf_op jit(solution)/shard_map/all_gather | solution.py:150
  13.1 65.4 %copy-start.12 = (bf16[1536,384]{1,0:T(8,128)(2,1)S(1)}, bf16[1536,384]{1,0:T(8,128)(2,1)}, u32[]{:S(2)}) copy-start(bf16[1536,384]{1,0:T(8,128)(2,1)} %param.20) | copy-start | bytes 3538948
  13.2 65.4 %copy-start.18 = (f32[1536]{0:T(1024)S(1)}, f32[1536]{0:T(1024)}, u32[]{:S(2)}) copy-start(f32[1536]{0:T(1024)} %param.16) | copy-start | bytes 18436
  87.7 13.0 %copy-start.17 = (s32[1,1024]{1,0:T(1,128)S(1)}, s32[1,1024]{1,0:T(1,128)}, u32[]{:S(2)}) copy-start(s32[1,1024]{1,0:T(1,128)} %seg_row.1) | copy-start | bytes 12292
  99.5 306.9 %reduce-scatter.13.cloned.1.call-start = ((), (), s32[]{:S(2)}) async-start(), calls=%async_computation.12 | async-start | bytes 3932160 | tf_op jit(solution)/shard_map/reduce_scatter | solution.py:143
  139.6 165.8 %slice-start = ((s8[4718592]{0:T(1024)(128)(4,1)}), s8[524288]{0:T(1024)(128)(4,1)S(1)}, s32[]{:S(2)}) async-start(s8[4718592]{0:T(1024)(128)(4,1)} %bitcast.83), calls=%async_computation.22 | async-start | bytes 1048576
  293.2 9.0 copy-start.16
  293.2 12.2 %slice-start.1 = ((s8[4718592]{0:T(1024)(128)(4,1)}), s8[4194304]{0:T(1024)(128)(4,1)S(1)}, s32[]{:S(2)}) async-start(s8[4718592]{0:T(1024)(128)(4,1)} %bitcast.83), calls=%async_computation.23 | async-start | bytes 8388608
  302.2 10.1 %slice-start.2 = ((s8[4718592]{0:T(1024)(128)(4,1)}), s8[4194304]{0:T(1024)(128)(4,1)S(1)}, s32[]{:S(2)}) async-start(s8[4718592]{0:T(1024)(128)(4,1)} %bitcast.85), calls=%async_computation.24 | async-start | bytes 8388608
  347.3 167.2 %all-reduce.4.cloned.1.call-start = ((), (), s32[]{:S(2)}) async-start(), calls=%async_computation.21 | async-start | bytes 9437184
  427.5 144.9 %reduce-scatter.19.cloned.1.call-start = ((), (), s32[]{:S(2)}) async-start(), calls=%async_computation.15 | async-start | bytes 5308416 | tf_op jit(solution)/shard_map/reduce_scatter | solution.py:176
  436.9 192.8 %reduce-scatter.21.cloned.1.call-start = ((), (), s32[]{:S(2)}) async-start(), calls=%async_computation.16 | async-start | bytes 5308416 | tf_op jit(solution)/shard_map/reduce_scatter | solution.py:176
  446.3 241.2 %reduce-scatter.23.cloned.1.call-start = ((), (), s32[]{:S(2)}) async-start(), calls=%async_computation.17 | async-start | bytes 5308416 | tf_op jit(solution)/shard_map/reduce_scatter | solution.py:176
  456.0 8.4 copy-start.19
  460.6 23.9 %all-to-all-start = ((bf16[4,256,384]{2,1,0:T(8,128)(2,1)}), bf16[4,256,384]{2,1,0:T(8,128)(2,1)S(1)}, u32[]{:S(2)}, u32[]{:S(2)}) async-start(bf16[4,256,384]{2,1,0:T(8,128)(2,1)} %fusion.23), calls=%async_computation.2 | async-start | bytes 1572864 | tf_op jit(solution)/shard_map/all_to_all | solution.py:185
  464.3 247.9 %reduce-scatter.17.cloned.1.call-start = ((), (), s32[]{:S(2)}) async-start(), calls=%async_computation.14 | async-start | bytes 737280 | tf_op jit(solution)/shard_map/reduce_scatter | solution.py:198
  516.7 245.5 %reduce-scatter.25.cloned.1.call-start = ((), (), s32[]{:S(2)}) async-start(), calls=%async_computation.20 | async-start | bytes 3981312
  530.1 294.5 %reduce-scatter.15.cloned.1.call-start = ((), (), s32[]{:S(2)}) async-start(), calls=%async_computation.13 | async-start | bytes 3932160 | tf_op jit(solution)/shard_map/reduce_scatter | solution.py:143
  538.6 349.6 %reduce-scatter.11.cloned.1.call-start = ((), (), s32[]{:S(2)}) async-start(), calls=%async_computation.10 | async-start | bytes 3932160 | tf_op jit(solution)/shard_map/reduce_scatter | solution.py:143
  763.4 124.8 %copy-start.4 = (bf16[256,1536]{1,0:T(8,128)(2,1)S(1)}, bf16[256,1536]{1,0:T(8,128)(2,1)}, u32[]{:S(2)}) copy-start(bf16[256,1536]{1,0:T(8,128)(2,1)} %reduce-scatter.13.cloned.1.call-done) | copy-start | bytes 2359300
  (15 other events, 53.4 us)
Sparse Core Ops, SparseCore 0:
  9.6 66.1 all-gather.6
  77.4 62.1 all-gather.8
  141.2 88.0 all-gather.12
  231.2 61.9 all-gather.10
  347.4 58.8 reduce-scatter.12
  427.6 86.8 all-reduce.3
  518.3 53.9 reduce-scatter.18
  575.8 53.8 reduce-scatter.20
  633.6 53.8 reduce-scatter.22
  690.2 22.0 reduce-scatter.16
  715.7 46.3 reduce-scatter.24
  764.3 60.2 reduce-scatter.14
  826.9 61.2 reduce-scatter.10

commit v2 on v1

--- a/solution.py
+++ b/solution.py
@@ -2,6 +2,7 @@
 
 import jax
 import jax.numpy as jnp
+import numpy as np
 from jax import lax
 from jax.experimental import pallas as pl
 from jax.experimental.pallas import tpu as pltpu
@@ -27,38 +28,324 @@
     return (back_rows, jnp.sum(gradient * values * factor, axis=0))
 
 
-def rope_tables(length, head_size):
-    half_size = head_size // 2
-    frequency = 10000.0 ** (-jnp.arange(half_size, dtype=F32) / half_size)
-    angles = jnp.arange(length, dtype=F32)[:, None] * frequency[None, :]
-    cosine, sine = jnp.cos(angles), jnp.sin(angles)
-    return (jnp.concatenate([cosine, cosine], 1), jnp.concatenate([-sine, sine], 1))
-
-
 def dot(left, right, dims=((1,), (0,))):
     return lax.dot_general(left, right, (dims, ((), ())), preferred_element_type=F32)
 
 
-def attend_forward_body(q_ref, k_ref, v_ref, cos_ref, sin_ref, seg_col, seg_row, qr_ref, kr_ref, vb_ref, p_ref, o_ref):
-    length = q_ref.shape[0]
+MESH = pl.DeviceIdType.MESH
+ANY = pl.BlockSpec(memory_space=pl.ANY)
+VM = pl.BlockSpec(memory_space=pltpu.VMEM)
+DMA = pltpu.SemaphoreType.DMA
+RANKS = 4
+
+
+def across(rank, k):
+    if k == 3:
+        return 3 - rank
+    if k == 1:
+        return rank + 1 - 2 * lax.rem(rank, 2)
+    if k == 2:
+        return rank + 2 - 4 * lax.div(rank, 2)
+    return rank
+
+
+def flip(index, bit):
+    step = 2**bit
+    return index + step - 2 * step * lax.rem(lax.div(index, step), 2)
+
+
+def inner_plane(rank):
+    return (rank == 1) | (rank == 2)
+
+
+def greet(peers):
+    barrier = pltpu.get_barrier_semaphore()
+    for peer in peers:
+        pl.semaphore_signal(barrier, inc=1, device_id=peer, device_id_type=MESH)
+    pl.semaphore_wait(barrier, len(peers))
+
+
+def line_peers(rank):
+    return [{"tensor": across(rank, k)} for k in (1, 2, 3)]
+
+
+class LineGather:
+    def __init__(self, rank, view, pieces, send_sems, recv_sems):
+        self.rank, self.view, self.pieces = rank, view, pieces
+        self.send_sems, self.recv_sems = send_sems, recv_sems
+        self.inner = inner_plane(rank)
+
+    @staticmethod
+    def sems(pieces):
+        return [DMA((4, pieces)), DMA((RANKS, pieces))]
+
+    def copy(self, source, piece, k, slot):
+        return pltpu.make_async_remote_copy(
+            src_ref=self.view(source, piece), dst_ref=self.view(source, piece),
+            send_sem=self.send_sems.at[slot, piece], recv_sem=self.recv_sems.at[source, piece],
+            device_id={"tensor": across(self.rank, k)}, device_id_type=MESH,
+        )
+
+    def start(self, piece):
+        self.copy(self.rank, piece, 2, 0).start()
+        self.copy(self.rank, piece, 1, 1).start()
+        pl.when(self.inner)(lambda: self.copy(self.rank, piece, 3, 2).start())
+
+    def arrive(self, k, piece):
+        source = across(self.rank, k)
+        self.copy(source, piece, 1, 3).wait_recv()
+        if k == 2:
+            pl.when(self.inner)(lambda: self.copy(source, piece, 1, 3).start())
+
+    def finish(self):
+        for piece in range(self.pieces):
+            self.copy(self.rank, piece, 2, 0).wait_send()
+            self.copy(self.rank, piece, 1, 1).wait_send()
+
+        @pl.when(self.inner)
+        def _():
+            for piece in range(self.pieces):
+                self.copy(self.rank, piece, 3, 2).wait_send()
+                self.copy(across(self.rank, 2), piece, 1, 3).wait_send()
+
+
+def local(source, target, sem):
+    return pltpu.make_async_copy(source, target, sem)
+
+
+def rope_numpy(length):
     half = HD // 2
-    cosine, sine = cos_ref[...], sin_ref[...]
-    q, k = q_ref[...], k_ref[...]
-    qr_ref[...] = (q * cosine + pltpu.roll(q, half, 1) * sine).astype(BF)
-    kr_ref[...] = (k * cosine + pltpu.roll(k, half, 1) * sine).astype(BF)
-    vb_ref[...] = v_ref[...].astype(BF)
+    frequency = np.float32(10000.0) ** (-np.arange(half, dtype=np.float32) / np.float32(half))
+    angles = np.arange(length, dtype=np.float32)[:, None] * frequency[None, :]
+    cosine, sine = np.cos(angles), np.sin(angles)
+    return (np.concatenate([cosine, cosine], 1), np.concatenate([-sine, sine], 1))
+
+
+def input_body(dp, tok, cot, seg, wo, wq, wk, wv, gain, cosine, sine,
+               x_out, a1_out, q_out, k_out, v_out, wo_out, cot_out,
+               xs, a1s, qkv, ws, wos, cots, x_ss, x_rs, z_ss, z_rs, d_ss, d_rs, c_ss, l_sem):
+    rank, group = lax.axis_index("tensor"), lax.axis_index("dp")
+    rows = tok.shape[0]
+    half_rows = rows // 2
+    mates = dp // 2
+    partner = flip(group, 0)
+    parity = lax.rem(group, 2)
+    pair = lax.div(group, 2)
+
+    def mate(step):
+        return lax.rem(pair + step, mates) * 2 + parity
+
+    first = [local(wo.at[group], wos.at[rank, group], l_sem.at[0]), local(tok, xs.at[rank], l_sem.at[1]), local(cot, cots, l_sem.at[2])]
+    weights = [local(w, ws.at[i], l_sem.at[3 + i]) for i, w in enumerate((wq, wk, wv))]
+    for c in first + weights:
+        c.start()
+    greet(line_peers(rank) + [{"dp": partner}] + [{"dp": mate(s)} for s in range(1, mates)])
+    out_gather = LineGather(rank, lambda s, p: wos.at[s, group], 1, z_ss, z_rs)
+    first[0].wait()
+    out_gather.start(0)
+    gather = LineGather(rank, lambda s, p: xs.at[s, pl.ds(p * half_rows, half_rows)], 2, x_ss, x_rs)
+    first[1].wait()
+    gather.start(0)
+    gather.start(1)
+    first[2].wait()
+    cots[...] = jnp.where(seg[...] >= 0, cots[...], jnp.zeros_like(cots))
+    for w in weights:
+        w.wait()
+
+    def chunk(source):
+        x = xs[source].astype(F32)
+        a1s[source] = (x * norm_factor(x) * gain[...]).astype(BF)
+        where = pl.ds(pl.multiple_of(source * rows, rows), rows)
+        for i in range(3):
+            product = dot(a1s[source], ws[i])
+            for h in range(product.shape[1] // HD):
+                head = product[:, h * HD : (h + 1) * HD]
+                if i < 2:
+                    head = head * cosine[where, :] + pltpu.roll(head, HD // 2, 1) * sine[where, :]
+                qkv[i, where, h * HD : (h + 1) * HD] = head.astype(BF)
+
+    chunk(rank)
+    for k in (1, 2, 3):
+        out_gather.arrive(k, 0)
+
+    def mate_copy(step):
+        return pltpu.make_async_remote_copy(
+            src_ref=wos.at[:, group], dst_ref=wos.at[:, group], send_sem=d_ss.at[step], recv_sem=d_rs.at[group],
+            device_id={"dp": mate(step)}, device_id_type=MESH)
+
+    def mate_arrival(step):
+        piece = mate(step)
+        return pltpu.make_async_remote_copy(
+            src_ref=wos.at[:, piece], dst_ref=wos.at[:, piece], send_sem=d_ss.at[step], recv_sem=d_rs.at[piece],
+            device_id={"dp": piece}, device_id_type=MESH)
+
+    def core_copy(step, owner):
+        piece = lax.rem(pair + step, mates) * 2 + owner
+        return pltpu.make_async_remote_copy(
+            src_ref=wos.at[:, piece], dst_ref=wos.at[:, piece], send_sem=c_ss.at[step], recv_sem=d_rs.at[piece],
+            device_id={"dp": partner}, device_id_type=MESH)
+
+    for step in range(1, mates):
+        mate_copy(step).start()
+    core_copy(0, parity).start()
+    for piece in range(2):
+        gather.arrive(1, piece)
+        gather.arrive(2, piece)
+    chunk(across(rank, 1))
+    chunk(across(rank, 2))
+    for step in range(1, mates):
+        mate_arrival(step).wait_recv()
+        core_copy(step, parity).start()
+    for piece in range(2):
+        gather.arrive(3, piece)
+    chunk(across(rank, 3))
+    for step in range(mates):
+        core_copy(step, 1 - parity).wait_recv()
+    gather.finish()
+    out_gather.finish()
+    for step in range(1, mates):
+        mate_copy(step).wait_send()
+    for step in range(mates):
+        core_copy(step, parity).wait_send()
+    last = [local(xs, x_out, l_sem.at[0]), local(a1s, a1_out, l_sem.at[1]), local(wos, wo_out, l_sem.at[2]),
+            local(qkv.at[0], q_out, l_sem.at[3]), local(qkv.at[1], k_out, l_sem.at[4]), local(qkv.at[2], v_out, l_sem.at[5]),
+            local(cots, cot_out, l_sem.at[6])]
+    for c in last:
+        c.start()
+    for c in last:
+        c.wait()
+
+
+def input_kernel(dp, tokens, cotangent, seg_own, w_out, w_query, w_key, w_value, gain, cosine, sine):
+    rows, model = tokens.shape
+    width = w_query.shape[1]
+    length = RANKS * rows
+    part = w_out.shape[0] // dp
+    mates = dp // 2
+    shard = jax.ShapeDtypeStruct((RANKS, rows, model), BF)
+    heads = jax.ShapeDtypeStruct((length, width), BF)
+    outs = pl.pallas_call(
+        functools.partial(input_body, dp),
+        in_specs=[ANY, ANY, VM, ANY, ANY, ANY, ANY, VM, VM, VM],
+        out_specs=[ANY] * 7,
+        out_shape=[shard, shard, heads, heads, heads, jax.ShapeDtypeStruct((RANKS, dp, part, model), BF),
+                   jax.ShapeDtypeStruct((rows, model), BF)],
+        scratch_shapes=[
+            pltpu.VMEM((RANKS, rows, model), BF), pltpu.VMEM((RANKS, rows, model), BF), pltpu.VMEM((3, length, width), BF),
+            pltpu.VMEM((3, model, width), BF), pltpu.VMEM((RANKS, dp, part, model), BF), pltpu.VMEM((rows, model), BF),
+            *LineGather.sems(2), *LineGather.sems(1),
+            DMA((mates,)), DMA((dp,)), DMA((mates,)), DMA((7,)),
+        ],
+        compiler_params=pltpu.CompilerParams(collective_id=1, has_side_effects=True, vmem_limit_bytes=56 << 20),
+        name="input_gather",
+    )(tokens, cotangent, seg_own, w_out.reshape(dp, part, model), w_query, w_key, w_value, gain, cosine, sine)
+    x_all, a1_all, query, key, value, w_out_all, cot_own = outs
+    return x_all, a1_all, query, key, value, w_out_all.reshape(RANKS, dp * part, model), cot_own
+
+
+def attend_body(q, k, v, cot, x_all, wo_all, seg_col, seg_row, gain,
+                p_out, dy_out, a2_out, h_out, ob_out,
+                qkv, ps, dys, obs, xs, wos, hs, a2s, y_ss, y_rs, o_ss, o_rs, l_sem):
+    rank = lax.axis_index("tensor")
+    heads = p_out.shape[0]
+    length = q.shape[0]
+    rows = cot.shape[0]
+    half_rows = rows // 2
     scale = HD ** (-0.5)
-    for start in range(0, length, QB):
-        extent = start + QB
-        scores = dot(qr_ref[start:extent, :], kr_ref[:extent, :], ((1,), (1,)))
-        rows = lax.broadcasted_iota(jnp.int32, (QB, extent), 0) + start
-        cols = lax.broadcasted_iota(jnp.int32, (QB, extent), 1)
-        allowed = (cols <= rows) & (seg_col[start:extent, :] == seg_row[:, :extent])
-        logits = jnp.where(allowed, scores * scale, NEG)
-        expo = jnp.exp(logits - jnp.max(logits, axis=-1, keepdims=True))
-        weights = (expo / jnp.sum(expo, axis=-1, keepdims=True)).astype(BF)
-        p_ref[0, start:extent, :extent] = weights
-        o_ref[start:extent, :] = dot(weights, vb_ref[:extent, :]).astype(BF)
+    loads = [local(cot, dys.at[rank], l_sem.at[0])]
+    loads += [local(t, qkv.at[i], l_sem.at[1 + i]) for i, t in enumerate((q, k, v))]
+    late = [local(x_all, xs, l_sem.at[4]), local(wo_all, wos, l_sem.at[5])]
+    for c in loads + late:
+        c.start()
+    greet(line_peers(rank))
+    grads = LineGather(rank, lambda s, p: dys.at[s, pl.ds(p * half_rows, half_rows)], 2, y_ss, y_rs)
+    attended = LineGather(rank, lambda s, p: obs.at[s, :, pl.ds(pl.multiple_of(p * HD, HD), HD)], heads, o_ss, o_rs)
+    loads[0].wait()
+    grads.start(0)
+    grads.start(1)
+    for c in loads[1:]:
+        c.wait()
+
+    def head(h, carry):
+        cols = pl.ds(pl.multiple_of(h * HD, HD), HD)
+        for start in range(0, length, QB):
+            extent = start + QB
+            scores = dot(qkv[0, start:extent, cols], qkv[1, :extent, cols], ((1,), (1,)))
+            row_ids = lax.broadcasted_iota(jnp.int32, (QB, extent), 0) + start
+            col_ids = lax.broadcasted_iota(jnp.int32, (QB, extent), 1)
+            allowed = (col_ids <= row_ids) & (seg_col[start:extent, :] == seg_row[:, :extent])
+            logits = jnp.where(allowed, scores * scale, NEG)
+            expo = jnp.exp(logits - jnp.max(logits, axis=-1, keepdims=True))
+            probs = (expo * (1.0 / jnp.sum(expo, axis=-1, keepdims=True))).astype(BF)
+            ps[h, start:extent, :extent] = probs
+            obs[rank, start:extent, cols] = dot(probs, qkv[2, :extent, cols]).astype(BF)
+        attended.start(h)
+        return carry
+
+    lax.fori_loop(0, heads, head, 0)
+    keep = local(ps, p_out, l_sem.at[6])
+    keep.start()
+    for c in late:
+        c.wait()
+
+    def add(source, first=False, last=False):
+        def block(b, carry):
+            part = dot(obs[source, pl.ds(pl.multiple_of(b * rows, rows), rows), :], wos[source])
+            total = part + (xs[b].astype(F32) if first else hs[b])
+            hs[b] = total
+            if last:
+                a2s[b] = (total * norm_factor(total) * gain[...]).astype(BF)
+            return carry
+
+        lax.fori_loop(0, RANKS, block, 0)
+
+    add(rank, first=True)
+    for piece in range(2):
+        grads.arrive(2, piece)
+    for piece in range(heads):
+        attended.arrive(2, piece)
+    for piece in range(heads):
+        attended.arrive(1, piece)
+    add(across(rank, 2))
+    add(across(rank, 1))
+    for piece in range(2):
+        grads.arrive(1, piece)
+        grads.arrive(3, piece)
+    dy_done = local(dys, dy_out, l_sem.at[0])
+    dy_done.start()
+    for piece in range(heads):
+        attended.arrive(3, piece)
+    add(across(rank, 3), last=True)
+    last = [local(a2s, a2_out, l_sem.at[1]), local(hs.at[rank], h_out, l_sem.at[2]),
+            local(obs.at[:, pl.ds(pl.multiple_of(rank * rows, rows), rows)], ob_out, l_sem.at[3])]
+    for c in last:
+        c.start()
+    grads.finish()
+    attended.finish()
+    for c in last + [keep, dy_done]:
+        c.wait()
+
+
+def attend_kernel(query, key, value, cot_own, x_all, w_out_all, seg_ids, gain):
+    length, width = query.shape
+    heads = width // HD
+    rows, model = cot_own.shape
+    shard = (RANKS, rows, model)
+    return pl.pallas_call(
+        attend_body,
+        in_specs=[ANY] * 6 + [VM] * 3,
+        out_specs=[ANY] * 5,
+        out_shape=[jax.ShapeDtypeStruct((heads, length, length), BF), jax.ShapeDtypeStruct(shard, BF), jax.ShapeDtypeStruct(shard, BF),
+                   jax.ShapeDtypeStruct((rows, model), F32), jax.ShapeDtypeStruct((RANKS, rows, width), BF)],
+        scratch_shapes=[
+            pltpu.VMEM((3, length, width), BF), pltpu.VMEM((heads, length, length), BF), pltpu.VMEM(shard, BF),
+            pltpu.VMEM((RANKS, length, width), BF), pltpu.VMEM(shard, BF), pltpu.VMEM((RANKS, width, model), BF),
+            pltpu.VMEM(shard, F32), pltpu.VMEM(shard, BF),
+            *LineGather.sems(2), *LineGather.sems(heads), DMA((7,)),
+        ],
+        compiler_params=pltpu.CompilerParams(collective_id=2, has_side_effects=True, vmem_limit_bytes=60 << 20),
+        name="attend_gather",
+    )(query, key, value, cot_own, x_all, w_out_all, seg_ids.reshape(length, 1), seg_ids.reshape(1, length), gain)
 
 
 def attend_backward_body(q_ref, k_ref, v_ref, do_ref, p_ref, cos_ref, sin_ref, dq_ref, dk_ref, dv_ref, ds_ref):
@@ -90,23 +377,6 @@
     probs = pl.BlockSpec((1, length, length), lambda h: (h, 0, 0))
     array = jax.ShapeDtypeStruct((length, width), BF)
     return head, table, probs, array
-
-
-def attend_forward(query, key, value, cosine, sine, seg_ids):
-    length, width = query.shape
-    heads = width // HD
-    head, table, probs, array = head_specs(length, width)
-    return pl.pallas_call(
-        attend_forward_body,
-        grid=(heads,),
-        in_specs=[head, head, head, table, table,
-                  pl.BlockSpec((length, 1), lambda h: (0, 0)), pl.BlockSpec((1, length), lambda h: (0, 0))],
-        out_specs=[head, head, head, probs, head],
-        out_shape=[array, array, array, jax.ShapeDtypeStruct((heads, length, length), BF), array],
-        compiler_params=pltpu.CompilerParams(dimension_semantics=("arbitrary",)),
-        cost_estimate=pl.CostEstimate(flops=4 * heads * length * length * HD, bytes_accessed=12 << 20, transcendentals=heads * length * length),
-        name="attend_forward",
-    )(query, key, value, cosine, sine, seg_ids.reshape(length, 1), seg_ids.reshape(1, length))
 
 
 def attend_backward(query, key, value, grad, probs_low, cosine, sine):
@@ -134,25 +404,22 @@
     ranks = length // own_rows
     tensor_rank = lax.axis_index("tensor")
     seg_ids = segments.reshape(length)
-    cosine, sine = rope_tables(length, HD)
-
-    def own(array):
-        return lax.dynamic_slice_in_dim(array, tensor_rank * own_rows, own_rows, 0)
+    cosine, sine = (jnp.asarray(t) for t in rope_numpy(length))
+    dp = lax.axis_size("dp")
+    seg_own = lax.dynamic_slice_in_dim(seg_ids, tensor_rank * own_rows, own_rows, 0).reshape(own_rows, 1)
 
     def scatter_rows(partial):
         return lax.psum_scatter(partial.astype(BF), "tensor", scatter_dimension=0, tiled=True).astype(F32)
 
-    tokens_all = lax.all_gather(tokens, "tensor", axis=0, tiled=True)
-    inputs_f = tokens_all.astype(F32)
-    rows_one = (inputs_f * norm_factor(inputs_f) * norm1_gain).astype(BF)
-    query, key, value = dot(rows_one, w_query), dot(rows_one, w_key), dot(rows_one, w_value)
-    query_rot, key_rot, value_low, probs_low, attended = attend_forward(query, key, value, cosine, sine, seg_ids)
-    attended_all = lax.all_gather(attended, "tensor", axis=0)
-    w_out_all = lax.all_gather(w_out, "tensor", axis=0)
-    hidden_f = inputs_f + lax.dot_general(
-        attended_all, w_out_all, (((0, 2), (0, 1)), ((), ())), preferred_element_type=F32
-    )
-    rows_two = (hidden_f * norm_factor(hidden_f) * norm2_gain).astype(BF)
+    x_all, a1_all, query_rot, key_rot, value_low, w_out_all, cot_own = input_kernel(
+        dp, tokens, cotangent, seg_own, w_out, w_query, w_key, w_value, norm1_gain.reshape(1, model), cosine, sine
+    )
+    probs_low, grad_rows, rows_two, hidden_own, attended_own = attend_kernel(
+        query_rot, key_rot, value_low, cot_own, x_all, w_out_all, seg_ids, norm2_gain.reshape(1, model)
+    )
+    rows_one = a1_all.reshape(length, model)
+    rows_two = rows_two.reshape(length, model)
+    grad_rows = grad_rows.reshape(length, model)
     gate_f = dot(rows_two, w_gate)
     up_f = dot(rows_two, w_up)
     unit_ids = tensor_rank * width_here + jnp.arange(width_here)
@@ -160,10 +427,7 @@
     sigma = jax.nn.sigmoid(gate_f)
     activated = jnp.where(unit_mask, gate_f * sigma, 0.0)
     inner_low = (activated * up_f).astype(BF)
-    hidden_own = own(hidden_f)
     output = (hidden_own + scatter_rows(dot(inner_low, w_down))).astype(BF)
-    cotangent_all = lax.all_gather(cotangent, "tensor", axis=0, tiled=True)
-    grad_rows = jnp.where((seg_ids >= 0)[:, None], cotangent_all, 0)
     grad_inner = dot(grad_rows, w_down, ((1,), (1,)))
     grad_gate_low = jnp.where(unit_mask, grad_inner * up_f * sigma * (1.0 + gate_f * (1.0 - sigma)), 0.0).astype(BF)
     grad_up_low = (grad_inner * activated).astype(BF)
@@ -176,14 +440,13 @@
         return lax.psum_scatter(partial, "dp", scatter_dimension=0, tiled=True)
 
     back_two, gain_two = norm_back(hidden_own, norm_factor(hidden_own), norm2_gain, grad_normed_two)
-    grad_hidden = own(grad_rows).astype(F32) + back_two
+    grad_hidden = cot_own.astype(F32) + back_two
     grad_hidden_low = grad_hidden.astype(BF)
     grad_attended_own = lax.dot_general(
         w_out_all, grad_hidden_low, (((2,), (1,)), ((), ())), preferred_element_type=F32
     ).astype(BF)
     grad_attended_own = jnp.transpose(grad_attended_own, (0, 2, 1))
     grad_attended = lax.all_to_all(grad_attended_own, "tensor", 0, 0).reshape(length, heads_width)
-    attended_own = lax.dynamic_slice_in_dim(attended_all, tensor_rank * own_rows, own_rows, 1)
     grad_out_part = jnp.stack([dot(attended_own[r], grad_hidden_low, ((0,), (0,))) for r in range(ranks)]).astype(BF)
     grad_q, grad_k, grad_v = attend_backward(query_rot, key_rot, value_low, grad_attended, probs_low, cosine, sine)
     grad_normed_one = scatter_rows(

time: 908 us -> 802 us (0.88)
  waiting for transfers between devices: 619 us -> 364 us
  Pallas kernels: 22.3 us -> 200 us
  matrix products: 124 us -> 107 us
  other arithmetic: 35.2 us -> 23 us
    all_gather x4 -> x0, waiting for transfers between devices: 250 us -> none  [the longest x1 85.8 us: on_device(): w_out_all = lax.all_gather(w_out, 'tensor', axis=0)]
    pallas_call x1 -> x2, Pallas kernels: 11.8 us -> 189 us  [the longest x1 112 us: attend_kernel(): pl.pallas_call(attend_body, in_specs=[ANY] * 6 + [VM] * 3, out_specs=[ANY...]
    dot_general x22 -> x19, matrix products: 110 us -> 102 us  [dot(): lax.dot_general(left, right, (dims, ((), ())), preferred_element_type=F32)]
    unnamed x15 -> x11, waiting for transfers between devices: 65.4 us -> 63.4 us
    unnamed x57 -> x55, local copies, waits for them, and re-layouts: 20.2 us -> 18.3 us
  transfers between devices with their start and end apart: 14 -> 10, of which waited for: 14 -> 10; matrix products, arithmetic and copies ran while one was open for 12% -> 11% of each run, Pallas kernels for 2% -> 1%
where the time goes in v2:
time: 802 us; the launch traced here: 796 us
  waiting for transfers between devices  364 us (45%)
  Pallas kernels  200 us (25%)
  matrix products  107 us (13%)
  blocking collectives  45.4 us (6%)
  local copies, waits for them, and re-layouts  36.8 us (5%)
  other arithmetic  23 us (3%)
  between operations  16 us (2%)
    reduce_scatter x3, waiting for transfers between devices, reduce_dp(): return lax.psum_scatter(partial, 'dp', scatter_dimension=0, tiled=True)  131 us
    reduce_scatter x3, waiting for transfers between devices, scatter_rows(): lax.psum_scatter(partial.astype(BF), 'tensor', scatter_dimension=0, tiled...  128 us
    pallas_call x1, Pallas kernels, attend_kernel(): pl.pallas_call(attend_body, in_specs=[ANY] * 6 + [VM] * 3, out_specs=[ANY...  112 us
    dot_general x19, matrix products, dot(): lax.dot_general(left, right, (dims, ((), ())), preferred_element_type=F32)  102 us
    pallas_call x1, Pallas kernels, input_kernel(): pl.pallas_call(functools.partial(input_body, dp), in_specs=[ANY, ANY, VM,...  77.4 us
    unnamed x11, waiting for transfers between devices  63.4 us
    psum x1, blocking collectives, on_device(): gain_one, gain_two = lax.psum((gain_one, gain_two), ('dp', 'tensor'))  45.4 us
    reduce_scatter x1, waiting for transfers between devices, on_device(): lax.psum_scatter(grad_out, 'tensor', scatter_dimension=0, tiled=True)[0]  22.6 us
  transfers between devices with their start and end apart: 10, of which 10 were waited for; matrix products, arithmetic and copies ran while one was open for 11% of the time, Pallas kernels for 1%

profile of v2, /device:TPU:0, one launch (start us, length us, event | category | flops | bytes accessed | tf_op | source)
XLA Modules:
  0.0 795.6 jit_solution(3854913290230685042)
XLA Ops:
  13.7 77.4 %input_gather.1 = (bf16[4,256,1536]{2,1,0:T(8,128)(2,1)}, bf16[4,256,1536]{2,1,0:T(8,128)(2,1)}, bf16[1024,384]{1,0:T(8,128)(2,1)}, bf16[1024,384]{1,0:T(8,128)(...) custom-call(bf16[256,1536]{1,0:T(8,128)(2,1)} %tok.1, ...), custom_call_target="tpu_custom_call" | custom-call | tf_op jit(solution)/shard_map/input_gather/pallas_call | solution.py:227
  91.1 111.9 %attend_gather.1 = (bf16[3,1024,1024]{2,1,0:T(8,128)(2,1)}, bf16[4,256,1536]{2,1,0:T(8,128)(2,1)}, bf16[4,256,1536]{2,1,0:T(8,128)(2,1)}, f32[256,1536]{1,0:T(8,128)}, bf16[4,256,384]{2,1,0:T(8,128)(2,1)}) custom-call(bf16[1024,384]{1,0:T(8,128)(2,1)} %get-tuple-element.26.q.q_ref, bf16[1024,384]{1,0:T(8,128)(2,1)} %get-tuple-element.27.k.k_ref, ...), custom_call_target="tpu_custom_call" | custom-call | tf_op jit(solution)/shard_map/attend_gather/pallas_call | solution.py:334
  203.0 9.9 %fusion.32 = f32[1024,1536]{1,0:T(8,128)} fusion(bf16[1024,1536]{1,0:T(8,128)(2,1)} %bitcast.91, bf16[1536,1536]{1,0:T(8,128)(2,1)} %param.24), kind=kOutput, calls=%fused_computation.73 | convolution fusion | flops 4831838208 | bytes 14155776 | tf_op jit(solution)/shard_map/dot_general | solution.py:32
  212.9 7.0 fusion.33
  220.0 14.2 %multiply_convert_fusion = (bf16[1024,1536]{1,0:T(8,128)(2,1)S(1)}, bf16[1024,1536]{1,0:T(8,128)(2,1)S(1)}, bf16[1024,1536]{1,0:T(8,128)(2,1)}) fusion(f32[1024,1536]{1,0:T(8,128)} %fusion.32, pred[1536]{0:T(1024)(128)(4,1)S(1)} %add_compare_fusion, f32[1024,1536]{1,0:T(8,128)} %fusion.33, bf16[1024,1536]{1,0:T(8,128)(2,1)} %bitcast.89, ...), kind=kOutput, calls=%fused_computation.5 | convolution fusion | flops 4858576896 | bytes 29885952 | tf_op jit(solution)/shard_map/dot_general | solution.py:32
  239.4 8.9 %add_convert_fusion.1 = bf16[1024,1536]{1,0:T(8,128)(2,1)} fusion(f32[1024,1536]{1,0:T(8,128)S(1)} %fusion.34, bf16[1024,1536]{1,0:T(8,128)(2,1)S(1)} %get-tuple-element.91, bf16[1536,1536]{1,0:T(8,128)(2,1)} %param.25), kind=kOutput, calls=%fused_computation.4 | convolution fusion | flops 4834983936 | bytes 17301504 | tf_op jit(solution)/shard_map/dot_general | solution.py:32
  249.9 57.6 %reduce-scatter.13.cloned.1.call-done = bf16[256,1536]{1,0:T(8,128)(2,1)} async-done(((bf16[1024,1536]{1,0:T(8,128)(2,1)}), bf16[256,1536]{1,0:T(8,128)(2,1)}) %reduce-scatter.13.cloned.1.call-update) | async-done | bytes 786448 | tf_op jit(solution)/shard_map/reduce_scatter | solution.py:412
  315.9 8.5 %copy.48 = bf16[4,384,1536]{1,0,2:T(4,128)(2,1)} copy(bf16[4,384,1536]{2,1,0:T(8,128)(2,1)} %pad_maximum_fusion) | data formatting | bytes 9437184 | tf_op jit(solution)/shard_map/stack | solution.py:450
  324.5 9.3 %convolution_convert_fusion.2 = bf16[1536,1536]{1,0:T(8,128)(2,1)} fusion(bf16[1024,1536]{1,0:T(8,128)(2,1)} %bitcast.92, bf16[1024,1536]{1,0:T(8,128)(2,1)} %copy-done.19), kind=kOutput, calls=%fused_computation.2 | convolution fusion | flops 4834197504 | bytes 11010048 | tf_op jit(solution)/shard_map/dot_general | solution.py:32
  333.8 9.5 %convolution_convert_fusion.1 = bf16[1536,1536]{1,0:T(8,128)(2,1)} fusion(bf16[1024,1536]{1,0:T(8,128)(2,1)} %bitcast.93, bf16[1024,1536]{1,0:T(8,128)(2,1)} %copy-done.18), kind=kOutput, calls=%fused_computation.1 | convolution fusion | flops 4834197504 | bytes 11010048 | tf_op jit(solution)/shard_map/dot_general | solution.py:32
  343.4 9.3 %convolution_convert_fusion = bf16[1536,1536]{1,0:T(8,128)(2,1)} fusion(bf16[1024,1536]{1,0:T(8,128)(2,1)} %bitcast.90, bf16[1024,1536]{1,0:T(8,128)(2,1)} %get-tuple-element.93), kind=kOutput, calls=%fused_computation | convolution fusion | flops 4834197504 | bytes 11010048 | tf_op jit(solution)/shard_map/dot_general | solution.py:32
  362.3 18.9 %all-to-all-done = bf16[4,256,384]{1,2,0:T(8,128)(2,1)S(1)} async-done(((bf16[4,256,384]{1,2,0:T(8,128)(2,1)}), bf16[4,256,384]{1,2,0:T(8,128)(2,1)S(1)}, u32[]{:S(2)}, u32[]{:S(2)}) %all-to-all-start) | async-done | bytes 786464 | tf_op jit(solution)/shard_map/all_to_all | solution.py:449
  382.4 10.6 %attend_backward.1 = (bf16[1024,384]{1,0:T(8,128)(2,1)}, bf16[1024,384]{1,0:T(8,128)(2,1)}, bf16[1024,384]{1,0:T(8,128)(2,1)}) custom-call(bf16[1024,384]{1,0:T(8,128)(2,1)} %get-tuple-element.26.q.q_ref, bf16[1024,384]{1,0:T(8,128)(2,1)} %get-tuple-element.27.k.k_ref, bf16[1024,384]{1,0:T(8,128)(2,1)} %get-tuple-element.28.v.v_ref, ...), custom_call_target="tpu_custom_call" | custom-call | flops 3221225472 | bytes 12582912 | tf_op jit(solution)/shard_map/attend_backward/pallas_call | solution.py:386
  396.5 15.0 %all-reduce.4.cloned.1.call-done = bf16[4,384,1536]{1,0,2:T(4,128)(2,1)} async-done(((bf16[4,384,1536]{1,0,2:T(4,128)(2,1)}), bf16[4,384,1536]{1,0,2:T(4,128)(2,1)}) %all-reduce.4.cloned.1.call-update) | async-done | bytes 4718608
  421.1 5.9 copy.53
  437.0 10.0 %convolution_convert_fusion.3 = bf16[1024,1536]{1,0:T(8,128)(2,1)} fusion(bf16[1024,1536]{1,0:T(8,128)(2,1)} %get-tuple-element.93, bf16[1536,1536]{1,0:T(8,128)(2,1)} %param.26), kind=kOutput, calls=%fused_computation.11 | convolution fusion | flops 4833411072 | bytes 11010048 | tf_op jit(solution)/shard_map/dot_general | solution.py:32
  449.0 20.3 %reduce-scatter.19.cloned.1.call-done = bf16[192,1536]{1,0:T(8,128)(2,1)} async-done(((bf16[1536,1536]{1,0:T(8,128)(2,1)}), bf16[192,1536]{1,0:T(8,128)(2,1)}) %reduce-scatter.19.cloned.1.call-update) | async-done | bytes 589840 | tf_op jit(solution)/shard_map/reduce_scatter | solution.py:440
  471.5 55.0 %reduce-scatter.21.cloned.1.call-done = bf16[192,1536]{1,0:T(8,128)(2,1)} async-done(((bf16[1536,1536]{1,0:T(8,128)(2,1)}), bf16[192,1536]{1,0:T(8,128)(2,1)}) %reduce-scatter.21.cloned.1.call-update) | async-done | bytes 589840 | tf_op jit(solution)/shard_map/reduce_scatter | solution.py:440
  528.7 55.4 %reduce-scatter.23.cloned.1.call-done = bf16[192,1536]{1,0:T(8,128)(2,1)} async-done(((bf16[1536,1536]{1,0:T(8,128)(2,1)}), bf16[192,1536]{1,0:T(8,128)(2,1)}) %reduce-scatter.23.cloned.1.call-update) | async-done | bytes 589840 | tf_op jit(solution)/shard_map/reduce_scatter | solution.py:440
  586.3 22.6 %reduce-scatter.17.cloned.1.call-done = bf16[1,384,192]{1,2,0:T(8,128)(2,1)} async-done(((bf16[4,384,192]{1,2,0:T(8,128)(2,1)}), bf16[1,384,192]{1,2,0:T(8,128)(2,1)}) %reduce-scatter.17.cloned.1.call-update) | async-done | bytes 147472 | tf_op jit(solution)/shard_map/reduce_scatter | solution.py:461
  610.5 48.3 %reduce-scatter.25.cloned.1.call-done = bf16[192,1152]{1,0:T(8,128)(2,1)} async-done(((bf16[1536,1152]{1,0:T(8,128)(2,1)}), bf16[192,1152]{1,0:T(8,128)(2,1)}) %reduce-scatter.25.cloned.1.call-update) | async-done | bytes 442384
  667.6 53.7 %reduce-scatter.15.cloned.1.call-done = bf16[256,1536]{1,0:T(8,128)(2,1)} async-done(((bf16[1024,1536]{1,0:T(8,128)(2,1)}), bf16[256,1536]{1,0:T(8,128)(2,1)}) %reduce-scatter.15.cloned.1.call-update) | async-done | bytes 786448 | tf_op jit(solution)/shard_map/reduce_scatter | solution.py:412
  723.0 45.4 %all-reduce.1 = (f32[1536]{0:T(1024)}, f32[1536]{0:T(1024)}) all-reduce(f32[1536]{0:T(1024)S(1)} %get-tuple-element.87, f32[1536]{0:T(1024)} %get-tuple-element.85), channel_id=1, replica_groups=mesh['dp'=8,'tensor'=4] {'dp','tensor'}, use_global_device_ids=true, to_apply=%region_8.9 | all-reduce | flops 3072 | bytes 24576 | tf_op jit(solution)/shard_map/psum | solution.py:459
  768.3 16.6 %reduce-scatter.11.cloned.1.call-done = bf16[256,1536]{1,0:T(8,128)(2,1)} async-done(((bf16[1024,1536]{1,0:T(8,128)(2,1)}), bf16[256,1536]{1,0:T(8,128)(2,1)}) %reduce-scatter.11.cloned.1.call-update) | async-done | bytes 786448 | tf_op jit(solution)/shard_map/reduce_scatter | solution.py:412
  (112 shorter events, 78.4 us)
Async XLA Ops:
  7.2 300.3 %reduce-scatter.13.cloned.1.call-start = ((), (), s32[]{:S(2)}) async-start(), calls=%async_computation.10 | async-start | bytes 3932160 | tf_op jit(solution)/shard_map/reduce_scatter | solution.py:412
  91.1 121.8 %slice-start.2 = ((s8[4718592]{0:T(1024)(128)(4,1)}), s8[524288]{0:T(1024)(128)(4,1)S(1)}, s32[]{:S(2)}) async-start(s8[4718592]{0:T(1024)(128)(4,1)} %bitcast.84), calls=%async_computation.20 | async-start | bytes 1048576
  203.0 9.9 %slice-start.3 = ((s8[4718592]{0:T(1024)(128)(4,1)}), s8[4194304]{0:T(1024)(128)(4,1)S(1)}, s32[]{:S(2)}) async-start(s8[4718592]{0:T(1024)(128)(4,1)} %bitcast.84), calls=%async_computation.21 | async-start | bytes 8388608
  203.0 9.9 %copy-start.16 = (bf16[4,256,1536]{2,1,0:T(8,128)(2,1)S(1)}, bf16[4,256,1536]{2,1,0:T(8,128)(2,1)}, u32[]{:S(2)}) copy-start(bf16[4,256,1536]{2,1,0:T(8,128)(2,1)} %get-tuple-element.33) | copy-start | bytes 9437188
  212.9 21.3 %slice-start = ((s8[4718592]{0:T(1024)(128)(4,1)}), s8[524288]{0:T(1024)(128)(4,1)S(1)}, s32[]{:S(2)}) async-start(s8[4718592]{0:T(1024)(128)(4,1)} %bitcast.82), calls=%async_computation.18 | async-start | bytes 1048576
  220.0 14.3 %slice-start.1 = ((s8[4718592]{0:T(1024)(128)(4,1)}), s8[4194304]{0:T(1024)(128)(4,1)S(1)}, s32[]{:S(2)}) async-start(s8[4718592]{0:T(1024)(128)(4,1)} %bitcast.82), calls=%async_computation.19 | async-start | bytes 8388608
  234.2 5.1 copy-start.19
  234.2 5.1 copy-start.18
  248.3 59.2 %copy-start.10 = (f32[1536]{0:T(1024)S(1)}, f32[1536]{0:T(1024)}, u32[]{:S(2)}) copy-start(f32[1536]{0:T(1024)} %param.19) | copy-start | bytes 18436
  248.3 61.5 %copy-start.3 = (bf16[256,1536]{1,0:T(8,128)(2,1)S(1)}, bf16[256,1536]{1,0:T(8,128)(2,1)}, u32[]{:S(2)}) copy-start(bf16[256,1536]{1,0:T(8,128)(2,1)} %get-tuple-element.29.cot) | copy-start | bytes 2359300
  248.3 163.1 %all-reduce.4.cloned.1.call-start = ((), (), s32[]{:S(2)}) async-start(), calls=%async_computation.17 | async-start | bytes 9437184
  249.9 61.5 %copy-start.12 = (f32[256]{0:T(256)}, f32[256]{0:T(256)S(1)}, u32[]{:S(2)}) copy-start(f32[256]{0:T(256)S(1)} %get-tuple-element.102) | copy-start | bytes 3076
  249.9 61.5 %copy-start.13 = (f32[256]{0:T(256)}, f32[256]{0:T(256)S(1)}, u32[]{:S(2)}) copy-start(f32[256]{0:T(256)S(1)} %get-tuple-element.101) | copy-start | bytes 3076
  324.4 144.9 %reduce-scatter.19.cloned.1.call-start = ((), (), s32[]{:S(2)}) async-start(), calls=%async_computation.13 | async-start | bytes 5308416 | tf_op jit(solution)/shard_map/reduce_scatter | solution.py:440
  333.8 192.7 %reduce-scatter.21.cloned.1.call-start = ((), (), s32[]{:S(2)}) async-start(), calls=%async_computation.14 | async-start | bytes 5308416 | tf_op jit(solution)/shard_map/reduce_scatter | solution.py:440
  343.3 240.8 %reduce-scatter.23.cloned.1.call-start = ((), (), s32[]{:S(2)}) async-start(), calls=%async_computation.15 | async-start | bytes 5308416 | tf_op jit(solution)/shard_map/reduce_scatter | solution.py:440
  352.7 8.4 %copy-start.17 = (u32[32]{0:T(128)S(1)}, u32[32]{0:T(128)}, u32[]{:S(2)}) copy-start(u32[32]{0:T(128)} %constant.64) | copy-start | bytes 388
  357.3 23.9 %all-to-all-start = ((bf16[4,256,384]{1,2,0:T(8,128)(2,1)}), bf16[4,256,384]{1,2,0:T(8,128)(2,1)S(1)}, u32[]{:S(2)}, u32[]{:S(2)}) async-start(bf16[4,256,384]{1,2,0:T(8,128)(2,1)} %fusion.20), calls=%async_computation.2 | async-start | bytes 1572864 | tf_op jit(solution)/shard_map/all_to_all | solution.py:449
  361.0 247.8 %reduce-scatter.17.cloned.1.call-start = ((), (), s32[]{:S(2)}) async-start(), calls=%async_computation.12 | async-start | bytes 737280 | tf_op jit(solution)/shard_map/reduce_scatter | solution.py:461
  413.6 245.2 %reduce-scatter.25.cloned.1.call-start = ((), (), s32[]{:S(2)}) async-start(), calls=%async_computation.16 | async-start | bytes 3981312
  427.1 294.3 %reduce-scatter.15.cloned.1.call-start = ((), (), s32[]{:S(2)}) async-start(), calls=%async_computation.11 | async-start | bytes 3932160 | tf_op jit(solution)/shard_map/reduce_scatter | solution.py:412
  437.0 348.0 %reduce-scatter.11.cloned.1.call-start = ((), (), s32[]{:S(2)}) async-start(), calls=%async_computation.9 | async-start | bytes 3932160 | tf_op jit(solution)/shard_map/reduce_scatter | solution.py:412
  586.3 135.1 %copy-start.11 = (f32[1536]{0:T(1024)S(1)}, f32[1536]{0:T(1024)}, u32[]{:S(2)}) copy-start(f32[1536]{0:T(1024)} %param.18) | copy-start | bytes 18436
  660.9 124.1 %copy-start.2 = (bf16[256,1536]{1,0:T(8,128)(2,1)S(1)}, bf16[256,1536]{1,0:T(8,128)(2,1)}, u32[]{:S(2)}) copy-start(bf16[256,1536]{1,0:T(8,128)(2,1)} %reduce-scatter.13.cloned.1.call-done) | copy-start | bytes 2359300
  (10 other events, 24.7 us)
Sparse Core Ops, SparseCore 0:
  248.4 59.0 reduce-scatter.12
  324.5 86.8 all-reduce.3
  415.3 53.9 reduce-scatter.18
  472.6 53.8 reduce-scatter.20
  530.2 53.8 reduce-scatter.22
  586.8 22.0 reduce-scatter.16
  612.3 46.4 reduce-scatter.24
  661.1 60.2 reduce-scatter.14
  723.7 61.2 reduce-scatter.10

commit v3 on v2

--- a/solution.py
+++ b/solution.py
@@ -111,6 +111,173 @@
 
 def local(source, target, sem):
     return pltpu.make_async_copy(source, target, sem)
+
+
+class LineScatter:
+    def __init__(self, rank, parts, inbox, send_sems, recv_sems, pieces):
+        self.rank, self.parts, self.inbox, self.pieces = rank, parts, inbox, pieces
+        self.send_sems, self.recv_sems = send_sems, recv_sems
+        self.inner = inner_plane(rank)
+        self.end = (rank == 0) | (rank == 3)
+        self.rows = parts.shape[1] // pieces
+
+    @staticmethod
+    def sems(pieces):
+        return [DMA((4, pieces)), DMA((4, pieces))]
+
+    def where(self, piece):
+        return pl.ds(piece * self.rows, self.rows)
+
+    def copy(self, part, slot, k, piece):
+        return pltpu.make_async_remote_copy(
+            src_ref=self.parts.at[part, self.where(piece)], dst_ref=self.inbox.at[slot, self.where(piece)],
+            send_sem=self.send_sems.at[part, piece], recv_sem=self.recv_sems.at[slot, piece],
+            device_id={"tensor": across(self.rank, k)}, device_id_type=MESH,
+        )
+
+    def send_far(self):
+        for piece in range(self.pieces):
+            pl.when(self.inner)(lambda: self.copy(3, 3, 3, piece).start())
+            pl.when(self.end)(lambda: self.copy(3, 0, 1, piece).start())
+
+    def send_two_end(self):
+        @pl.when(self.end)
+        def _():
+            for piece in range(self.pieces):
+                self.copy(2, 2, 2, piece).start()
+
+    def send_two_inner(self):
+        @pl.when(self.inner)
+        def _():
+            for piece in range(self.pieces):
+                where = self.where(piece)
+                self.copy(3, 0, 1, piece).wait_recv()
+                self.parts[2, where] = (self.parts[2, where].astype(F32) + self.inbox[0, where].astype(F32)).astype(BF)
+                self.copy(2, 2, 2, piece).start()
+
+    def send_near(self):
+        for piece in range(self.pieces):
+            self.copy(1, 1, 1, piece).start()
+
+    def total(self, target):
+        for piece in range(self.pieces):
+            where = self.where(piece)
+            self.copy(1, 1, 1, piece).wait_recv()
+            self.copy(2, 2, 2, piece).wait_recv()
+            target[where] = (self.parts[0, where].astype(F32) + self.inbox[1, where].astype(F32)) + self.inbox[2, where].astype(F32)
+
+        @pl.when(self.inner)
+        def _():
+            for piece in range(self.pieces):
+                where = self.where(piece)
+                self.copy(3, 3, 3, piece).wait_recv()
+                target[where] += self.inbox[3, where].astype(F32)
+
+    def finish(self):
+        for piece in range(self.pieces):
+            for part in (1, 2, 3):
+                self.copy(part, part, part, piece).wait_send()
+
+
+class GroupReduce:
+    def __init__(self, group, dp, send, keep, first, boxes, split, sems):
+        self.group, self.dp, self.send, self.keep, self.first, self.boxes = group, dp, send, keep, first, boxes
+        self.bits = dp.bit_length() - 1
+        self.mates = dp // 2
+        columns = first.shape[3]
+        self.cols = (pl.ds(0, split), pl.ds(split, columns - split))
+        self.sems = sems
+
+    @staticmethod
+    def sem_shapes(dp, count):
+        mates, bits = dp // 2, dp.bit_length() - 1
+        shapes = [DMA((count, mates)), DMA((count, mates))]
+        for t in range(1, bits):
+            shapes += [DMA((2, count, mates >> t)), DMA((2, count, mates >> t))]
+        return shapes
+
+    @staticmethod
+    def box_shapes(dp, count, share, columns, split):
+        mates, bits = dp // 2, dp.bit_length() - 1
+        shapes = [pltpu.VMEM((count, mates, share, columns), BF)]
+        for t in range(1, bits):
+            shapes += [pltpu.VMEM((count, mates >> t, share, split), BF), pltpu.VMEM((count, mates >> t, share, columns - split), BF)]
+        return shapes
+
+    def peers(self):
+        return [{"dp": flip(self.group, b)} for b in range(self.bits)]
+
+    def bit(self, b):
+        return lax.rem(lax.div(self.group, 2**b), 2)
+
+    def copy0(self, w, j):
+        return pltpu.make_async_remote_copy(
+            src_ref=self.send(w, 2 * j + 1 - self.bit(0)), dst_ref=self.first.at[w, j],
+            send_sem=self.sems[0].at[w, j], recv_sem=self.sems[1].at[w, j],
+            device_id={"dp": flip(self.group, 0)}, device_id_type=MESH)
+
+    def place(self, t, half, j, mine):
+        n = self.bits
+        if half == 0:
+            low = sum((self.bit(i) * 2 ** (i - 1) for i in range(1, t)), 0)
+            bit = self.bit(t)
+            return (2 * j + (bit if mine else 1 - bit)) * 2 ** (t - 1) + low
+        high = sum((self.bit(n - i) * 2 ** (n - 1 - i) for i in range(1, t)), 0)
+        bit = self.bit(n - t)
+        return high + (bit if mine else 1 - bit) * 2 ** (n - 1 - t) + j
+
+    def copy(self, t, half, w, j):
+        return pltpu.make_async_remote_copy(
+            src_ref=self.keep(w, self.place(t, half, j, False)).at[:, self.cols[half]], dst_ref=self.boxes[2 * (t - 1) + half].at[w, j],
+            send_sem=self.sems[2 * t].at[half, w, j], recv_sem=self.sems[2 * t + 1].at[half, w, j],
+            device_id={"dp": flip(self.group, t if half == 0 else self.bits - t)}, device_id_type=MESH)
+
+    def start0(self, w):
+        for j in range(self.mates):
+            self.copy0(w, j).start()
+
+    def start(self, t, w):
+        for j in range(self.mates >> t):
+            for half in range(2):
+                self.copy(t, half, w, j).start()
+
+    def add0(self, w):
+        def body(j, carry):
+            self.copy0(w, j).wait_recv()
+            mine = self.keep(w, j)
+            mine[...] = (mine[...].astype(F32) + self.first[w, j].astype(F32)).astype(BF)
+            return carry
+
+        lax.fori_loop(0, self.mates, body, 0)
+        self.start(1, w)
+
+    def add(self, t, w, target=None):
+        for half in range(2):
+            def body(j, carry):
+                self.copy(t, half, w, j).wait_recv()
+                mine = self.keep(w, self.place(t, half, j, True)).at[:, self.cols[half]]
+                value = mine[...].astype(F32) + self.boxes[2 * (t - 1) + half][w, j].astype(F32)
+                if target is None:
+                    mine[...] = value.astype(BF)
+                else:
+                    target[:, self.cols[half]] = value
+                return carry
+
+            lax.fori_loop(0, self.mates >> t, body, 0)
+        if target is None:
+            self.start(t + 1, w)
+
+    def finish(self, count):
+        def body(w, carry):
+            for j in range(self.mates):
+                self.copy0(w, j).wait_send()
+            for t in range(1, self.bits):
+                for j in range(self.mates >> t):
+                    for half in range(2):
+                        self.copy(t, half, w, j).wait_send()
+            return carry
+
+        lax.fori_loop(0, count, body, 0)
 
 
 def rope_numpy(length):
@@ -348,52 +515,450 @@
     )(query, key, value, cot_own, x_all, w_out_all, seg_ids.reshape(length, 1), seg_ids.reshape(1, length), gain)
 
 
-def attend_backward_body(q_ref, k_ref, v_ref, do_ref, p_ref, cos_ref, sin_ref, dq_ref, dk_ref, dv_ref, ds_ref):
-    length = q_ref.shape[0]
-    half = HD // 2
-    scale = HD ** (-0.5)
-
-    def unrope(grad, rows):
-        return (grad * cos_ref[rows, :] - pltpu.roll(grad, half, 1) * sin_ref[rows, :]).astype(BF)
-
-    for start in range(0, length, QB):
-        extent = start + QB
-        rows = slice(start, extent)
-        grad_p = dot(do_ref[rows, :], v_ref[:extent, :], ((1,), (1,)))
-        p = p_ref[0, rows, :extent].astype(F32)
-        weighted = p * grad_p
-        delta = jnp.sum(weighted, axis=-1, keepdims=True)
-        ds_ref[rows, :extent] = ((weighted - p * delta) * scale).astype(BF)
-        dq_ref[rows, :] = unrope(dot(ds_ref[rows, :extent], k_ref[:extent, :]), rows)
-    for start in range(0, length, QB):
-        rows = slice(start, start + QB)
-        dk_ref[rows, :] = unrope(dot(ds_ref[start:, rows], q_ref[start:, :], ((0,), (0,))), rows)
-        dv_ref[rows, :] = dot(p_ref[0, start:, rows], do_ref[start:, :], ((0,), (0,))).astype(BF)
-
-
-def head_specs(length, width):
-    head = pl.BlockSpec((length, HD), lambda h: (0, h))
-    table = pl.BlockSpec((length, HD), lambda h: (0, 0))
-    probs = pl.BlockSpec((1, length, length), lambda h: (h, 0, 0))
-    array = jax.ShapeDtypeStruct((length, width), BF)
-    return head, table, probs, array
-
-
-def attend_backward(query, key, value, grad, probs_low, cosine, sine):
+def pick(step, choices):
+    value = choices[-1]
+    for i in range(len(choices) - 1):
+        value = jnp.where(step == i, choices[i], value)
+    return value
+
+
+FT = 768
+WB = 384
+
+
+def mlp_body(a2, dy, wg, wu, wd, hid, cot, gran, gain,
+             g_out, down_out, dh_out, gain_out,
+             lefts, acts, ws, parts, inbox, stage, downs, hs, cots, total, gains, r_ss, r_rs, l_sem, s_sem):
+    rank = lax.axis_index("tensor")
+    rows, model = cot.shape
+    width = wg.shape[1]
+    per, share = stage.shape[1], stage.shape[2]
+    loads = [local(wg, ws.at[0], l_sem.at[0]), local(a2, lefts.at[0], l_sem.at[1]), local(wu, ws.at[1], l_sem.at[2]),
+             local(dy, lefts.at[1], l_sem.at[3]), local(wd, ws.at[2], l_sem.at[4])]
+    late = [local(hid, hs, l_sem.at[5]), local(cot, cots, l_sem.at[6])]
+    for c in loads + late:
+        c.start()
+    greet(line_peers(rank))
+    scatter = LineScatter(rank, parts, inbox, r_ss, r_rs, 2)
+    order = [across(rank, k) for k in (3, 2, 1, 0)]
+    limit = FF // 8 * lax.shift_left(1, gran[0] - 1) - rank * width
+
+    def step(i, carry):
+        j = pick(i, order)
+
+        def tile(t, inner_carry):
+            cols = pl.ds(pl.multiple_of(t * FT, FT), FT)
+
+            @pl.when((i == 0) & (t == 0))
+            def _():
+                loads[0].wait()
+                loads[1].wait()
+
+            gate = dot(lefts[0, j], ws[0, :, cols])
+
+            @pl.when((i == 0) & (t == 0))
+            def _():
+                loads[2].wait()
+
+            up = dot(lefts[0, j], ws[1, :, cols])
+
+            @pl.when((i == 0) & (t == 0))
+            def _():
+                loads[3].wait()
+                loads[4].wait()
+
+            dz = dot(lefts[1, j], ws[2, cols, :], ((1,), (1,)))
+            unit = lax.broadcasted_iota(jnp.int32, gate.shape, 1) + t * FT
+            mask = unit < limit
+            sigma = jax.nn.sigmoid(gate)
+            active = jnp.where(mask, gate * sigma, 0.0)
+            acts[2, j, :, cols] = (active * up).astype(BF)
+            acts[0, j, :, cols] = jnp.where(mask, dz * up * sigma * (1.0 + gate * (1.0 - sigma)), 0.0).astype(BF)
+            acts[1, j, :, cols] = (dz * active).astype(BF)
+            return inner_carry
+
+        lax.fori_loop(0, width // FT, tile, 0)
+
+        def back(t, inner_carry):
+            cols = pl.ds(pl.multiple_of(t * FT, FT), FT)
+            parts[3 - i, :, cols] = (
+                dot(acts[0, j], ws[0, cols, :], ((1,), (1,))) + dot(acts[1, j], ws[1, cols, :], ((1,), (1,)))
+            ).astype(BF)
+            return inner_carry
+
+        lax.fori_loop(0, model // FT, back, 0)
+        pl.when(i == 0)(scatter.send_far)
+        pl.when(i == 1)(scatter.send_two_end)
+
+        @pl.when(i == 2)
+        def _():
+            scatter.send_near()
+            scatter.send_two_inner()
+
+        return carry
+
+    lax.fori_loop(0, 4, step, 0)
+    blocks = model // WB
+
+    def put(i, slot):
+        w, b = lax.div(i, blocks), lax.rem(i, blocks)
+        return local(stage.at[slot], g_out.at[w, pl.ds(b * per, per)], s_sem.at[slot])
+
+    def grads(i, carry):
+        slot = lax.rem(i, 2)
+        w, b = lax.div(i, blocks), lax.rem(i, blocks)
+        left = lax.div(w, 2)
+        cols = pl.ds(pl.multiple_of(b * WB, WB), WB)
+        value = dot(lefts[left, 0, :, cols], acts[w, 0], ((0,), (0,)))
+        for s in range(1, RANKS):
+            value += dot(lefts[left, s, :, cols], acts[w, s], ((0,), (0,)))
+        pl.when(i >= 2)(lambda: put(i - 2, slot).wait())
+        low = value.astype(BF)
+        for p in range(per):
+            stage[slot, p] = low[p * share : (p + 1) * share]
+        put(i, slot).start()
+        return carry
+
+    lax.fori_loop(0, 3 * blocks, grads, 0)
+
+    def down(i, carry):
+        downs[3 - i] = dot(acts[2, pick(i, order)], ws[2]).astype(BF)
+        return carry
+
+    lax.fori_loop(0, 4, down, 0)
+    keep = local(downs, down_out, l_sem.at[0])
+    keep.start()
+    for c in late:
+        c.wait()
+    scatter.total(total)
+    values, gradient = hs[...], total[...]
+    factor = norm_factor(values)
+    back_rows, gain_rows = norm_back(values, factor, gain[...], gradient)
+    total[...] = cots[...].astype(F32) + back_rows
+    gains[...] = gain_rows.reshape(1, model)
+    last = [local(total, dh_out, l_sem.at[1]), local(gains, gain_out, l_sem.at[2])]
+    for c in last:
+        c.start()
+    scatter.finish()
+    put(3 * blocks - 2, 0).wait()
+    put(3 * blocks - 1, 1).wait()
+    for c in last + [keep]:
+        c.wait()
+
+
+def mlp_kernel(dp, a2, dy, w_gate, w_up, w_down, hidden_own, cot_own, granularity, gain):
+    rows, model = cot_own.shape
+    width = w_gate.shape[1]
+    share = model // dp
+    shard = (RANKS, rows, model)
+    return pl.pallas_call(
+        mlp_body,
+        in_specs=[ANY] * 7 + [pl.BlockSpec(memory_space=pltpu.SMEM), VM],
+        out_specs=[ANY] * 4,
+        out_shape=[jax.ShapeDtypeStruct((3, dp, share, width), BF), jax.ShapeDtypeStruct(shard, BF),
+                   jax.ShapeDtypeStruct((rows, model), F32), jax.ShapeDtypeStruct((1, model), F32)],
+        scratch_shapes=[
+            pltpu.VMEM((2, *shard), BF), pltpu.VMEM((3, RANKS, rows, width), BF), pltpu.VMEM((3, model, width), BF),
+            pltpu.VMEM(shard, BF), pltpu.VMEM(shard, BF), pltpu.VMEM((2, WB // share, share, width), BF), pltpu.VMEM(shard, BF),
+            pltpu.VMEM((rows, model), F32), pltpu.VMEM((rows, model), BF), pltpu.VMEM((rows, model), F32), pltpu.VMEM((1, model), F32),
+            *LineScatter.sems(2), DMA((7,)), DMA((2,)),
+        ],
+        compiler_params=pltpu.CompilerParams(collective_id=3, has_side_effects=True, vmem_limit_bytes=63 << 20),
+        name="mlp_scatter",
+    )(a2, dy, w_gate, w_up, w_down, hidden_own, cot_own, granularity, gain)
+
+
+def attention_back_body(dp, dh, wo_all, downs, grads, q, k, v, p_all, hid, cosine, sine,
+                        out_out, dq_out, dk_out, dv_out, gf_out,
+                        dhs, low, wos, parts, inbox, dobs, dos, qkv, ps, ds, dqkv, hs, outs, kept, finals, *rest):
+    rank, group = lax.axis_index("tensor"), lax.axis_index("dp")
+    rounds = 2 * (dp.bit_length() - 1)
+    first, boxes, rest = rest[0], rest[1 : rounds - 1], rest[rounds - 1 :]
+    sems, (r_ss, r_rs, a_ss, a_rs, l_sem, p_sem, f_sem) = rest[:rounds], rest[rounds:]
+    rows, model = dh.shape
+    length, width = q.shape
+    heads, half, scale = width // HD, HD // 2, HD ** (-0.5)
+    count = grads.shape[0]
+    parity = lax.rem(group, 2)
+    loads = [local(dh, dhs, l_sem.at[0]), local(wo_all, wos, l_sem.at[1]), local(downs, parts, l_sem.at[2])]
+    owns = [local(grads.at[w, :, parity], kept.at[w], f_sem.at[w]) for w in range(count)]
+    late = [local(t, qkv.at[i], l_sem.at[3 + i]) for i, t in enumerate((q, k, v))] + [local(hid, hs, l_sem.at[6])]
+    for c in loads + owns + late:
+        c.start()
+
+    def probs(h):
+        return local(p_all.at[h], ps.at[lax.rem(h, 2)], p_sem.at[lax.rem(h, 2)])
+
+    probs(0).start()
+    probs(1).start()
+    reduce = GroupReduce(
+        group, dp, lambda w, d: grads.at[w, lax.div(d, 2), lax.rem(d, 2)], lambda w, j: kept.at[w, j], first, boxes, model // 2, sems)
+    greet(line_peers(rank) + reduce.peers())
+    for w in range(count):
+        reduce.start0(w)
+    scatter = LineScatter(rank, parts, inbox, r_ss, r_rs, 2)
+
+    def exchange(k, source):
+        where = pl.ds(pl.multiple_of(source * rows, rows), rows)
+        return pltpu.make_async_remote_copy(
+            src_ref=dobs.at[k - 1], dst_ref=dos.at[where], send_sem=a_ss.at[k], recv_sem=a_rs.at[source],
+            device_id={"tensor": across(rank, k)}, device_id_type=MESH)
+
+    loads[0].wait()
+    low[...] = dhs[...].astype(BF)
+    loads[1].wait()
+    for k in (3, 2, 1):
+        dobs[k - 1] = dot(low[...], wos[across(rank, k)], ((1,), (1,))).astype(BF)
+        exchange(k, rank).start()
+    dos[pl.ds(pl.multiple_of(rank * rows, rows), rows), :] = dot(low[...], wos[rank], ((1,), (1,))).astype(BF)
+    loads[2].wait()
+    scatter.send_far()
+    scatter.send_two_end()
+    scatter.send_near()
+    for c in owns:
+        c.wait()
+
+    def fold(w, carry):
+        reduce.add0(w)
+        return carry
+
+    lax.fori_loop(0, count, fold, 0)
+    for c in late:
+        c.wait()
+    for k in (3, 2, 1):
+        exchange(k, across(rank, k)).wait_recv()
+
+    def head(h, carry):
+        cols = pl.ds(pl.multiple_of(h * HD, HD), HD)
+        slot = lax.rem(h, 2)
+        probs(h).wait()
+
+        def unrope(grad, start):
+            where = slice(start, start + QB)
+            return (grad * cosine[where, :] - pltpu.roll(grad, half, 1) * sine[where, :]).astype(BF)
+
+        for start in range(0, length, QB):
+            extent = start + QB
+            where = slice(start, extent)
+            grad_p = dot(dos[where, cols], qkv[2, :extent, cols], ((1,), (1,)))
+            p = ps[slot, where, :extent].astype(F32)
+            weighted = p * grad_p
+            delta = jnp.sum(weighted, axis=-1, keepdims=True)
+            ds[where, :extent] = ((weighted - p * delta) * scale).astype(BF)
+            dqkv[0, where, cols] = unrope(dot(ds[where, :extent], qkv[1, :extent, cols]), start)
+        for start in range(0, length, QB):
+            where = slice(start, start + QB)
+            dqkv[1, where, cols] = unrope(dot(ds[start:, where], qkv[0, start:, cols], ((0,), (0,))), start)
+            dqkv[2, where, cols] = dot(ps[slot, start:, where], dos[start:, cols], ((0,), (0,))).astype(BF)
+        pl.when(h + 2 < heads)(lambda: probs(h + 2).start())
+        return carry
+
+    lax.fori_loop(0, heads, head, 0)
+    done = [local(dqkv.at[i], t, l_sem.at[i]) for i, t in enumerate((dq_out, dk_out, dv_out))]
+    for c in done:
+        c.start()
+    reduce.add(1, 0)
+    scatter.send_two_inner()
+    reduce.add(1, 1)
+    reduce.add(1, 2)
+    for t in range(2, reduce.bits - 1):
+        for w in range(count):
+            reduce.add(t, w)
+
+    def put(w):
+        return local(finals.at[w], gf_out.at[w], f_sem.at[w])
+
+    for w in range(count):
+        reduce.add(reduce.bits - 1, w, finals.at[w])
+        put(w).start()
+    scatter.total(dhs)
+    outs[...] = (hs[...] + dhs[...]).astype(BF)
+    last = local(outs, out_out, l_sem.at[3])
+    last.start()
+    scatter.finish()
+    for k in (1, 2, 3):
+        exchange(k, rank).wait_send()
+    reduce.finish(count)
+    for w in range(count):
+        put(w).wait()
+    for c in done + [last]:
+        c.wait()
+
+
+def attention_back_kernel(dp, grad_hidden, w_out_all, down_parts, grads_ff, query, key, value, probs_low, hidden_own, cosine, sine):
+    rows, model = grad_hidden.shape
     length, width = query.shape
-    heads = width // HD
-    head, table, probs, array = head_specs(length, width)
+    count, _, share, columns = grads_ff.shape
+    mates = dp // 2
+    shard = (RANKS, rows, model)
+    heads = jax.ShapeDtypeStruct((length, width), BF)
     return pl.pallas_call(
-        attend_backward_body,
-        grid=(heads,),
-        in_specs=[head, head, head, head, probs, table, table],
-        out_specs=[head, head, head],
-        out_shape=[array, array, array],
-        scratch_shapes=[pltpu.VMEM((length, length), BF)],
-        compiler_params=pltpu.CompilerParams(dimension_semantics=("arbitrary",)),
-        cost_estimate=pl.CostEstimate(flops=8 * heads * length * length * HD, bytes_accessed=12 << 20, transcendentals=0),
-        name="attend_backward",
-    )(query, key, value, grad, probs_low, cosine, sine)
+        functools.partial(attention_back_body, dp),
+        in_specs=[ANY] * 9 + [VM, VM],
+        out_specs=[ANY] * 5,
+        out_shape=[jax.ShapeDtypeStruct((rows, model), BF), heads, heads, heads, jax.ShapeDtypeStruct((count, share, columns), F32)],
+        scratch_shapes=[
+            pltpu.VMEM((rows, model), F32), pltpu.VMEM((rows, model), BF), pltpu.VMEM((RANKS, width, model), BF),
+            pltpu.VMEM(shard, BF), pltpu.VMEM(shard, BF), pltpu.VMEM((3, rows, width), BF), pltpu.VMEM((length, width), BF),
+            pltpu.VMEM((3, length, width), BF), pltpu.VMEM((2, length, length), BF), pltpu.VMEM((length, length), BF),
+            pltpu.VMEM((3, length, width), BF), pltpu.VMEM((rows, model), F32), pltpu.VMEM((rows, model), BF),
+            pltpu.VMEM((count, mates, share, columns), BF), pltpu.VMEM((count, share, columns), F32),
+            *GroupReduce.box_shapes(dp, count, share, columns, columns // 2), *GroupReduce.sem_shapes(dp, count),
+            *LineScatter.sems(2), DMA((4,)), DMA((RANKS,)), DMA((7,)), DMA((2,)), DMA((count,)),
+        ],
+        compiler_params=pltpu.CompilerParams(collective_id=4, has_side_effects=True, vmem_limit_bytes=63 << 20),
+        name="attention_back",
+    )(grad_hidden, w_out_all, down_parts, grads_ff.reshape(count, mates, 2, share, columns),
+      query, key, value, probs_low, hidden_own, cosine, sine)
+
+
+def input_back_body(dp, dq, dk, dv, a1, wq, wk, wv, tok, dh, ob, gain, gain2,
+                    dx_out, gains_out, gqkv_out, gout_out,
+                    dqkv, a1s, ws, xs, dhs, low, obs, parts, inbox, g1, g2, f1, f2, f2_low, box2, f3, gbuf, gbox, total, dxs, *rest):
+    rank, group = lax.axis_index("tensor"), lax.axis_index("dp")
+    bits = dp.bit_length() - 1
+    boxes = [rest[: 2 * bits - 1], rest[2 * bits - 1 : 4 * bits - 2]]
+    rest = rest[4 * bits - 2 :]
+    sems = [rest[: 2 * bits], rest[2 * bits : 4 * bits]]
+    r_ss, r_rs, z_ss, z_rs, g_ss, g_rs, l_sem = rest[4 * bits :]
+    rows, model = tok.shape
+    width = dq.shape[1]
+    share = g1.shape[1]
+    per = WB // share
+    parity = lax.rem(group, 2)
+    loads = [local(t, dqkv.at[i], l_sem.at[i]) for i, t in enumerate((dq, dk, dv))]
+    loads += [local(t, ws.at[i], l_sem.at[3 + i]) for i, t in enumerate((wq, wk, wv))]
+    late = [local(dh, dhs, l_sem.at[6]), local(ob, obs, l_sem.at[7]), local(a1, a1s, l_sem.at[8]), local(tok, xs, l_sem.at[9])]
+    for c in loads + late:
+        c.start()
+    scatter = LineScatter(rank, parts, inbox, r_ss, r_rs, 2)
+    mixed = GroupReduce(group, dp, lambda w, d: g1.at[d], lambda w, j: g1.at[2 * j + parity], boxes[0][0], boxes[0][1:], f1.shape[1] // 256 * 128, sems[0])
+    output = GroupReduce(group, dp, lambda w, d: g2.at[d], lambda w, j: g2.at[2 * j + parity], boxes[1][0], boxes[1][1:], f2.shape[1] // 256 * 128, sems[1])
+    greet(line_peers(rank) + mixed.peers())
+    order = [across(rank, k) for k in (3, 2, 1, 0)]
+    for c in loads:
+        c.wait()
+
+    def step(i, carry):
+        where = pl.ds(pl.multiple_of(pick(i, order) * rows, rows), rows)
+        value = dot(dqkv[0, where, :], ws[0], ((1,), (1,)))
+        for s in (1, 2):
+            value += dot(dqkv[s, where, :], ws[s], ((1,), (1,)))
+        parts[3 - i] = value.astype(BF)
+        pl.when(i == 0)(scatter.send_far)
+        pl.when(i == 1)(scatter.send_two_end)
+        pl.when(i == 2)(scatter.send_near)
+        return carry
+
+    lax.fori_loop(0, 4, step, 0)
+    for c in late:
+        c.wait()
+    low[...] = dhs[...].astype(BF)
+
+    def out_block(b, carry):
+        cols = pl.ds(pl.multiple_of(b * WB, WB), WB)
+        for r in range(RANKS):
+            value = dot(low[:, cols], obs[r], ((0,), (0,))).astype(BF)
+            for p in range(per):
+                g2[b * per + p, :, r * width : (r + 1) * width] = value[p * share : (p + 1) * share]
+        return carry
+
+    lax.fori_loop(0, model // WB, out_block, 0)
+    output.start0(0)
+
+    def mixed_block(b, carry):
+        cols = pl.ds(pl.multiple_of(b * WB, WB), WB)
+        for s in range(3):
+            value = dot(a1s[:, cols], dqkv[s], ((0,), (0,))).astype(BF)
+            for p in range(per):
+                g1[b * per + p, :, s * width : (s + 1) * width] = value[p * share : (p + 1) * share]
+        return carry
+
+    lax.fori_loop(0, model // WB, mixed_block, 0)
+    mixed.start0(0)
+    output.add0(0)
+    mixed.add0(0)
+    scatter.send_two_inner()
+    for t in range(1, bits - 1):
+        output.add(t, 0)
+        mixed.add(t, 0)
+    output.add(bits - 1, 0, f2)
+    ends = LineScatter(rank, f2_low, box2, z_ss, z_rs, 1)
+    for k in range(4):
+        column = pl.ds(pl.multiple_of(across(rank, k) * width, HD), width)
+        f2_low[k] = f2[:, column].astype(BF)
+    ends.send_far()
+    ends.send_two_end()
+    ends.send_near()
+    mixed.add(bits - 1, 0, f1)
+    done = [local(f1, gqkv_out, l_sem.at[0])]
+    done[0].start()
+    scatter.total(total)
+    values, gradient = xs[...].astype(F32), total[...]
+    back_rows, gain_rows = norm_back(values, norm_factor(values), gain[...], gradient)
+    dxs[...] = (dhs[...] + back_rows).astype(BF)
+    done.append(local(dxs, dx_out, l_sem.at[1]))
+    done[1].start()
+    gbuf[0, 0:1, :] = gain_rows.reshape(1, model)
+    gbuf[0, 1:2, :] = gain2[...]
+    turns = [{"tensor": across(rank, 1)}, {"tensor": across(rank, 2)}] + [{"dp": flip(group, b)} for b in range(bits)]
+
+    def swap(t):
+        return pltpu.make_async_remote_copy(
+            src_ref=gbuf.at[t], dst_ref=gbox.at[t], send_sem=g_ss.at[t], recv_sem=g_rs.at[t], device_id=turns[t], device_id_type=MESH)
+
+    swap(0).start()
+    ends.send_two_inner()
+    for t in range(len(turns)):
+        swap(t).wait_recv()
+        gbuf[t + 1] = gbuf[t] + gbox[t]
+        if t + 1 < len(turns):
+            swap(t + 1).start()
+    done.append(local(gbuf.at[len(turns)], gains_out, l_sem.at[2]))
+    done[2].start()
+    ends.total(f3)
+    done.append(local(f3, gout_out, l_sem.at[3]))
+    done[3].start()
+    scatter.finish()
+    ends.finish()
+    mixed.finish(1)
+    output.finish(1)
+    for t in range(len(turns)):
+        swap(t).wait_send()
+    for c in done:
+        c.wait()
+
+
+def input_back_kernel(dp, grad_q, grad_k, grad_v, a1_all, w_query, w_key, w_value, tokens, grad_hidden, attended_own, gain, gain_two):
+    rows, model = tokens.shape
+    length, width = grad_q.shape
+    share = model // dp
+    bits = dp.bit_length() - 1
+    shard = (RANKS, rows, model)
+    wide = (3 * width, RANKS * width)
+    splits = [w // 256 * 128 for w in wide]
+    return pl.pallas_call(
+        functools.partial(input_back_body, dp),
+        in_specs=[ANY] * 10 + [VM, VM],
+        out_specs=[ANY] * 4,
+        out_shape=[jax.ShapeDtypeStruct((rows, model), BF), jax.ShapeDtypeStruct((2, model), F32),
+                   jax.ShapeDtypeStruct((share, wide[0]), F32), jax.ShapeDtypeStruct((share, width), F32)],
+        scratch_shapes=[
+            pltpu.VMEM((3, length, width), BF), pltpu.VMEM((length, model), BF), pltpu.VMEM((3, model, width), BF),
+            pltpu.VMEM((rows, model), BF), pltpu.VMEM((rows, model), F32), pltpu.VMEM((rows, model), BF), pltpu.VMEM((RANKS, rows, width), BF),
+            pltpu.VMEM(shard, BF), pltpu.VMEM(shard, BF),
+            pltpu.VMEM((dp, share, wide[0]), BF), pltpu.VMEM((dp, share, wide[1]), BF),
+            pltpu.VMEM((share, wide[0]), F32), pltpu.VMEM((share, wide[1]), F32),
+            pltpu.VMEM((RANKS, share, width), BF), pltpu.VMEM((RANKS, share, width), BF), pltpu.VMEM((share, width), F32),
+            pltpu.VMEM((bits + 3, 2, model), F32), pltpu.VMEM((bits + 2, 2, model), F32),
+            pltpu.VMEM((rows, model), F32), pltpu.VMEM((rows, model), BF),
+            *GroupReduce.box_shapes(dp, 1, share, wide[0], splits[0]), *GroupReduce.box_shapes(dp, 1, share, wide[1], splits[1]),
+            *GroupReduce.sem_shapes(dp, 1), *GroupReduce.sem_shapes(dp, 1),
+            *LineScatter.sems(2), *LineScatter.sems(1), DMA((bits + 2,)), DMA((bits + 2,)), DMA((10,)),
+        ],
+        compiler_params=pltpu.CompilerParams(collective_id=5, has_side_effects=True, vmem_limit_bytes=63 << 20),
+        name="input_back",
+    )(grad_q, grad_k, grad_v, a1_all.reshape(length, model), w_query, w_key, w_value, tokens, grad_hidden, attended_own, gain, gain_two)
 
 
 def on_device(tokens, segments, granularity, norm1_gain, norm2_gain, w_query, w_key, w_value, w_out, w_gate, w_up, w_down, cotangent):
@@ -408,9 +973,6 @@
     dp = lax.axis_size("dp")
     seg_own = lax.dynamic_slice_in_dim(seg_ids, tensor_rank * own_rows, own_rows, 0).reshape(own_rows, 1)
 
-    def scatter_rows(partial):
-        return lax.psum_scatter(partial.astype(BF), "tensor", scatter_dimension=0, tiled=True).astype(F32)
-
     x_all, a1_all, query_rot, key_rot, value_low, w_out_all, cot_own = input_kernel(
         dp, tokens, cotangent, seg_own, w_out, w_query, w_key, w_value, norm1_gain.reshape(1, model), cosine, sine
     )
@@ -418,59 +980,27 @@
         query_rot, key_rot, value_low, cot_own, x_all, w_out_all, seg_ids, norm2_gain.reshape(1, model)
     )
     rows_one = a1_all.reshape(length, model)
-    rows_two = rows_two.reshape(length, model)
-    grad_rows = grad_rows.reshape(length, model)
-    gate_f = dot(rows_two, w_gate)
-    up_f = dot(rows_two, w_up)
-    unit_ids = tensor_rank * width_here + jnp.arange(width_here)
-    unit_mask = unit_ids[None, :] < (FF // 8 * 2 ** (granularity - 1))[:, None]
-    sigma = jax.nn.sigmoid(gate_f)
-    activated = jnp.where(unit_mask, gate_f * sigma, 0.0)
-    inner_low = (activated * up_f).astype(BF)
-    output = (hidden_own + scatter_rows(dot(inner_low, w_down))).astype(BF)
-    grad_inner = dot(grad_rows, w_down, ((1,), (1,)))
-    grad_gate_low = jnp.where(unit_mask, grad_inner * up_f * sigma * (1.0 + gate_f * (1.0 - sigma)), 0.0).astype(BF)
-    grad_up_low = (grad_inner * activated).astype(BF)
-    grad_normed_two = scatter_rows(dot(grad_gate_low, w_gate, ((1,), (1,))) + dot(grad_up_low, w_up, ((1,), (1,))))
-    grad_gate = dot(rows_two, grad_gate_low, ((0,), (0,))).astype(BF)
-    grad_up = dot(rows_two, grad_up_low, ((0,), (0,))).astype(BF)
-    grad_down_t = dot(grad_rows, inner_low, ((0,), (0,))).astype(BF)
-
-    def reduce_dp(partial):
-        return lax.psum_scatter(partial, "dp", scatter_dimension=0, tiled=True)
-
-    back_two, gain_two = norm_back(hidden_own, norm_factor(hidden_own), norm2_gain, grad_normed_two)
-    grad_hidden = cot_own.astype(F32) + back_two
-    grad_hidden_low = grad_hidden.astype(BF)
-    grad_attended_own = lax.dot_general(
-        w_out_all, grad_hidden_low, (((2,), (1,)), ((), ())), preferred_element_type=F32
-    ).astype(BF)
-    grad_attended_own = jnp.transpose(grad_attended_own, (0, 2, 1))
-    grad_attended = lax.all_to_all(grad_attended_own, "tensor", 0, 0).reshape(length, heads_width)
-    grad_out_part = jnp.stack([dot(attended_own[r], grad_hidden_low, ((0,), (0,))) for r in range(ranks)]).astype(BF)
-    grad_q, grad_k, grad_v = attend_backward(query_rot, key_rot, value_low, grad_attended, probs_low, cosine, sine)
-    grad_normed_one = scatter_rows(
-        dot(grad_q, w_query, ((1,), (1,))) + dot(grad_k, w_key, ((1,), (1,))) + dot(grad_v, w_value, ((1,), (1,)))
+    grads_ff, down_parts, grad_hidden, gain_two = mlp_kernel(
+        dp, rows_two, grad_rows, w_gate, w_up, w_down, hidden_own, cot_own, granularity, norm2_gain.reshape(1, model)
     )
-    grads_qkv = reduce_dp(jnp.concatenate([dot(rows_one, g, ((0,), (0,))).astype(BF) for g in (grad_q, grad_k, grad_v)], axis=1)).astype(F32)
-    inputs_own = tokens.astype(F32)
-    back_one, gain_one = norm_back(inputs_own, norm_factor(inputs_own), norm1_gain, grad_normed_one)
-    grad_tokens = (grad_hidden + back_one).astype(BF)
-    gain_one, gain_two = lax.psum((gain_one, gain_two), ("dp", "tensor"))
-    grad_out = lax.psum_scatter(grad_out_part, "dp", scatter_dimension=2, tiled=True)
-    grad_out = lax.psum_scatter(grad_out, "tensor", scatter_dimension=0, tiled=True)[0].astype(F32)
+    output, grad_q, grad_k, grad_v, own_ff = attention_back_kernel(
+        dp, grad_hidden, w_out_all, down_parts, grads_ff, query_rot, key_rot, value_low, probs_low, hidden_own, cosine, sine
+    )
+    grad_tokens, gains, own_qkv, own_out = input_back_kernel(
+        dp, grad_q, grad_k, grad_v, a1_all, w_query, w_key, w_value, tokens, grad_hidden, attended_own, norm1_gain.reshape(1, model), gain_two
+    )
     return (
         output,
         grad_tokens,
-        gain_one,
-        gain_two,
-        grads_qkv[:, :heads_width],
-        grads_qkv[:, heads_width : 2 * heads_width],
-        grads_qkv[:, 2 * heads_width :],
-        grad_out,
-        reduce_dp(grad_gate).astype(F32),
-        reduce_dp(grad_up).astype(F32),
-        reduce_dp(grad_down_t).astype(F32).T,
+        gains[0],
+        gains[1],
+        own_qkv[:, :heads_width],
+        own_qkv[:, heads_width : 2 * heads_width],
+        own_qkv[:, 2 * heads_width :],
+        own_out.T,
+        own_ff[0],
+        own_ff[1],
+        own_ff[2].T,
     )
 
 

time: 802 us -> 429 us (0.53)
  waiting for transfers between devices: 364 us -> 0 us
  Pallas kernels: 200 us -> 411 us
  matrix products: 107 us -> 0 us
  blocking collectives: 45.4 us -> 0 us
  other arithmetic: 23 us -> 0 us
  local copies, waits for them, and re-layouts: 36.8 us -> 15.7 us
  between operations: 16 us -> 1.34 us
    reduce_scatter x7 -> x0, waiting for transfers between devices: 281 us -> none  [the longest x3 131 us: reduce_dp(): return lax.psum_scatter(partial, 'dp', scatter_dimension=0, tiled=True)]
    pallas_call x1 -> x3, Pallas kernels: 10.6 us -> 222 us  [the longest x1 77.2 us: input_back_kernel(): pl.pallas_call(functools.partial(input_back_body, dp), in_specs=[ANY] * 1...]
    dot_general x20 -> x0, matrix products: 107 us -> none  [the longest x19 102 us: dot(): lax.dot_general(left, right, (dims, ((), ())), preferred_element_type=F32)]
    unnamed x11 -> x0, waiting for transfers between devices: 63.4 us -> none
    psum x1 -> x0, blocking collectives: 45.4 us -> none  [on_device(): gain_one, gain_two = lax.psum((gain_one, gain_two), ('dp', 'tensor'))]
    all_to_all x1 -> x0, waiting for transfers between devices: 18.9 us -> none  [on_device(): lax.all_to_all(grad_attended_own, 'tensor', 0, 0)]
    unnamed x55 -> x9, local copies, waits for them, and re-layouts: 18.3 us -> 2.48 us
    convert_element_type x5 -> x0, other arithmetic: 11.3 us -> none  [the longest x1 3.62 us: on_device(): grad_tokens = (grad_hidden + back_one).astype(BF)]
  transfers between devices with their start and end apart: 10 -> 0, of which waited for: 10 -> 0; matrix products, arithmetic and copies ran while one was open for 11% -> 0% of each run, Pallas kernels for 1% -> 0%
where the time goes in v3:
time: 429 us; the launch traced here: 428 us
  Pallas kernels  411 us (96%)
  local copies, waits for them, and re-layouts  15.7 us (4%)
    pallas_call x1, Pallas kernels, attend_kernel(): pl.pallas_call(attend_body, in_specs=[ANY] * 6 + [VM] * 3, out_specs=[ANY...  112 us
    pallas_call x1, Pallas kernels, input_kernel(): pl.pallas_call(functools.partial(input_body, dp), in_specs=[ANY, ANY, VM,...  77.5 us
    pallas_call x1, Pallas kernels, input_back_kernel(): pl.pallas_call(functools.partial(input_back_body, dp), in_specs=[ANY] * 1...  77.2 us
    pallas_call x1, Pallas kernels, attention_back_kernel(): pl.pallas_call(functools.partial(attention_back_body, dp), in_specs=[ANY]...  76.1 us
    pallas_call x1, Pallas kernels, mlp_kernel(): pl.pallas_call(mlp_body, in_specs=[ANY] * 7 + [pl.BlockSpec(memory_space=...  69 us

profile of v3, /device:TPU:0, one launch (start us, length us, event | category | flops | bytes accessed | tf_op | source)
XLA Modules:
  0.0 428.3 jit_solution(7076969447329928751)
XLA Ops:
  1.3 0.7 dynamic-slice_bitcast_fusion
  2.0 1.3 reshape.50.gain
  3.3 1.3 reshape.52.gain
  4.6 0.8 copy.26.seg
  5.4 1.7 copy.27.seg_col
  7.1 77.5 %input_gather.1 = (bf16[4,256,1536]{2,1,0:T(8,128)(2,1)}, bf16[4,256,1536]{2,1,0:T(8,128)(2,1)}, bf16[1024,384]{1,0:T(8,128)(2,1)}, bf16[1024,384]{1,0:T(8,128)(...) custom-call(bf16[256,1536]{1,0:T(8,128)(2,1)} %tok.3, ...), custom_call_target="tpu_custom_call" | custom-call | tf_op jit(solution)/shard_map/input_gather/pallas_call | solution.py:394
  84.6 111.6 %attend_gather.1 = (bf16[3,1024,1024]{2,1,0:T(8,128)(2,1)}, bf16[4,256,1536]{2,1,0:T(8,128)(2,1)}, bf16[4,256,1536]{2,1,0:T(8,128)(2,1)}, f32[256,1536]{1,0:T(8,128)}, bf16[4,256,384]{2,1,0:T(8,128)(2,1)}) custom-call(bf16[1024,384]{1,0:T(8,128)(2,1)} %get-tuple-element.36.q, bf16[1024,384]{1,0:T(8,128)(2,1)} %get-tuple-element.37.k, ...), custom_call_target="tpu_custom_call" | custom-call | tf_op jit(solution)/shard_map/attend_gather/pallas_call | solution.py:501
  196.1 69.0 %mlp_scatter.1 = (bf16[3,8,192,1536]{3,2,1,0:T(8,128)(2,1)}, bf16[4,256,1536]{2,1,0:T(8,128)(2,1)}, f32[256,1536]{1,0:T(8,128)}, f32[1,1536]{1,0:T(1,128)}) custom-call(bf16[4,256,1536]{2,1,0:T(8,128)(2,1)} %get-tuple-element.42.a2, bf16[4,256,1536]{2,1,0:T(8,128)(2,1)} %get-tuple-element.43.dy, bf16[1536,1536]{1,0:T(8,128)(2,1)} %wg.1, ...), custom_call_target="tpu_custom_call" | custom-call | tf_op jit(solution)/shard_map/mlp_scatter/pallas_call | solution.py:654
  265.1 76.1 %attention_back.1 = (bf16[256,1536]{1,0:T(8,128)(2,1)}, bf16[1024,384]{1,0:T(8,128)(2,1)}, bf16[1024,384]{1,0:T(8,128)(2,1)}, bf16[1024,384]{1,0:T(8,128)(2,1)}, f32[3,192,1536]{2,1,0:T(8,128)}) custom-call(f32[256,1536]{1,0:T(8,128)} %get-tuple-element.45.dh, bf16[4,384,1536]{2,1,0:T(8,128)(2,1)} %bitcast.17, ...), custom_call_target="tpu_custom_call" | custom-call | tf_op jit(solution)/shard_map/attention_back/pallas_call | solution.py:795
  341.2 77.2 %input_back.1 = (bf16[256,1536]{1,0:T(8,128)(2,1)}, f32[2,1536]{1,0:T(2,128)}, f32[192,1152]{1,0:T(8,128)}, f32[192,384]{1,0:T(8,128)}) custom-call(bf16[1024,384]{1,0:T(8,128)(2,1)} %get-tuple-element.50.dq, bf16[1024,384]{1,0:T(8,128)(2,1)} %get-tuple-element.51.dk, bf16[1024,384]{1,0:T(8,128)(2,1)} %get-tuple-element.52.dv, bf16[1024,1536]{1,0:T(8,128)(2,1)} %bitcast.19, ...), custom_call_target="tpu_custom_call" | custom-call | tf_op jit(solution)/shard_map/input_back/pallas_call | solution.py:940
  418.4 1.4 slice_reduce_fusion
  419.8 2.1 fusion
  421.9 0.0 copy-start
  421.9 0.0 copy-start.1
  421.9 4.0 slice_bitcast_fusion
  425.8 0.0 copy-start.2
  425.8 0.0 copy-done
  425.8 0.9 copy.32
  426.7 0.0 copy-done.1
  426.7 0.9 copy.33
  427.6 0.0 copy-done.2
  427.6 0.7 copy.34
Async XLA Ops:
  421.9 4.0 copy-start
  421.9 4.9 %copy-start.1 = (bf16[256,1536]{1,0:T(8,128)(2,1)S(1)}, bf16[256,1536]{1,0:T(8,128)(2,1)}, u32[]{:S(2)}) copy-start(bf16[256,1536]{1,0:T(8,128)(2,1)} %get-tuple-element.81) | copy-start | bytes 2359300
  425.8 1.8 copy-start.2

commit v4 on v3

--- a/solution.py
+++ b/solution.py
@@ -260,7 +260,7 @@
                 if target is None:
                     mine[...] = value.astype(BF)
                 else:
-                    target[:, self.cols[half]] = value
+                    target[:, self.cols[half]] = value.astype(target.dtype)
                 return carry
 
             lax.fori_loop(0, self.mates >> t, body, 0)
@@ -288,63 +288,101 @@
     return (np.concatenate([cosine, cosine], 1), np.concatenate([-sine, sine], 1))
 
 
-def input_body(dp, tok, cot, seg, wo, wq, wk, wv, gain, cosine, sine,
-               x_out, a1_out, q_out, k_out, v_out, wo_out, cot_out,
-               xs, a1s, qkv, ws, wos, cots, x_ss, x_rs, z_ss, z_rs, d_ss, d_rs, c_ss, l_sem):
+def column_of(row, target):
+    target[...] = jnp.transpose(jnp.broadcast_to(row.astype(F32), (HD, row.shape[1])))
+
+
+def forward_body(dp, tok, cot, seg, wo, wq, wk, wv, gain, gain2, cosine, sine,
+                 a1_out, q_out, k_out, v_out, wo_out, cot_out, p_out, dy_out, a2_out, h_out, ob_out,
+                 xs, a1s, qkv, ws, wos, dys, obs, ps, hs, segs,
+                 x_ss, x_rs, z_ss, z_rs, d_ss, d_rs, c_ss, y_ss, y_rs, o_ss, o_rs, l_sem, k_sem):
     rank, group = lax.axis_index("tensor"), lax.axis_index("dp")
-    rows = tok.shape[0]
+    rows, model = tok.shape
+    length, width = q_out.shape
+    heads = width // HD
+    scale = HD ** (-0.5)
     half_rows = rows // 2
-    mates = dp // 2
+    parts = wo.shape[0]
+    mates = parts // 2
+    member = lax.rem(group, parts)
+    base = group - member
+    parity = lax.rem(member, 2)
+    pair = lax.div(member, 2)
     partner = flip(group, 0)
-    parity = lax.rem(group, 2)
-    pair = lax.div(group, 2)
 
     def mate(step):
         return lax.rem(pair + step, mates) * 2 + parity
 
-    first = [local(wo.at[group], wos.at[rank, group], l_sem.at[0]), local(tok, xs.at[rank], l_sem.at[1]), local(cot, cots, l_sem.at[2])]
+    first = [local(wo.at[member], wos.at[rank, member], l_sem.at[0]), local(tok, xs.at[rank], l_sem.at[1]), local(cot, dys.at[rank], l_sem.at[2])]
     weights = [local(w, ws.at[i], l_sem.at[3 + i]) for i, w in enumerate((wq, wk, wv))]
     for c in first + weights:
         c.start()
-    greet(line_peers(rank) + [{"dp": partner}] + [{"dp": mate(s)} for s in range(1, mates)])
-    out_gather = LineGather(rank, lambda s, p: wos.at[s, group], 1, z_ss, z_rs)
+    column_of(seg[...], segs)
+    greet(line_peers(rank) + [{"dp": partner}] + [{"dp": base + mate(s)} for s in range(1, mates)])
+    out_gather = LineGather(rank, lambda s, p: wos.at[s, member], 1, z_ss, z_rs)
+    gather = LineGather(rank, lambda s, p: xs.at[s, pl.ds(p * half_rows, half_rows)], 2, x_ss, x_rs)
+    grads = LineGather(rank, lambda s, p: dys.at[s, pl.ds(p * half_rows, half_rows)], 2, y_ss, y_rs)
+    attended = LineGather(rank, lambda s, p: obs.at[s, :, pl.ds(pl.multiple_of(p * HD, HD), HD)], heads, o_ss, o_rs)
     first[0].wait()
     out_gather.start(0)
-    gather = LineGather(rank, lambda s, p: xs.at[s, pl.ds(p * half_rows, half_rows)], 2, x_ss, x_rs)
     first[1].wait()
     gather.start(0)
     gather.start(1)
     first[2].wait()
-    cots[...] = jnp.where(seg[...] >= 0, cots[...], jnp.zeros_like(cots))
+    real = segs[pl.ds(pl.multiple_of(rank * rows, rows), rows), :1] >= 0.0
+    dys[rank] = jnp.where(real, dys[rank], jnp.zeros((rows, model), BF))
+    grads.start(0)
+    grads.start(1)
+    keep = [local(dys.at[rank], cot_out, k_sem.at[0])]
+    keep[0].start()
     for w in weights:
         w.wait()
 
     def chunk(source):
         x = xs[source].astype(F32)
-        a1s[source] = (x * norm_factor(x) * gain[...]).astype(BF)
+        a1s[source] = (x * norm_factor(x) * gain[...].reshape(1, model)).astype(BF)
         where = pl.ds(pl.multiple_of(source * rows, rows), rows)
         for i in range(3):
             product = dot(a1s[source], ws[i])
-            for h in range(product.shape[1] // HD):
+            for h in range(heads):
                 head = product[:, h * HD : (h + 1) * HD]
                 if i < 2:
                     head = head * cosine[where, :] + pltpu.roll(head, HD // 2, 1) * sine[where, :]
                 qkv[i, where, h * HD : (h + 1) * HD] = head.astype(BF)
 
-    chunk(rank)
-    for k in (1, 2, 3):
-        out_gather.arrive(k, 0)
+    def chunks(i, carry):
+        @pl.when(i == 1)
+        def _():
+            for k in (1, 2, 3):
+                out_gather.arrive(k, 0)
+            for step in range(1, mates):
+                mate_copy(step).start()
+            core_copy(0, parity).start()
+            for piece in range(2):
+                gather.arrive(1, piece)
+                gather.arrive(2, piece)
+
+        @pl.when(i == 3)
+        def _():
+            for step in range(1, mates):
+                mate_arrival(step).wait_recv()
+                core_copy(step, parity).start()
+            for piece in range(2):
+                gather.arrive(3, piece)
+
+        chunk(pick(i, [rank, across(rank, 1), across(rank, 2), across(rank, 3)]))
+        return carry
 
     def mate_copy(step):
         return pltpu.make_async_remote_copy(
-            src_ref=wos.at[:, group], dst_ref=wos.at[:, group], send_sem=d_ss.at[step], recv_sem=d_rs.at[group],
-            device_id={"dp": mate(step)}, device_id_type=MESH)
+            src_ref=wos.at[:, member], dst_ref=wos.at[:, member], send_sem=d_ss.at[step], recv_sem=d_rs.at[member],
+            device_id={"dp": base + mate(step)}, device_id_type=MESH)
 
     def mate_arrival(step):
         piece = mate(step)
         return pltpu.make_async_remote_copy(
             src_ref=wos.at[:, piece], dst_ref=wos.at[:, piece], send_sem=d_ss.at[step], recv_sem=d_rs.at[piece],
-            device_id={"dp": piece}, device_id_type=MESH)
+            device_id={"dp": base + piece}, device_id_type=MESH)
 
     def core_copy(step, owner):
         piece = lax.rem(pair + step, mates) * 2 + owner
@@ -352,86 +390,10 @@
             src_ref=wos.at[:, piece], dst_ref=wos.at[:, piece], send_sem=c_ss.at[step], recv_sem=d_rs.at[piece],
             device_id={"dp": partner}, device_id_type=MESH)
 
-    for step in range(1, mates):
-        mate_copy(step).start()
-    core_copy(0, parity).start()
-    for piece in range(2):
-        gather.arrive(1, piece)
-        gather.arrive(2, piece)
-    chunk(across(rank, 1))
-    chunk(across(rank, 2))
-    for step in range(1, mates):
-        mate_arrival(step).wait_recv()
-        core_copy(step, parity).start()
-    for piece in range(2):
-        gather.arrive(3, piece)
-    chunk(across(rank, 3))
-    for step in range(mates):
-        core_copy(step, 1 - parity).wait_recv()
-    gather.finish()
-    out_gather.finish()
-    for step in range(1, mates):
-        mate_copy(step).wait_send()
-    for step in range(mates):
-        core_copy(step, parity).wait_send()
-    last = [local(xs, x_out, l_sem.at[0]), local(a1s, a1_out, l_sem.at[1]), local(wos, wo_out, l_sem.at[2]),
-            local(qkv.at[0], q_out, l_sem.at[3]), local(qkv.at[1], k_out, l_sem.at[4]), local(qkv.at[2], v_out, l_sem.at[5]),
-            local(cots, cot_out, l_sem.at[6])]
-    for c in last:
+    lax.fori_loop(0, RANKS, chunks, 0)
+    keep += [local(a1s, a1_out, k_sem.at[1])] + [local(qkv.at[i], t, k_sem.at[2 + i]) for i, t in enumerate((q_out, k_out, v_out))]
+    for c in keep[1:]:
         c.start()
-    for c in last:
-        c.wait()
-
-
-def input_kernel(dp, tokens, cotangent, seg_own, w_out, w_query, w_key, w_value, gain, cosine, sine):
-    rows, model = tokens.shape
-    width = w_query.shape[1]
-    length = RANKS * rows
-    part = w_out.shape[0] // dp
-    mates = dp // 2
-    shard = jax.ShapeDtypeStruct((RANKS, rows, model), BF)
-    heads = jax.ShapeDtypeStruct((length, width), BF)
-    outs = pl.pallas_call(
-        functools.partial(input_body, dp),
-        in_specs=[ANY, ANY, VM, ANY, ANY, ANY, ANY, VM, VM, VM],
-        out_specs=[ANY] * 7,
-        out_shape=[shard, shard, heads, heads, heads, jax.ShapeDtypeStruct((RANKS, dp, part, model), BF),
-                   jax.ShapeDtypeStruct((rows, model), BF)],
-        scratch_shapes=[
-            pltpu.VMEM((RANKS, rows, model), BF), pltpu.VMEM((RANKS, rows, model), BF), pltpu.VMEM((3, length, width), BF),
-            pltpu.VMEM((3, model, width), BF), pltpu.VMEM((RANKS, dp, part, model), BF), pltpu.VMEM((rows, model), BF),
-            *LineGather.sems(2), *LineGather.sems(1),
-            DMA((mates,)), DMA((dp,)), DMA((mates,)), DMA((7,)),
-        ],
-        compiler_params=pltpu.CompilerParams(collective_id=1, has_side_effects=True, vmem_limit_bytes=56 << 20),
-        name="input_gather",
-    )(tokens, cotangent, seg_own, w_out.reshape(dp, part, model), w_query, w_key, w_value, gain, cosine, sine)
-    x_all, a1_all, query, key, value, w_out_all, cot_own = outs
-    return x_all, a1_all, query, key, value, w_out_all.reshape(RANKS, dp * part, model), cot_own
-
-
-def attend_body(q, k, v, cot, x_all, wo_all, seg_col, seg_row, gain,
-                p_out, dy_out, a2_out, h_out, ob_out,
-                qkv, ps, dys, obs, xs, wos, hs, a2s, y_ss, y_rs, o_ss, o_rs, l_sem):
-    rank = lax.axis_index("tensor")
-    heads = p_out.shape[0]
-    length = q.shape[0]
-    rows = cot.shape[0]
-    half_rows = rows // 2
-    scale = HD ** (-0.5)
-    loads = [local(cot, dys.at[rank], l_sem.at[0])]
-    loads += [local(t, qkv.at[i], l_sem.at[1 + i]) for i, t in enumerate((q, k, v))]
-    late = [local(x_all, xs, l_sem.at[4]), local(wo_all, wos, l_sem.at[5])]
-    for c in loads + late:
-        c.start()
-    greet(line_peers(rank))
-    grads = LineGather(rank, lambda s, p: dys.at[s, pl.ds(p * half_rows, half_rows)], 2, y_ss, y_rs)
-    attended = LineGather(rank, lambda s, p: obs.at[s, :, pl.ds(pl.multiple_of(p * HD, HD), HD)], heads, o_ss, o_rs)
-    loads[0].wait()
-    grads.start(0)
-    grads.start(1)
-    for c in loads[1:]:
-        c.wait()
 
     def head(h, carry):
         cols = pl.ds(pl.multiple_of(h * HD, HD), HD)
@@ -440,7 +402,7 @@
             scores = dot(qkv[0, start:extent, cols], qkv[1, :extent, cols], ((1,), (1,)))
             row_ids = lax.broadcasted_iota(jnp.int32, (QB, extent), 0) + start
             col_ids = lax.broadcasted_iota(jnp.int32, (QB, extent), 1)
-            allowed = (col_ids <= row_ids) & (seg_col[start:extent, :] == seg_row[:, :extent])
+            allowed = (col_ids <= row_ids) & (segs[start:extent, :1] == seg[:, :extent].astype(F32))
             logits = jnp.where(allowed, scores * scale, NEG)
             expo = jnp.exp(logits - jnp.max(logits, axis=-1, keepdims=True))
             probs = (expo * (1.0 / jnp.sum(expo, axis=-1, keepdims=True))).astype(BF)
@@ -450,18 +412,21 @@
         return carry
 
     lax.fori_loop(0, heads, head, 0)
-    keep = local(ps, p_out, l_sem.at[6])
-    keep.start()
-    for c in late:
-        c.wait()
+    for step in range(mates):
+        core_copy(step, 1 - parity).wait_recv()
+    more = [local(ps, p_out, k_sem.at[5]), local(wos, wo_out, k_sem.at[6])]
+    for c in more:
+        c.start()
+    keep += more
 
     def add(source, first=False, last=False):
         def block(b, carry):
-            part = dot(obs[source, pl.ds(pl.multiple_of(b * rows, rows), rows), :], wos[source])
+            weight = wos[source].reshape(width, model)
+            part = dot(obs[source, pl.ds(pl.multiple_of(b * rows, rows), rows), :], weight)
             total = part + (xs[b].astype(F32) if first else hs[b])
             hs[b] = total
             if last:
-                a2s[b] = (total * norm_factor(total) * gain[...]).astype(BF)
+                xs[b] = (total * norm_factor(total) * gain2[...].reshape(1, model)).astype(BF)
             return carry
 
         lax.fori_loop(0, RANKS, block, 0)
@@ -478,41 +443,55 @@
     for piece in range(2):
         grads.arrive(1, piece)
         grads.arrive(3, piece)
-    dy_done = local(dys, dy_out, l_sem.at[0])
-    dy_done.start()
+    more = [local(dys, dy_out, l_sem.at[0])]
+    more[0].start()
     for piece in range(heads):
         attended.arrive(3, piece)
+    gather.finish()
     add(across(rank, 3), last=True)
-    last = [local(a2s, a2_out, l_sem.at[1]), local(hs.at[rank], h_out, l_sem.at[2]),
-            local(obs.at[:, pl.ds(pl.multiple_of(rank * rows, rows), rows)], ob_out, l_sem.at[3])]
-    for c in last:
+    more += [local(xs, a2_out, l_sem.at[1]), local(hs.at[rank], h_out, l_sem.at[2]),
+             local(obs.at[:, pl.ds(pl.multiple_of(rank * rows, rows), rows)], ob_out, l_sem.at[3])]
+    for c in more[1:]:
         c.start()
+    out_gather.finish()
+    for step in range(1, mates):
+        mate_copy(step).wait_send()
+    for step in range(mates):
+        core_copy(step, parity).wait_send()
     grads.finish()
     attended.finish()
-    for c in last + [keep, dy_done]:
+    for c in keep + more:
         c.wait()
 
 
-def attend_kernel(query, key, value, cot_own, x_all, w_out_all, seg_ids, gain):
-    length, width = query.shape
+def forward_kernel(dp, tokens, cotangent, segments, w_out, w_query, w_key, w_value, gain, gain2, cosine, sine):
+    rows, model = tokens.shape
+    width = w_query.shape[1]
     heads = width // HD
-    rows, model = cot_own.shape
-    shard = (RANKS, rows, model)
-    return pl.pallas_call(
-        attend_body,
-        in_specs=[ANY] * 6 + [VM] * 3,
-        out_specs=[ANY] * 5,
-        out_shape=[jax.ShapeDtypeStruct((heads, length, length), BF), jax.ShapeDtypeStruct(shard, BF), jax.ShapeDtypeStruct(shard, BF),
+    length = RANKS * rows
+    parts = min(dp, 8)
+    mates = parts // 2
+    shape = (RANKS, rows, model)
+    shard, wide = jax.ShapeDtypeStruct(shape, BF), jax.ShapeDtypeStruct((length, width), BF)
+    outs = pl.pallas_call(
+        functools.partial(forward_body, dp),
+        in_specs=[ANY, ANY, VM, ANY, ANY, ANY, ANY, VM, VM, VM, VM],
+        out_specs=[ANY] * 11,
+        out_shape=[shard, wide, wide, wide, jax.ShapeDtypeStruct((RANKS, parts, width // parts, model), BF),
+                   jax.ShapeDtypeStruct((rows, model), BF), jax.ShapeDtypeStruct((heads, length, length), BF), shard, shard,
                    jax.ShapeDtypeStruct((rows, model), F32), jax.ShapeDtypeStruct((RANKS, rows, width), BF)],
         scratch_shapes=[
-            pltpu.VMEM((3, length, width), BF), pltpu.VMEM((heads, length, length), BF), pltpu.VMEM(shard, BF),
-            pltpu.VMEM((RANKS, length, width), BF), pltpu.VMEM(shard, BF), pltpu.VMEM((RANKS, width, model), BF),
-            pltpu.VMEM(shard, F32), pltpu.VMEM(shard, BF),
-            *LineGather.sems(2), *LineGather.sems(heads), DMA((7,)),
+            pltpu.VMEM(shape, BF), pltpu.VMEM(shape, BF), pltpu.VMEM((3, length, width), BF), pltpu.VMEM((3, model, width), BF),
+            pltpu.VMEM((RANKS, parts, width // parts, model), BF), pltpu.VMEM(shape, BF), pltpu.VMEM((RANKS, length, width), BF),
+            pltpu.VMEM((heads, length, length), BF), pltpu.VMEM(shape, F32), pltpu.VMEM((length, HD), F32),
+            *LineGather.sems(2), *LineGather.sems(1), DMA((mates,)), DMA((parts,)), DMA((mates,)),
+            *LineGather.sems(2), *LineGather.sems(heads), DMA((6,)), DMA((7,)),
         ],
-        compiler_params=pltpu.CompilerParams(collective_id=2, has_side_effects=True, vmem_limit_bytes=60 << 20),
-        name="attend_gather",
-    )(query, key, value, cot_own, x_all, w_out_all, seg_ids.reshape(length, 1), seg_ids.reshape(1, length), gain)
+        compiler_params=pltpu.CompilerParams(collective_id=1, has_side_effects=True, vmem_limit_bytes=62 << 20),
+        name="forward_gather",
+    )(tokens, cotangent, segments, w_out.reshape(parts, width // parts, model), w_query, w_key, w_value, gain, gain2, cosine, sine)
+    a1_all, query, key, value, w_out_all, cot_own, probs, dy, a2, hidden, attended = outs
+    return a1_all, query, key, value, w_out_all.reshape(RANKS, width, model), cot_own, probs, dy, a2, hidden, attended
 
 
 def pick(step, choices):
@@ -633,7 +612,7 @@
     scatter.total(total)
     values, gradient = hs[...], total[...]
     factor = norm_factor(values)
-    back_rows, gain_rows = norm_back(values, factor, gain[...], gradient)
+    back_rows, gain_rows = norm_back(values, factor, gain[...].reshape(1, model), gradient)
     total[...] = cots[...].astype(F32) + back_rows
     gains[...] = gain_rows.reshape(1, model)
     last = [local(total, dh_out, l_sem.at[1]), local(gains, gain_out, l_sem.at[2])]
@@ -796,13 +775,13 @@
         functools.partial(attention_back_body, dp),
         in_specs=[ANY] * 9 + [VM, VM],
         out_specs=[ANY] * 5,
-        out_shape=[jax.ShapeDtypeStruct((rows, model), BF), heads, heads, heads, jax.ShapeDtypeStruct((count, share, columns), F32)],
+        out_shape=[jax.ShapeDtypeStruct((rows, model), BF), heads, heads, heads, jax.ShapeDtypeStruct((count, share, columns), BF)],
         scratch_shapes=[
             pltpu.VMEM((rows, model), F32), pltpu.VMEM((rows, model), BF), pltpu.VMEM((RANKS, width, model), BF),
             pltpu.VMEM(shard, BF), pltpu.VMEM(shard, BF), pltpu.VMEM((3, rows, width), BF), pltpu.VMEM((length, width), BF),
             pltpu.VMEM((3, length, width), BF), pltpu.VMEM((2, length, length), BF), pltpu.VMEM((length, length), BF),
             pltpu.VMEM((3, length, width), BF), pltpu.VMEM((rows, model), F32), pltpu.VMEM((rows, model), BF),
-            pltpu.VMEM((count, mates, share, columns), BF), pltpu.VMEM((count, share, columns), F32),
+            pltpu.VMEM((count, mates, share, columns), BF), pltpu.VMEM((count, share, columns), BF),
             *GroupReduce.box_shapes(dp, count, share, columns, columns // 2), *GroupReduce.sem_shapes(dp, count),
             *LineScatter.sems(2), DMA((4,)), DMA((RANKS,)), DMA((7,)), DMA((2,)), DMA((count,)),
         ],
@@ -895,7 +874,7 @@
     done[0].start()
     scatter.total(total)
     values, gradient = xs[...].astype(F32), total[...]
-    back_rows, gain_rows = norm_back(values, norm_factor(values), gain[...], gradient)
+    back_rows, gain_rows = norm_back(values, norm_factor(values), gain[...].reshape(1, model), gradient)
     dxs[...] = (dhs[...] + back_rows).astype(BF)
     done.append(local(dxs, dx_out, l_sem.at[1]))
     done[1].start()
@@ -961,47 +940,87 @@
     )(grad_q, grad_k, grad_v, a1_all.reshape(length, model), w_query, w_key, w_value, tokens, grad_hidden, attended_own, gain, gain_two)
 
 
+def finish_body(output, dx, gains, mixed, out_t, ff,
+                output_out, dx_out, gain1_out, gain2_out, q_out, k_out, v_out, wo_out, gate_out, up_out, down_out,
+                b0, b1, gs, g1, g2, ms, ot, fs, gate, up, down, i_sem, o_sem):
+    width = q_out.shape[1]
+    loads = [local(s, t, i_sem.at[i]) for i, (s, t) in enumerate(
+        ((ff.at[2], fs.at[2]), (ff.at[0], fs.at[0]), (ff.at[1], fs.at[1]), (mixed, ms), (output, b0), (dx, b1), (out_t, ot), (gains, gs)))]
+    for c in loads:
+        c.start()
+    sent = []
+
+    def put(source, target):
+        sent.append(local(source, target, o_sem.at[len(sent)]))
+        sent[-1].start()
+
+    loads[1].wait()
+    gate[...] = fs[0].astype(F32)
+    put(gate, gate_out)
+    loads[2].wait()
+    up[...] = fs[1].astype(F32)
+    put(up, up_out)
+    loads[4].wait()
+    put(b0, output_out)
+    loads[5].wait()
+    put(b1, dx_out)
+    loads[3].wait()
+    for i, target in enumerate((q_out, k_out, v_out)):
+        put(ms.at[:, pl.ds(i * width, width)], target)
+    loads[0].wait()
+    down[...] = fs[2].astype(F32)
+    put(down, down_out)
+    loads[6].wait()
+    put(ot, wo_out)
+    loads[7].wait()
+    g1[...] = gs[0]
+    put(g1, gain1_out)
+    g2[...] = gs[1]
+    put(g2, gain2_out)
+    for c in sent:
+        c.wait()
+
+
+def finish_kernel(output, dx, gains, mixed, out_t, ff):
+    rows, model = output.shape
+    share, width = out_t.shape
+    columns = ff.shape[2]
+    gain, head, wide = ((model,), F32), ((share, width), F32), ((share, columns), F32)
+    outs = [((rows, model), BF), ((rows, model), BF), gain, gain, head, head, head, head, wide, wide, wide]
+    return pl.pallas_call(
+        finish_body,
+        in_specs=[ANY] * 6,
+        out_specs=[ANY] * 11,
+        out_shape=[jax.ShapeDtypeStruct(*o) for o in outs],
+        scratch_shapes=[
+            pltpu.VMEM((rows, model), BF), pltpu.VMEM((rows, model), BF), pltpu.VMEM((2, model), F32), pltpu.VMEM((model,), F32), pltpu.VMEM((model,), F32),
+            pltpu.VMEM((share, 3 * width), F32), pltpu.VMEM((share, width), F32),
+            pltpu.VMEM((3, share, columns), BF), pltpu.VMEM((share, columns), F32), pltpu.VMEM((share, columns), F32), pltpu.VMEM((share, columns), F32),
+            DMA((8,)), DMA((11,)),
+        ],
+        compiler_params=pltpu.CompilerParams(vmem_limit_bytes=63 << 20),
+        name="finish",
+    )(output, dx, gains, mixed, out_t, ff)
+
+
 def on_device(tokens, segments, granularity, norm1_gain, norm2_gain, w_query, w_key, w_value, w_out, w_gate, w_up, w_down, cotangent):
-    own_rows, model = tokens.shape
     length = segments.shape[1]
-    heads_width = w_query.shape[1]
-    width_here = w_gate.shape[1]
-    ranks = length // own_rows
-    tensor_rank = lax.axis_index("tensor")
-    seg_ids = segments.reshape(length)
     cosine, sine = (jnp.asarray(t) for t in rope_numpy(length))
     dp = lax.axis_size("dp")
-    seg_own = lax.dynamic_slice_in_dim(seg_ids, tensor_rank * own_rows, own_rows, 0).reshape(own_rows, 1)
-
-    x_all, a1_all, query_rot, key_rot, value_low, w_out_all, cot_own = input_kernel(
-        dp, tokens, cotangent, seg_own, w_out, w_query, w_key, w_value, norm1_gain.reshape(1, model), cosine, sine
+    a1_all, query_rot, key_rot, value_low, w_out_all, cot_own, probs_low, grad_rows, rows_two, hidden_own, attended_own = forward_kernel(
+        dp, tokens, cotangent, segments, w_out, w_query, w_key, w_value, norm1_gain, norm2_gain, cosine, sine
     )
-    probs_low, grad_rows, rows_two, hidden_own, attended_own = attend_kernel(
-        query_rot, key_rot, value_low, cot_own, x_all, w_out_all, seg_ids, norm2_gain.reshape(1, model)
-    )
-    rows_one = a1_all.reshape(length, model)
     grads_ff, down_parts, grad_hidden, gain_two = mlp_kernel(
-        dp, rows_two, grad_rows, w_gate, w_up, w_down, hidden_own, cot_own, granularity, norm2_gain.reshape(1, model)
+        dp, rows_two, grad_rows, w_gate, w_up, w_down, hidden_own, cot_own, granularity, norm2_gain
     )
     output, grad_q, grad_k, grad_v, own_ff = attention_back_kernel(
         dp, grad_hidden, w_out_all, down_parts, grads_ff, query_rot, key_rot, value_low, probs_low, hidden_own, cosine, sine
     )
     grad_tokens, gains, own_qkv, own_out = input_back_kernel(
-        dp, grad_q, grad_k, grad_v, a1_all, w_query, w_key, w_value, tokens, grad_hidden, attended_own, norm1_gain.reshape(1, model), gain_two
+        dp, grad_q, grad_k, grad_v, a1_all, w_query, w_key, w_value, tokens, grad_hidden, attended_own, norm1_gain, gain_two
     )
-    return (
-        output,
-        grad_tokens,
-        gains[0],
-        gains[1],
-        own_qkv[:, :heads_width],
-        own_qkv[:, heads_width : 2 * heads_width],
-        own_qkv[:, 2 * heads_width :],
-        own_out.T,
-        own_ff[0],
-        own_ff[1],
-        own_ff[2].T,
-    )
+    outs = finish_kernel(output, grad_tokens, gains, own_qkv, own_out, own_ff)
+    return tuple(o.T if i in (7, 10) else o for i, o in enumerate(outs))
 
 
 def solution(mesh):

time: 429 us -> 404 us (0.942)
  local copies, waits for them, and re-layouts: 15.7 us -> 0 us
  Pallas kernels: 411 us -> 402 us
    pallas_call x2, Pallas kernels: 189 us -> 180 us  [the longest x1 176 us: forward_kernel(): pl.pallas_call(functools.partial(forward_body, dp), in_specs=[ANY, ANY, V...]
where the time goes in v4:
time: 404 us
  Pallas kernels  402 us (100%)
    pallas_call x1, Pallas kernels, forward_kernel(): pl.pallas_call(functools.partial(forward_body, dp), in_specs=[ANY, ANY, V...  176 us
    pallas_call x1, Pallas kernels, input_back_kernel(): pl.pallas_call(functools.partial(input_back_body, dp), in_specs=[ANY] * 1...  77.9 us
    pallas_call x1, Pallas kernels, attention_back_kernel(): pl.pallas_call(functools.partial(attention_back_body, dp), in_specs=[ANY]...  76.2 us
    pallas_call x1, Pallas kernels, mlp_kernel(): pl.pallas_call(mlp_body, in_specs=[ANY] * 7 + [pl.BlockSpec(memory_space=...  68.1 us

profile of v4, /device:TPU:0, one launch (start us, length us, event | category | flops | bytes accessed | tf_op | source)
XLA Modules:
  0.0 403.8 jit_solution(9227221314264377721)
XLA Ops:
  1.3 176.0 %forward_gather.1 = (bf16[4,256,1536]{2,1,0:T(8,128)(2,1)}, bf16[1024,384]{1,0:T(8,128)(2,1)}, bf16[1024,384]{1,0:T(8,128)(2,1)}, bf16[1024,384]{1,0:T(8,128)(2,...) custom-call(bf16[256,1536]{1,0:T(8,128)(2,1)} %tok.3, ...), custom_call_target="tpu_custom_call" | custom-call | tf_op jit(solution)/shard_map/forward_gather/pallas_call | solution.py:476
  177.3 68.1 %mlp_scatter.1 = (bf16[3,8,192,1536]{3,2,1,0:T(8,128)(2,1)}, bf16[4,256,1536]{2,1,0:T(8,128)(2,1)}, f32[256,1536]{1,0:T(8,128)}, f32[1,1536]{1,0:T(1,128)}) custom-call(bf16[4,256,1536]{2,1,0:T(8,128)(2,1)} %get-tuple-element.46.a2, bf16[4,256,1536]{2,1,0:T(8,128)(2,1)} %get-tuple-element.47.dy, bf16[1536,1536]{1,0:T(8,128)(2,1)} %wg.1, ...), custom_call_target="tpu_custom_call" | custom-call | tf_op jit(solution)/shard_map/mlp_scatter/pallas_call | solution.py:633
  245.4 76.2 %attention_back.1 = (bf16[256,1536]{1,0:T(8,128)(2,1)}, bf16[1024,384]{1,0:T(8,128)(2,1)}, bf16[1024,384]{1,0:T(8,128)(2,1)}, bf16[1024,384]{1,0:T(8,128)(2,1)}, bf16[3,192,1536]{2,1,0:T(8,128)(2,1)}) custom-call(f32[256,1536]{1,0:T(8,128)} %get-tuple-element.50.dh, bf16[4,384,1536]{2,1,0:T(8,128)(2,1)} %bitcast.7, ...), custom_call_target="tpu_custom_call" | custom-call | tf_op jit(solution)/shard_map/attention_back/pallas_call | solution.py:774
  321.6 77.9 %input_back.1 = (bf16[256,1536]{1,0:T(8,128)(2,1)}, f32[2,1536]{1,0:T(2,128)}, f32[192,1152]{1,0:T(8,128)}, f32[192,384]{1,0:T(8,128)}) custom-call(bf16[1024,384]{1,0:T(8,128)(2,1)} %get-tuple-element.59.dq, bf16[1024,384]{1,0:T(8,128)(2,1)} %get-tuple-element.60.dk, bf16[1024,384]{1,0:T(8,128)(2,1)} %get-tuple-element.61.dv, bf16[1024,1536]{1,0:T(8,128)(2,1)} %bitcast.8, ...), custom_call_target="tpu_custom_call" | custom-call | tf_op jit(solution)/shard_map/input_back/pallas_call | solution.py:919
  399.5 4.1 %finish.1 = (bf16[256,1536]{1,0:T(8,128)(2,1)}, bf16[256,1536]{1,0:T(8,128)(2,1)}, f32[1536]{0:T(1024)}, f32[1536]{0:T(1024)}, f32[192,384]{1,0:T(8,128)}, /*ind...) custom-call(bf16[256,1536]{1,0:T(8,128)(2,1)} %get-tuple-element.58., ...), custom_call_target="tpu_custom_call" | custom-call | tf_op jit(solution)/shard_map/finish/pallas_call | solution.py:990

commit v5 on v4

--- a/solution.py
+++ b/solution.py
@@ -135,8 +135,8 @@
             device_id={"tensor": across(self.rank, k)}, device_id_type=MESH,
         )
 
-    def send_far(self):
-        for piece in range(self.pieces):
+    def send_far(self, pieces=None):
+        for piece in pieces or range(self.pieces):
             pl.when(self.inner)(lambda: self.copy(3, 3, 3, piece).start())
             pl.when(self.end)(lambda: self.copy(3, 0, 1, piece).start())
 
@@ -295,7 +295,7 @@
 def forward_body(dp, tok, cot, seg, wo, wq, wk, wv, gain, gain2, cosine, sine,
                  a1_out, q_out, k_out, v_out, wo_out, cot_out, p_out, dy_out, a2_out, h_out, ob_out,
                  xs, a1s, qkv, ws, wos, dys, obs, ps, hs, segs,
-                 x_ss, x_rs, z_ss, z_rs, d_ss, d_rs, c_ss, y_ss, y_rs, o_ss, o_rs, l_sem, k_sem):
+                 x_ss, x_rs, z_ss, z_rs, d_ss, d_rs, c_ss, y_ss, y_rs, o_ss, o_rs, l_sem, k_sem, b_sem):
     rank, group = lax.axis_index("tensor"), lax.axis_index("dp")
     rows, model = tok.shape
     length, width = q_out.shape
@@ -427,6 +427,7 @@
             hs[b] = total
             if last:
                 xs[b] = (total * norm_factor(total) * gain2[...].reshape(1, model)).astype(BF)
+                local(xs.at[b], a2_out.at[b], b_sem.at[b]).start()
             return carry
 
         lax.fori_loop(0, RANKS, block, 0)
@@ -449,7 +450,7 @@
         attended.arrive(3, piece)
     gather.finish()
     add(across(rank, 3), last=True)
-    more += [local(xs, a2_out, l_sem.at[1]), local(hs.at[rank], h_out, l_sem.at[2]),
+    more += [local(hs.at[rank], h_out, l_sem.at[2]),
              local(obs.at[:, pl.ds(pl.multiple_of(rank * rows, rows), rows)], ob_out, l_sem.at[3])]
     for c in more[1:]:
         c.start()
@@ -462,6 +463,8 @@
     attended.finish()
     for c in keep + more:
         c.wait()
+    for b in range(RANKS):
+        local(xs.at[b], a2_out.at[b], b_sem.at[b]).wait()
 
 
 def forward_kernel(dp, tokens, cotangent, segments, w_out, w_query, w_key, w_value, gain, gain2, cosine, sine):
@@ -485,7 +488,7 @@
             pltpu.VMEM((RANKS, parts, width // parts, model), BF), pltpu.VMEM(shape, BF), pltpu.VMEM((RANKS, length, width), BF),
             pltpu.VMEM((heads, length, length), BF), pltpu.VMEM(shape, F32), pltpu.VMEM((length, HD), F32),
             *LineGather.sems(2), *LineGather.sems(1), DMA((mates,)), DMA((parts,)), DMA((mates,)),
-            *LineGather.sems(2), *LineGather.sems(heads), DMA((6,)), DMA((7,)),
+            *LineGather.sems(2), *LineGather.sems(heads), DMA((6,)), DMA((7,)), DMA((RANKS,)),
         ],
         compiler_params=pltpu.CompilerParams(collective_id=1, has_side_effects=True, vmem_limit_bytes=62 << 20),
         name="forward_gather",
@@ -523,7 +526,7 @@
     limit = FF // 8 * lax.shift_left(1, gran[0] - 1) - rank * width
 
     def step(i, carry):
-        j = pick(i, order)
+        where = pl.ds(pl.multiple_of(pick(i, order) * rows, rows), rows)
 
         def tile(t, inner_carry):
             cols = pl.ds(pl.multiple_of(t * FT, FT), FT)
@@ -533,27 +536,27 @@
                 loads[0].wait()
                 loads[1].wait()
 
-            gate = dot(lefts[0, j], ws[0, :, cols])
+            gate = dot(lefts[0, where, :], ws[0, :, cols])
 
             @pl.when((i == 0) & (t == 0))
             def _():
                 loads[2].wait()
 
-            up = dot(lefts[0, j], ws[1, :, cols])
+            up = dot(lefts[0, where, :], ws[1, :, cols])
 
             @pl.when((i == 0) & (t == 0))
             def _():
                 loads[3].wait()
                 loads[4].wait()
 
-            dz = dot(lefts[1, j], ws[2, cols, :], ((1,), (1,)))
+            dz = dot(lefts[1, where, :], ws[2, cols, :], ((1,), (1,)))
             unit = lax.broadcasted_iota(jnp.int32, gate.shape, 1) + t * FT
             mask = unit < limit
             sigma = jax.nn.sigmoid(gate)
             active = jnp.where(mask, gate * sigma, 0.0)
-            acts[2, j, :, cols] = (active * up).astype(BF)
-            acts[0, j, :, cols] = jnp.where(mask, dz * up * sigma * (1.0 + gate * (1.0 - sigma)), 0.0).astype(BF)
-            acts[1, j, :, cols] = (dz * active).astype(BF)
+            acts[2, where, cols] = (active * up).astype(BF)
+            acts[0, where, cols] = jnp.where(mask, dz * up * sigma * (1.0 + gate * (1.0 - sigma)), 0.0).astype(BF)
+            acts[1, where, cols] = (dz * active).astype(BF)
             return inner_carry
 
         lax.fori_loop(0, width // FT, tile, 0)
@@ -561,7 +564,7 @@
         def back(t, inner_carry):
             cols = pl.ds(pl.multiple_of(t * FT, FT), FT)
             parts[3 - i, :, cols] = (
-                dot(acts[0, j], ws[0, cols, :], ((1,), (1,))) + dot(acts[1, j], ws[1, cols, :], ((1,), (1,)))
+                dot(acts[0, where, :], ws[0, cols, :], ((1,), (1,))) + dot(acts[1, where, :], ws[1, cols, :], ((1,), (1,)))
             ).astype(BF)
             return inner_carry
 
@@ -588,9 +591,7 @@
         w, b = lax.div(i, blocks), lax.rem(i, blocks)
         left = lax.div(w, 2)
         cols = pl.ds(pl.multiple_of(b * WB, WB), WB)
-        value = dot(lefts[left, 0, :, cols], acts[w, 0], ((0,), (0,)))
-        for s in range(1, RANKS):
-            value += dot(lefts[left, s, :, cols], acts[w, s], ((0,), (0,)))
+        value = dot(lefts[left, :, cols], acts[w], ((0,), (0,)))
         pl.when(i >= 2)(lambda: put(i - 2, slot).wait())
         low = value.astype(BF)
         for p in range(per):
@@ -601,7 +602,8 @@
     lax.fori_loop(0, 3 * blocks, grads, 0)
 
     def down(i, carry):
-        downs[3 - i] = dot(acts[2, pick(i, order)], ws[2]).astype(BF)
+        where = pl.ds(pl.multiple_of(pick(i, order) * rows, rows), rows)
+        downs[3 - i] = dot(acts[2, where, :], ws[2]).astype(BF)
         return carry
 
     lax.fori_loop(0, 4, down, 0)
@@ -637,14 +639,14 @@
         out_shape=[jax.ShapeDtypeStruct((3, dp, share, width), BF), jax.ShapeDtypeStruct(shard, BF),
                    jax.ShapeDtypeStruct((rows, model), F32), jax.ShapeDtypeStruct((1, model), F32)],
         scratch_shapes=[
-            pltpu.VMEM((2, *shard), BF), pltpu.VMEM((3, RANKS, rows, width), BF), pltpu.VMEM((3, model, width), BF),
+            pltpu.VMEM((2, RANKS * rows, model), BF), pltpu.VMEM((3, RANKS * rows, width), BF), pltpu.VMEM((3, model, width), BF),
             pltpu.VMEM(shard, BF), pltpu.VMEM(shard, BF), pltpu.VMEM((2, WB // share, share, width), BF), pltpu.VMEM(shard, BF),
             pltpu.VMEM((rows, model), F32), pltpu.VMEM((rows, model), BF), pltpu.VMEM((rows, model), F32), pltpu.VMEM((1, model), F32),
             *LineScatter.sems(2), DMA((7,)), DMA((2,)),
         ],
         compiler_params=pltpu.CompilerParams(collective_id=3, has_side_effects=True, vmem_limit_bytes=63 << 20),
         name="mlp_scatter",
-    )(a2, dy, w_gate, w_up, w_down, hidden_own, cot_own, granularity, gain)
+    )(a2.reshape(-1, model), dy.reshape(-1, model), w_gate, w_up, w_down, hidden_own, cot_own, granularity, gain)
 
 
 def attention_back_body(dp, dh, wo_all, downs, grads, q, k, v, p_all, hid, cosine, sine,
@@ -659,7 +661,7 @@
     heads, half, scale = width // HD, HD // 2, HD ** (-0.5)
     count = grads.shape[0]
     parity = lax.rem(group, 2)
-    loads = [local(dh, dhs, l_sem.at[0]), local(wo_all, wos, l_sem.at[1]), local(downs, parts, l_sem.at[2])]
+    loads = [local(downs, parts, l_sem.at[2]), local(dh, dhs, l_sem.at[0]), local(wo_all, wos, l_sem.at[1])]
     owns = [local(grads.at[w, :, parity], kept.at[w], f_sem.at[w]) for w in range(count)]
     late = [local(t, qkv.at[i], l_sem.at[3 + i]) for i, t in enumerate((q, k, v))] + [local(hid, hs, l_sem.at[6])]
     for c in loads + owns + late:
@@ -676,6 +678,8 @@
     for w in range(count):
         reduce.start0(w)
     scatter = LineScatter(rank, parts, inbox, r_ss, r_rs, 2)
+    loads[0].wait()
+    scatter.send_far([0])
 
     def exchange(k, source):
         where = pl.ds(pl.multiple_of(source * rows, rows), rows)
@@ -683,17 +687,16 @@
             src_ref=dobs.at[k - 1], dst_ref=dos.at[where], send_sem=a_ss.at[k], recv_sem=a_rs.at[source],
             device_id={"tensor": across(rank, k)}, device_id_type=MESH)
 
-    loads[0].wait()
+    loads[1].wait()
     low[...] = dhs[...].astype(BF)
-    loads[1].wait()
+    loads[2].wait()
     for k in (3, 2, 1):
         dobs[k - 1] = dot(low[...], wos[across(rank, k)], ((1,), (1,))).astype(BF)
         exchange(k, rank).start()
-    dos[pl.ds(pl.multiple_of(rank * rows, rows), rows), :] = dot(low[...], wos[rank], ((1,), (1,))).astype(BF)
-    loads[2].wait()
-    scatter.send_far()
+    scatter.send_far([1])
     scatter.send_two_end()
     scatter.send_near()
+    dos[pl.ds(pl.multiple_of(rank * rows, rows), rows), :] = dot(low[...], wos[rank], ((1,), (1,))).astype(BF)
     for c in owns:
         c.wait()
 
@@ -807,7 +810,7 @@
     parity = lax.rem(group, 2)
     loads = [local(t, dqkv.at[i], l_sem.at[i]) for i, t in enumerate((dq, dk, dv))]
     loads += [local(t, ws.at[i], l_sem.at[3 + i]) for i, t in enumerate((wq, wk, wv))]
-    late = [local(dh, dhs, l_sem.at[6]), local(ob, obs, l_sem.at[7]), local(a1, a1s, l_sem.at[8]), local(tok, xs, l_sem.at[9])]
+    late = [local(a1, a1s, l_sem.at[8]), local(dh, dhs, l_sem.at[6]), local(ob, obs, l_sem.at[7]), local(tok, xs, l_sem.at[9])]
     for c in loads + late:
         c.start()
     scatter = LineScatter(rank, parts, inbox, r_ss, r_rs, 2)
@@ -827,10 +830,37 @@
         pl.when(i == 0)(scatter.send_far)
         pl.when(i == 1)(scatter.send_two_end)
         pl.when(i == 2)(scatter.send_near)
+
+        @pl.when(i == 0)
+        def _():
+            late[0].wait()
+
+        row = jnp.sum(value * a1s[where, :].astype(F32), axis=0, keepdims=True)
+        gbuf[0, 0:1, :] = jnp.where(i == 0, row, gbuf[0, 0:1, :] + row)
         return carry
 
+    gbuf[0, 0:1, :] = jnp.zeros((1, model), F32)
     lax.fori_loop(0, 4, step, 0)
-    for c in late:
+    gbuf[0, 0:1, :] = gbuf[0, 0:1, :] / gain[...].reshape(1, model)
+    gbuf[0, 1:2, :] = gain2[...]
+
+    def swap(t):
+        return pltpu.make_async_remote_copy(
+            src_ref=gbuf.at[t], dst_ref=gbox.at[t], send_sem=g_ss.at[t], recv_sem=g_rs.at[t], device_id={"dp": flip(group, t)}, device_id_type=MESH)
+
+    def advance(t):
+        swap(t).wait_recv()
+        gbuf[t + 1] = gbuf[t] + gbox[t]
+        if t + 1 < bits:
+            swap(t + 1).start()
+
+    def share_gains(k, source):
+        return pltpu.make_async_remote_copy(
+            src_ref=gbuf.at[bits], dst_ref=gbox.at[bits + source], send_sem=g_ss.at[bits + k], recv_sem=g_rs.at[bits + source],
+            device_id={"tensor": across(rank, k)}, device_id_type=MESH)
+
+    swap(0).start()
+    for c in late[1:]:
         c.wait()
     low[...] = dhs[...].astype(BF)
 
@@ -843,6 +873,7 @@
         return carry
 
     lax.fori_loop(0, model // WB, out_block, 0)
+    advance(0)
     output.start0(0)
 
     def mixed_block(b, carry):
@@ -854,6 +885,11 @@
         return carry
 
     lax.fori_loop(0, model // WB, mixed_block, 0)
+    for t in range(1, bits):
+        advance(t)
+    for k in (1, 2, 3):
+        share_gains(k, rank).start()
+    gbox[bits + rank] = gbuf[bits]
     mixed.start0(0)
     output.add0(0)
     mixed.add0(0)
@@ -874,27 +910,18 @@
     done[0].start()
     scatter.total(total)
     values, gradient = xs[...].astype(F32), total[...]
-    back_rows, gain_rows = norm_back(values, norm_factor(values), gain[...].reshape(1, model), gradient)
+    back_rows, _ = norm_back(values, norm_factor(values), gain[...].reshape(1, model), gradient)
     dxs[...] = (dhs[...] + back_rows).astype(BF)
     done.append(local(dxs, dx_out, l_sem.at[1]))
     done[1].start()
-    gbuf[0, 0:1, :] = gain_rows.reshape(1, model)
-    gbuf[0, 1:2, :] = gain2[...]
-    turns = [{"tensor": across(rank, 1)}, {"tensor": across(rank, 2)}] + [{"dp": flip(group, b)} for b in range(bits)]
-
-    def swap(t):
-        return pltpu.make_async_remote_copy(
-            src_ref=gbuf.at[t], dst_ref=gbox.at[t], send_sem=g_ss.at[t], recv_sem=g_rs.at[t], device_id=turns[t], device_id_type=MESH)
-
-    swap(0).start()
+    for k in (1, 2, 3):
+        share_gains(k, across(rank, k)).wait_recv()
+    for t in range(bits):
+        swap(t).wait_send()
+    gbuf[0] = ((gbox[bits] + gbox[bits + 1]) + gbox[bits + 2]) + gbox[bits + 3]
+    done.append(local(gbuf.at[0], gains_out, l_sem.at[2]))
+    done[2].start()
     ends.send_two_inner()
-    for t in range(len(turns)):
-        swap(t).wait_recv()
-        gbuf[t + 1] = gbuf[t] + gbox[t]
-        if t + 1 < len(turns):
-            swap(t + 1).start()
-    done.append(local(gbuf.at[len(turns)], gains_out, l_sem.at[2]))
-    done[2].start()
     ends.total(f3)
     done.append(local(f3, gout_out, l_sem.at[3]))
     done[3].start()
@@ -902,8 +929,8 @@
     ends.finish()
     mixed.finish(1)
     output.finish(1)
-    for t in range(len(turns)):
-        swap(t).wait_send()
+    for k in (1, 2, 3):
+        share_gains(k, rank).wait_send()
     for c in done:
         c.wait()
 
@@ -929,11 +956,11 @@
             pltpu.VMEM((dp, share, wide[0]), BF), pltpu.VMEM((dp, share, wide[1]), BF),
             pltpu.VMEM((share, wide[0]), F32), pltpu.VMEM((share, wide[1]), F32),
             pltpu.VMEM((RANKS, share, width), BF), pltpu.VMEM((RANKS, share, width), BF), pltpu.VMEM((share, width), F32),
-            pltpu.VMEM((bits + 3, 2, model), F32), pltpu.VMEM((bits + 2, 2, model), F32),
+            pltpu.VMEM((bits + 1, 2, model), F32), pltpu.VMEM((bits + RANKS, 2, model), F32),
             pltpu.VMEM((rows, model), F32), pltpu.VMEM((rows, model), BF),
             *GroupReduce.box_shapes(dp, 1, share, wide[0], splits[0]), *GroupReduce.box_shapes(dp, 1, share, wide[1], splits[1]),
             *GroupReduce.sem_shapes(dp, 1), *GroupReduce.sem_shapes(dp, 1),
-            *LineScatter.sems(2), *LineScatter.sems(1), DMA((bits + 2,)), DMA((bits + 2,)), DMA((10,)),
+            *LineScatter.sems(2), *LineScatter.sems(1), DMA((bits + RANKS,)), DMA((bits + RANKS,)), DMA((10,)),
         ],
         compiler_params=pltpu.CompilerParams(collective_id=5, has_side_effects=True, vmem_limit_bytes=63 << 20),
         name="input_back",

time: 404 us -> 393 us (0.973)
  Pallas kernels: 402 us -> 391 us
    pallas_call x1, Pallas kernels: 77.9 us -> 68.6 us  [input_back_kernel(): pl.pallas_call(functools.partial(input_back_body, dp), in_specs=[ANY] * 1...]
where the time goes in v5:
time: 393 us; the launch traced here: 392 us
  Pallas kernels  391 us (99%)
    pallas_call x1, Pallas kernels, forward_kernel(): pl.pallas_call(functools.partial(forward_body, dp), in_specs=[ANY, ANY, V...  175 us
    pallas_call x1, Pallas kernels, attention_back_kernel(): pl.pallas_call(functools.partial(attention_back_body, dp), in_specs=[ANY]...  74.7 us
    pallas_call x1, Pallas kernels, input_back_kernel(): pl.pallas_call(functools.partial(input_back_body, dp), in_specs=[ANY] * 1...  68.6 us
    pallas_call x1, Pallas kernels, mlp_kernel(): pl.pallas_call(mlp_body, in_specs=[ANY] * 7 + [pl.BlockSpec(memory_space=...  68.1 us

profile of v5, /device:TPU:0, one launch (start us, length us, event | category | flops | bytes accessed | tf_op | source)
XLA Modules:
  0.0 392.2 jit_solution(18309230797946892036)
XLA Ops:
  1.3 175.2 %forward_gather.1 = (bf16[4,256,1536]{2,1,0:T(8,128)(2,1)}, bf16[1024,384]{1,0:T(8,128)(2,1)}, bf16[1024,384]{1,0:T(8,128)(2,1)}, bf16[1024,384]{1,0:T(8,128)(2,...) custom-call(bf16[256,1536]{1,0:T(8,128)(2,1)} %tok.3, ...), custom_call_target="tpu_custom_call" | custom-call | tf_op jit(solution)/shard_map/forward_gather/pallas_call | solution.py:479
  176.5 68.1 %mlp_scatter.1 = (bf16[3,8,192,1536]{3,2,1,0:T(8,128)(2,1)}, bf16[4,256,1536]{2,1,0:T(8,128)(2,1)}, f32[256,1536]{1,0:T(8,128)}, f32[1,1536]{1,0:T(1,128)}) custom-call(bf16[1024,1536]{1,0:T(8,128)(2,1)} %bitcast.11, bf16[1024,1536]{1,0:T(8,128)(2,1)} %bitcast.10, bf16[1536,1536]{1,0:T(8,128)(2,1)} %wg.1, bf16[1536,1536]{1,0:T(8,128)(2,1)} %wu.1, ...), custom_call_target="tpu_custom_call" | custom-call | tf_op jit(solution)/shard_map/mlp_scatter/pallas_call | solution.py:635
  244.6 74.7 %attention_back.1 = (bf16[256,1536]{1,0:T(8,128)(2,1)}, bf16[1024,384]{1,0:T(8,128)(2,1)}, bf16[1024,384]{1,0:T(8,128)(2,1)}, bf16[1024,384]{1,0:T(8,128)(2,1)}, bf16[3,192,1536]{2,1,0:T(8,128)(2,1)}) custom-call(f32[256,1536]{1,0:T(8,128)} %get-tuple-element.50.dh, bf16[4,384,1536]{2,1,0:T(8,128)(2,1)} %bitcast.9, ...), custom_call_target="tpu_custom_call" | custom-call | tf_op jit(solution)/shard_map/attention_back/pallas_call | solution.py:777
  319.3 68.6 %input_back.1 = (bf16[256,1536]{1,0:T(8,128)(2,1)}, f32[2,1536]{1,0:T(2,128)}, f32[192,1152]{1,0:T(8,128)}, f32[192,384]{1,0:T(8,128)}) custom-call(bf16[1024,384]{1,0:T(8,128)(2,1)} %get-tuple-element.59.dq, bf16[1024,384]{1,0:T(8,128)(2,1)} %get-tuple-element.60.dk, bf16[1024,384]{1,0:T(8,128)(2,1)} %get-tuple-element.61.dv, bf16[1024,1536]{1,0:T(8,128)(2,1)} %bitcast.12, ...), custom_call_target="tpu_custom_call" | custom-call | tf_op jit(solution)/shard_map/input_back/pallas_call | solution.py:946
  387.9 4.1 %finish.1 = (bf16[256,1536]{1,0:T(8,128)(2,1)}, bf16[256,1536]{1,0:T(8,128)(2,1)}, f32[1536]{0:T(1024)}, f32[1536]{0:T(1024)}, f32[192,384]{1,0:T(8,128)}, /*ind...) custom-call(bf16[256,1536]{1,0:T(8,128)(2,1)} %get-tuple-element.58., ...), custom_call_target="tpu_custom_call" | custom-call | tf_op jit(solution)/shard_map/finish/pallas_call | solution.py:1017

commit v6 on v5

--- a/solution.py
+++ b/solution.py
@@ -321,7 +321,13 @@
     greet(line_peers(rank) + [{"dp": partner}] + [{"dp": base + mate(s)} for s in range(1, mates)])
     out_gather = LineGather(rank, lambda s, p: wos.at[s, member], 1, z_ss, z_rs)
     gather = LineGather(rank, lambda s, p: xs.at[s, pl.ds(p * half_rows, half_rows)], 2, x_ss, x_rs)
-    grads = LineGather(rank, lambda s, p: dys.at[s, pl.ds(p * half_rows, half_rows)], 2, y_ss, y_rs)
+
+    def near(k, source):
+        return pltpu.make_async_remote_copy(
+            src_ref=dys.at[source], dst_ref=dys.at[source], send_sem=y_ss.at[k], recv_sem=y_rs.at[k],
+            device_id={"tensor": across(rank, k)}, device_id_type=MESH)
+
+    inner = inner_plane(rank)
     attended = LineGather(rank, lambda s, p: obs.at[s, :, pl.ds(pl.multiple_of(p * HD, HD), HD)], heads, o_ss, o_rs)
     first[0].wait()
     out_gather.start(0)
@@ -331,8 +337,8 @@
     first[2].wait()
     real = segs[pl.ds(pl.multiple_of(rank * rows, rows), rows), :1] >= 0.0
     dys[rank] = jnp.where(real, dys[rank], jnp.zeros((rows, model), BF))
-    grads.start(0)
-    grads.start(1)
+    near(1, rank).start()
+    pl.when(inner)(near(3, rank).start)
     keep = [local(dys.at[rank], cot_out, k_sem.at[0])]
     keep[0].start()
     for w in weights:
@@ -433,19 +439,23 @@
         lax.fori_loop(0, RANKS, block, 0)
 
     add(rank, first=True)
-    for piece in range(2):
-        grads.arrive(2, piece)
     for piece in range(heads):
         attended.arrive(2, piece)
     for piece in range(heads):
         attended.arrive(1, piece)
     add(across(rank, 2))
     add(across(rank, 1))
-    for piece in range(2):
-        grads.arrive(1, piece)
-        grads.arrive(3, piece)
-    more = [local(dys, dy_out, l_sem.at[0])]
+    one, three = across(rank, 1), across(rank, 3)
+    near(1, one).wait_recv()
+    more = [local(dys.at[one], dy_out.at[one], l_sem.at[0])]
     more[0].start()
+    inner_copy = local(dys.at[three], dy_out.at[three], l_sem.at[1])
+
+    @pl.when(inner)
+    def _():
+        near(3, three).wait_recv()
+        inner_copy.start()
+
     for piece in range(heads):
         attended.arrive(3, piece)
     gather.finish()
@@ -459,8 +469,14 @@
         mate_copy(step).wait_send()
     for step in range(mates):
         core_copy(step, parity).wait_send()
-    grads.finish()
     attended.finish()
+    near(1, rank).wait_send()
+
+    @pl.when(inner)
+    def _():
+        near(3, rank).wait_send()
+        inner_copy.wait()
+
     for c in keep + more:
         c.wait()
     for b in range(RANKS):
@@ -488,7 +504,7 @@
             pltpu.VMEM((RANKS, parts, width // parts, model), BF), pltpu.VMEM(shape, BF), pltpu.VMEM((RANKS, length, width), BF),
             pltpu.VMEM((heads, length, length), BF), pltpu.VMEM(shape, F32), pltpu.VMEM((length, HD), F32),
             *LineGather.sems(2), *LineGather.sems(1), DMA((mates,)), DMA((parts,)), DMA((mates,)),
-            *LineGather.sems(2), *LineGather.sems(heads), DMA((6,)), DMA((7,)), DMA((RANKS,)),
+            DMA((4,)), DMA((4,)), *LineGather.sems(heads), DMA((6,)), DMA((7,)), DMA((RANKS,)),
         ],
         compiler_params=pltpu.CompilerParams(collective_id=1, has_side_effects=True, vmem_limit_bytes=62 << 20),
         name="forward_gather",
@@ -510,19 +526,69 @@
 
 def mlp_body(a2, dy, wg, wu, wd, hid, cot, gran, gain,
              g_out, down_out, dh_out, gain_out,
-             lefts, acts, ws, parts, inbox, stage, downs, hs, cots, total, gains, r_ss, r_rs, l_sem, s_sem):
+             lefts, acts, ws, parts, inbox, stage, downs, hs, cots, total, gains, r_ss, r_rs, y_ss, y_rs, l_sem, s_sem):
     rank = lax.axis_index("tensor")
     rows, model = cot.shape
     width = wg.shape[1]
     per, share = stage.shape[1], stage.shape[2]
+    end = (rank == 0) | (rank == 3)
+
+    def part(source):
+        return pl.ds(pl.multiple_of(source * rows, rows), rows)
+
+    def dy_load(k, sem):
+        return local(dy.at[across(rank, k)], lefts.at[1, part(across(rank, k))], l_sem.at[sem])
+
+    inner = inner_plane(rank)
+    half = rows // 2
+
+    def piece_of(source, piece):
+        return pl.ds(pl.multiple_of(source * rows + piece * half, half), half)
+
+    def hand(slot, shard, piece, k, kept=True):
+        where = piece_of(across(rank, shard), piece)
+        source = dy.at[across(rank, shard), pl.ds(piece * half, half)] if kept else lefts.at[1, where]
+        return pltpu.make_async_remote_copy(
+            src_ref=source, dst_ref=lefts.at[1, where], send_sem=y_ss.at[slot, piece], recv_sem=y_rs.at[slot, piece],
+            device_id={"tensor": across(rank, k)}, device_id_type=MESH)
+
+    def mid(piece):
+        return hand(0, 1, piece, 3)
+
+    def second(piece):
+        return hand(1, 3, piece, 1)
+
+    def third(piece):
+        return hand(2, 2, piece, 1, False)
+
+    def arrived(slot, shard, piece):
+        where = piece_of(across(rank, shard), piece)
+        return pltpu.make_async_remote_copy(
+            src_ref=lefts.at[1, where], dst_ref=lefts.at[1, where], send_sem=y_ss.at[slot, piece], recv_sem=y_rs.at[slot, piece],
+            device_id={"tensor": across(rank, 1)}, device_id_type=MESH)
+
+    own = local(cot, lefts.at[1, part(rank)], l_sem.at[7])
+    own.start()
     loads = [local(wg, ws.at[0], l_sem.at[0]), local(a2, lefts.at[0], l_sem.at[1]), local(wu, ws.at[1], l_sem.at[2]),
-             local(dy, lefts.at[1], l_sem.at[3]), local(wd, ws.at[2], l_sem.at[4])]
+             dy_load(1, 3), local(wd, ws.at[2], l_sem.at[4])]
+    inner_load = dy_load(3, 8)
+    pl.when(inner)(inner_load.start)
     late = [local(hid, hs, l_sem.at[5]), local(cot, cots, l_sem.at[6])]
     for c in loads + late:
         c.start()
     greet(line_peers(rank))
+
+    @pl.when(inner)
+    def _():
+        mid(0).start()
+        second(0).start()
+        mid(1).start()
+        second(1).start()
+
     scatter = LineScatter(rank, parts, inbox, r_ss, r_rs, 2)
-    order = [across(rank, k) for k in (3, 2, 1, 0)]
+    planes = [rank] + [across(rank, k) for k in (1, 2, 3)]
+    kinds = [jnp.where(end, a, b) for a, b in zip((1, 2, 0, 3), (3, 1, 2, 0))]
+    order = [jnp.where(end, planes[a], planes[b]) for a, b in zip((1, 2, 0, 3), (3, 1, 2, 0))]
     limit = FF // 8 * lax.shift_left(1, gran[0] - 1) - rank * width
 
     def step(i, carry):
@@ -547,7 +613,19 @@
             @pl.when((i == 0) & (t == 0))
             def _():
                 loads[3].wait()
+                pl.when(inner)(inner_load.wait)
+                own.wait()
                 loads[4].wait()
+
+            @pl.when((i == 1) & (t == 0) & end)
+            def _():
+                for piece in range(2):
+                    arrived(1, 2, piece).wait_recv()
+
+            @pl.when((i == 3) & (t == 0) & end)
+            def _():
+                for piece in range(2):
+                    arrived(2, 3, piece).wait_recv()
 
             dz = dot(lefts[1, where, :], ws[2, cols, :], ((1,), (1,)))
             unit = lax.broadcasted_iota(jnp.int32, gate.shape, 1) + t * FT
@@ -563,20 +641,28 @@
 
         def back(t, inner_carry):
             cols = pl.ds(pl.multiple_of(t * FT, FT), FT)
-            parts[3 - i, :, cols] = (
+            parts[pick(i, kinds), :, cols] = (
                 dot(acts[0, where, :], ws[0, cols, :], ((1,), (1,))) + dot(acts[1, where, :], ws[1, cols, :], ((1,), (1,)))
             ).astype(BF)
             return inner_carry
 
         lax.fori_loop(0, model // FT, back, 0)
-        pl.when(i == 0)(scatter.send_far)
-        pl.when(i == 1)(scatter.send_two_end)
-
-        @pl.when(i == 2)
+
+        @pl.when(inner & (i == 0))
         def _():
+            scatter.send_far()
+            arrived(0, 2, 0).wait_recv()
+            third(0).start()
+
+        @pl.when(inner & (i == 1))
+        def _():
+            arrived(0, 2, 1).wait_recv()
+            third(1).start()
             scatter.send_near()
-            scatter.send_two_inner()
-
+
+        pl.when(end & (i == 0))(scatter.send_near)
+        pl.when(end & (i == 1))(scatter.send_two_end)
+        pl.when(end & (i == 3))(scatter.send_far)
         return carry
 
     lax.fori_loop(0, 4, step, 0)
@@ -599,11 +685,13 @@
         put(i, slot).start()
         return carry
 
-    lax.fori_loop(0, 3 * blocks, grads, 0)
+    lax.fori_loop(0, 3 * blocks - 3, grads, 0)
+    scatter.send_two_inner()
+    lax.fori_loop(3 * blocks - 3, 3 * blocks, grads, 0)
 
     def down(i, carry):
         where = pl.ds(pl.multiple_of(pick(i, order) * rows, rows), rows)
-        downs[3 - i] = dot(acts[2, where, :], ws[2]).astype(BF)
+        downs[pick(i, kinds)] = dot(acts[2, where, :], ws[2]).astype(BF)
         return carry
 
     lax.fori_loop(0, 4, down, 0)
@@ -621,6 +709,14 @@
     for c in last:
         c.start()
     scatter.finish()
+
+    @pl.when(inner)
+    def _():
+        for piece in range(2):
+            mid(piece).wait_send()
+            second(piece).wait_send()
+            third(piece).wait_send()
+
     put(3 * blocks - 2, 0).wait()
     put(3 * blocks - 1, 1).wait()
     for c in last + [keep]:
@@ -642,11 +738,11 @@
             pltpu.VMEM((2, RANKS * rows, model), BF), pltpu.VMEM((3, RANKS * rows, width), BF), pltpu.VMEM((3, model, width), BF),
             pltpu.VMEM(shard, BF), pltpu.VMEM(shard, BF), pltpu.VMEM((2, WB // share, share, width), BF), pltpu.VMEM(shard, BF),
             pltpu.VMEM((rows, model), F32), pltpu.VMEM((rows, model), BF), pltpu.VMEM((rows, model), F32), pltpu.VMEM((1, model), F32),
-            *LineScatter.sems(2), DMA((7,)), DMA((2,)),
+            *LineScatter.sems(2), DMA((3, 2)), DMA((3, 2)), DMA((9,)), DMA((2,)),
         ],
         compiler_params=pltpu.CompilerParams(collective_id=3, has_side_effects=True, vmem_limit_bytes=63 << 20),
         name="mlp_scatter",
-    )(a2.reshape(-1, model), dy.reshape(-1, model), w_gate, w_up, w_down, hidden_own, cot_own, granularity, gain)
+    )(a2.reshape(-1, model), dy, w_gate, w_up, w_down, hidden_own, cot_own, granularity, gain)
 
 
 def attention_back_body(dp, dh, wo_all, downs, grads, q, k, v, p_all, hid, cosine, sine,

time: 393 us -> 367 us (0.934)
  Pallas kernels: 391 us -> 365 us
    pallas_call x1, Pallas kernels: 175 us -> 141 us  [forward_kernel(): pl.pallas_call(functools.partial(forward_body, dp), in_specs=[ANY, ANY, V...]
    pallas_call x1, Pallas kernels: 68.1 us -> 77.4 us  [mlp_kernel(): pl.pallas_call(mlp_body, in_specs=[ANY] * 7 + [pl.BlockSpec(memory_space=...]
where the time goes in v6:
time: 367 us; the launch traced here: 366 us
  Pallas kernels  365 us (99%)
    pallas_call x1, Pallas kernels, forward_kernel(): pl.pallas_call(functools.partial(forward_body, dp), in_specs=[ANY, ANY, V...  141 us
    pallas_call x1, Pallas kernels, mlp_kernel(): pl.pallas_call(mlp_body, in_specs=[ANY] * 7 + [pl.BlockSpec(memory_space=...  77.4 us
    pallas_call x1, Pallas kernels, attention_back_kernel(): pl.pallas_call(functools.partial(attention_back_body, dp), in_specs=[ANY]...  74.2 us
    pallas_call x1, Pallas kernels, input_back_kernel(): pl.pallas_call(functools.partial(input_back_body, dp), in_specs=[ANY] * 1...  67.7 us

profile of v6, /device:TPU:0, one launch (start us, length us, event | category | flops | bytes accessed | tf_op | source)
XLA Modules:
  0.0 366.3 jit_solution(9528690655349261034)
XLA Ops:
  1.3 141.3 %forward_gather.1 = (bf16[4,256,1536]{2,1,0:T(8,128)(2,1)}, bf16[1024,384]{1,0:T(8,128)(2,1)}, bf16[1024,384]{1,0:T(8,128)(2,1)}, bf16[1024,384]{1,0:T(8,128)(2,...) custom-call(bf16[256,1536]{1,0:T(8,128)(2,1)} %tok.3, ...), custom_call_target="tpu_custom_call" | custom-call | tf_op jit(solution)/shard_map/forward_gather/pallas_call | solution.py:495
  142.6 77.4 %mlp_scatter.1 = (bf16[3,8,192,1536]{3,2,1,0:T(8,128)(2,1)}, bf16[4,256,1536]{2,1,0:T(8,128)(2,1)}, f32[256,1536]{1,0:T(8,128)}, f32[1,1536]{1,0:T(1,128)}) custom-call(bf16[1024,1536]{1,0:T(8,128)(2,1)} %bitcast.9, bf16[4,256,1536]{2,1,0:T(8,128)(2,1)} %get-tuple-element.47.dy, bf16[1536,1536]{1,0:T(8,128)(2,1)} %wg.1, bf16[1536,1536]{1,0:T(8,128)(2,1)} %wu.1, ...), custom_call_target="tpu_custom_call" | custom-call | tf_op jit(solution)/shard_map/mlp_scatter/pallas_call | solution.py:731
  220.1 74.2 %attention_back.1 = (bf16[256,1536]{1,0:T(8,128)(2,1)}, bf16[1024,384]{1,0:T(8,128)(2,1)}, bf16[1024,384]{1,0:T(8,128)(2,1)}, bf16[1024,384]{1,0:T(8,128)(2,1)}, bf16[3,192,1536]{2,1,0:T(8,128)(2,1)}) custom-call(f32[256,1536]{1,0:T(8,128)} %get-tuple-element.50.dh, bf16[4,384,1536]{2,1,0:T(8,128)(2,1)} %bitcast.8, ...), custom_call_target="tpu_custom_call" | custom-call | tf_op jit(solution)/shard_map/attention_back/pallas_call | solution.py:873
  294.3 67.7 %input_back.1 = (bf16[256,1536]{1,0:T(8,128)(2,1)}, f32[2,1536]{1,0:T(2,128)}, f32[192,1152]{1,0:T(8,128)}, f32[192,384]{1,0:T(8,128)}) custom-call(bf16[1024,384]{1,0:T(8,128)(2,1)} %get-tuple-element.59.dq, bf16[1024,384]{1,0:T(8,128)(2,1)} %get-tuple-element.60.dk, bf16[1024,384]{1,0:T(8,128)(2,1)} %get-tuple-element.61.dv, bf16[1024,1536]{1,0:T(8,128)(2,1)} %bitcast.10, ...), custom_call_target="tpu_custom_call" | custom-call | tf_op jit(solution)/shard_map/input_back/pallas_call | solution.py:1042
  362.0 4.1 %finish.1 = (bf16[256,1536]{1,0:T(8,128)(2,1)}, bf16[256,1536]{1,0:T(8,128)(2,1)}, f32[1536]{0:T(1024)}, f32[1536]{0:T(1024)}, f32[192,384]{1,0:T(8,128)}, /*ind...) custom-call(bf16[256,1536]{1,0:T(8,128)(2,1)} %get-tuple-element.58., ...), custom_call_target="tpu_custom_call" | custom-call | tf_op jit(solution)/shard_map/finish/pallas_call | solution.py:1113

commit v7 on v6

--- a/solution.py
+++ b/solution.py
@@ -146,17 +146,17 @@
             for piece in range(self.pieces):
                 self.copy(2, 2, 2, piece).start()
 
-    def send_two_inner(self):
+    def send_two_inner(self, pieces=None):
         @pl.when(self.inner)
         def _():
-            for piece in range(self.pieces):
+            for piece in pieces or range(self.pieces):
                 where = self.where(piece)
                 self.copy(3, 0, 1, piece).wait_recv()
                 self.parts[2, where] = (self.parts[2, where].astype(F32) + self.inbox[0, where].astype(F32)).astype(BF)
                 self.copy(2, 2, 2, piece).start()
 
-    def send_near(self):
-        for piece in range(self.pieces):
+    def send_near(self, pieces=None):
+        for piece in pieces or range(self.pieces):
             self.copy(1, 1, 1, piece).start()
 
     def total(self, target):
@@ -585,7 +585,7 @@
         mid(1).start()
         second(1).start()
 
-    scatter = LineScatter(rank, parts, inbox, r_ss, r_rs, 2)
+    scatter = LineScatter(rank, parts, inbox, r_ss, r_rs, 4)
     planes = [rank] + [across(rank, k) for k in (1, 2, 3)]
     kinds = [jnp.where(end, a, b) for a, b in zip((1, 2, 0, 3), (3, 1, 2, 0))]
     order = [jnp.where(end, planes[a], planes[b]) for a, b in zip((1, 2, 0, 3), (3, 1, 2, 0))]
@@ -663,6 +663,11 @@
         pl.when(end & (i == 0))(scatter.send_near)
         pl.when(end & (i == 1))(scatter.send_two_end)
         pl.when(end & (i == 3))(scatter.send_far)
+
+        @pl.when((end & (i == 0)) | (inner & (i == 1)))
+        def _():
+            downs[1] = dot(acts[2, where, :], ws[2]).astype(BF)
+
         return carry
 
     lax.fori_loop(0, 4, step, 0)
@@ -683,18 +688,19 @@
         for p in range(per):
             stage[slot, p] = low[p * share : (p + 1) * share]
         put(i, slot).start()
+        for piece in range(4):
+            pl.when(i == 3 * blocks - 7 + 2 * piece)(lambda: scatter.send_two_inner([piece]))
         return carry
 
-    lax.fori_loop(0, 3 * blocks - 3, grads, 0)
-    scatter.send_two_inner()
-    lax.fori_loop(3 * blocks - 3, 3 * blocks, grads, 0)
+    lax.fori_loop(0, 3 * blocks, grads, 0)
 
     def down(i, carry):
-        where = pl.ds(pl.multiple_of(pick(i, order) * rows, rows), rows)
-        downs[pick(i, kinds)] = dot(acts[2, where, :], ws[2]).astype(BF)
+        kind = jnp.where(i == 2, 0, i + 2)
+        where = part(pick(i, [planes[2], planes[3], rank]))
+        downs[kind] = dot(acts[2, where, :], ws[2]).astype(BF)
         return carry
 
-    lax.fori_loop(0, 4, down, 0)
+    lax.fori_loop(0, 3, down, 0)
     keep = local(downs, down_out, l_sem.at[0])
     keep.start()
     for c in late:
@@ -738,16 +744,16 @@
             pltpu.VMEM((2, RANKS * rows, model), BF), pltpu.VMEM((3, RANKS * rows, width), BF), pltpu.VMEM((3, model, width), BF),
             pltpu.VMEM(shard, BF), pltpu.VMEM(shard, BF), pltpu.VMEM((2, WB // share, share, width), BF), pltpu.VMEM(shard, BF),
             pltpu.VMEM((rows, model), F32), pltpu.VMEM((rows, model), BF), pltpu.VMEM((rows, model), F32), pltpu.VMEM((1, model), F32),
-            *LineScatter.sems(2), DMA((3, 2)), DMA((3, 2)), DMA((9,)), DMA((2,)),
+            *LineScatter.sems(4), DMA((3, 2)), DMA((3, 2)), DMA((9,)), DMA((2,)),
         ],
         compiler_params=pltpu.CompilerParams(collective_id=3, has_side_effects=True, vmem_limit_bytes=63 << 20),
         name="mlp_scatter",
     )(a2.reshape(-1, model), dy, w_gate, w_up, w_down, hidden_own, cot_own, granularity, gain)
 
 
-def attention_back_body(dp, dh, wo_all, downs, grads, q, k, v, p_all, hid, cosine, sine,
-                        out_out, dq_out, dk_out, dv_out, gf_out,
-                        dhs, low, wos, parts, inbox, dobs, dos, qkv, ps, ds, dqkv, hs, outs, kept, finals, *rest):
+def attention_back_body(dp, dh, wo_all, downs, grads, q, k, v, p_all, hid, wq, wk, wv, cosine, sine,
+                        out_out, dq_out, dk_out, dv_out, gf_out, da_out,
+                        dhs, low, wos, parts, inbox, dobs, dos, qkv, ps, ds, dqkv, hs, outs, kept, finals, ws, shares, *rest):
     rank, group = lax.axis_index("tensor"), lax.axis_index("dp")
     rounds = 2 * (dp.bit_length() - 1)
     first, boxes, rest = rest[0], rest[1 : rounds - 1], rest[rounds - 1 :]
@@ -760,6 +766,7 @@
     loads = [local(downs, parts, l_sem.at[2]), local(dh, dhs, l_sem.at[0]), local(wo_all, wos, l_sem.at[1])]
     owns = [local(grads.at[w, :, parity], kept.at[w], f_sem.at[w]) for w in range(count)]
     late = [local(t, qkv.at[i], l_sem.at[3 + i]) for i, t in enumerate((q, k, v))] + [local(hid, hs, l_sem.at[6])]
+    late += [local(t, ws.at[i], l_sem.at[7 + i]) for i, t in enumerate((wq, wk, wv))]
     for c in loads + owns + late:
         c.start()
 
@@ -803,6 +810,7 @@
     lax.fori_loop(0, count, fold, 0)
     for c in late:
         c.wait()
+    scatter.send_two_inner([0])
     for k in (3, 2, 1):
         exchange(k, across(rank, k)).wait_recv()
 
@@ -829,14 +837,26 @@
             dqkv[1, where, cols] = unrope(dot(ds[start:, where], qkv[0, start:, cols], ((0,), (0,))), start)
             dqkv[2, where, cols] = dot(ps[slot, start:, where], dos[start:, cols], ((0,), (0,))).astype(BF)
         pl.when(h + 2 < heads)(lambda: probs(h + 2).start())
+        pl.when(h == 0)(lambda: scatter.send_two_inner([1]))
         return carry
 
     lax.fori_loop(0, heads, head, 0)
     done = [local(dqkv.at[i], t, l_sem.at[i]) for i, t in enumerate((dq_out, dk_out, dv_out))]
     for c in done:
         c.start()
+
+    def share_of(k, carry):
+        where = pl.ds(pl.multiple_of(pick(k, [rank] + [across(rank, i) for i in (1, 2, 3)]) * rows, rows), rows)
+        value = dot(dqkv[0, where, :], ws[0], ((1,), (1,)))
+        for s in (1, 2):
+            value += dot(dqkv[s, where, :], ws[s], ((1,), (1,)))
+        shares[k] = value.astype(BF)
+        return carry
+
     reduce.add(1, 0)
-    scatter.send_two_inner()
+    lax.fori_loop(0, RANKS, share_of, 0)
+    done.append(local(shares, da_out, l_sem.at[4]))
+    done[-1].start()
     reduce.add(1, 1)
     reduce.add(1, 2)
     for t in range(2, reduce.bits - 1):
@@ -863,7 +883,7 @@
         c.wait()
 
 
-def attention_back_kernel(dp, grad_hidden, w_out_all, down_parts, grads_ff, query, key, value, probs_low, hidden_own, cosine, sine):
+def attention_back_kernel(dp, grad_hidden, w_out_all, down_parts, grads_ff, query, key, value, probs_low, hidden_own, w_query, w_key, w_value, cosine, sine):
     rows, model = grad_hidden.shape
     length, width = query.shape
     count, _, share, columns = grads_ff.shape
@@ -872,27 +892,29 @@
     heads = jax.ShapeDtypeStruct((length, width), BF)
     return pl.pallas_call(
         functools.partial(attention_back_body, dp),
-        in_specs=[ANY] * 9 + [VM, VM],
-        out_specs=[ANY] * 5,
-        out_shape=[jax.ShapeDtypeStruct((rows, model), BF), heads, heads, heads, jax.ShapeDtypeStruct((count, share, columns), BF)],
+        in_specs=[ANY] * 12 + [VM, VM],
+        out_specs=[ANY] * 6,
+        out_shape=[jax.ShapeDtypeStruct((rows, model), BF), heads, heads, heads, jax.ShapeDtypeStruct((count, share, columns), BF),
+                   jax.ShapeDtypeStruct(shard, BF)],
         scratch_shapes=[
             pltpu.VMEM((rows, model), F32), pltpu.VMEM((rows, model), BF), pltpu.VMEM((RANKS, width, model), BF),
             pltpu.VMEM(shard, BF), pltpu.VMEM(shard, BF), pltpu.VMEM((3, rows, width), BF), pltpu.VMEM((length, width), BF),
             pltpu.VMEM((3, length, width), BF), pltpu.VMEM((2, length, length), BF), pltpu.VMEM((length, length), BF),
             pltpu.VMEM((3, length, width), BF), pltpu.VMEM((rows, model), F32), pltpu.VMEM((rows, model), BF),
             pltpu.VMEM((count, mates, share, columns), BF), pltpu.VMEM((count, share, columns), BF),
+            pltpu.VMEM((3, model, width), BF), pltpu.VMEM(shard, BF),
             *GroupReduce.box_shapes(dp, count, share, columns, columns // 2), *GroupReduce.sem_shapes(dp, count),
-            *LineScatter.sems(2), DMA((4,)), DMA((RANKS,)), DMA((7,)), DMA((2,)), DMA((count,)),
+            *LineScatter.sems(2), DMA((4,)), DMA((RANKS,)), DMA((10,)), DMA((2,)), DMA((count,)),
         ],
         compiler_params=pltpu.CompilerParams(collective_id=4, has_side_effects=True, vmem_limit_bytes=63 << 20),
         name="attention_back",
     )(grad_hidden, w_out_all, down_parts, grads_ff.reshape(count, mates, 2, share, columns),
-      query, key, value, probs_low, hidden_own, cosine, sine)
-
-
-def input_back_body(dp, dq, dk, dv, a1, wq, wk, wv, tok, dh, ob, gain, gain2,
+      query, key, value, probs_low, hidden_own, w_query, w_key, w_value, cosine, sine)
+
+
+def input_back_body(dp, dq, dk, dv, a1, da, tok, dh, ob, gain, gain2,
                     dx_out, gains_out, gqkv_out, gout_out,
-                    dqkv, a1s, ws, xs, dhs, low, obs, parts, inbox, g1, g2, f1, f2, f2_low, box2, f3, gbuf, gbox, total, dxs, *rest):
+                    dqkv, a1s, xs, dhs, low, obs, parts, inbox, g1, g2, f1, f2, f2_low, box2, f3, gbuf, gbox, total, dxs, *rest):
     rank, group = lax.axis_index("tensor"), lax.axis_index("dp")
     bits = dp.bit_length() - 1
     boxes = [rest[: 2 * bits - 1], rest[2 * bits - 1 : 4 * bits - 2]]
@@ -904,39 +926,30 @@
     share = g1.shape[1]
     per = WB // share
     parity = lax.rem(group, 2)
-    loads = [local(t, dqkv.at[i], l_sem.at[i]) for i, t in enumerate((dq, dk, dv))]
-    loads += [local(t, ws.at[i], l_sem.at[3 + i]) for i, t in enumerate((wq, wk, wv))]
+    loads = [local(da, parts, l_sem.at[3])]
     late = [local(a1, a1s, l_sem.at[8]), local(dh, dhs, l_sem.at[6]), local(ob, obs, l_sem.at[7]), local(tok, xs, l_sem.at[9])]
+    late += [local(t, dqkv.at[i], l_sem.at[i]) for i, t in enumerate((dq, dk, dv))]
     for c in loads + late:
         c.start()
     scatter = LineScatter(rank, parts, inbox, r_ss, r_rs, 2)
     mixed = GroupReduce(group, dp, lambda w, d: g1.at[d], lambda w, j: g1.at[2 * j + parity], boxes[0][0], boxes[0][1:], f1.shape[1] // 256 * 128, sems[0])
     output = GroupReduce(group, dp, lambda w, d: g2.at[d], lambda w, j: g2.at[2 * j + parity], boxes[1][0], boxes[1][1:], f2.shape[1] // 256 * 128, sems[1])
     greet(line_peers(rank) + mixed.peers())
-    order = [across(rank, k) for k in (3, 2, 1, 0)]
     for c in loads:
         c.wait()
-
-    def step(i, carry):
-        where = pl.ds(pl.multiple_of(pick(i, order) * rows, rows), rows)
-        value = dot(dqkv[0, where, :], ws[0], ((1,), (1,)))
-        for s in (1, 2):
-            value += dot(dqkv[s, where, :], ws[s], ((1,), (1,)))
-        parts[3 - i] = value.astype(BF)
-        pl.when(i == 0)(scatter.send_far)
-        pl.when(i == 1)(scatter.send_two_end)
-        pl.when(i == 2)(scatter.send_near)
-
-        @pl.when(i == 0)
-        def _():
-            late[0].wait()
-
-        row = jnp.sum(value * a1s[where, :].astype(F32), axis=0, keepdims=True)
-        gbuf[0, 0:1, :] = jnp.where(i == 0, row, gbuf[0, 0:1, :] + row)
+    scatter.send_far()
+    scatter.send_two_end()
+    scatter.send_near()
+    late[0].wait()
+
+    def gain_rows(k, carry):
+        where = pl.ds(pl.multiple_of(pick(k, [rank] + [across(rank, i) for i in (1, 2, 3)]) * rows, rows), rows)
+        row = jnp.sum(parts[k].astype(F32) * a1s[where, :].astype(F32), axis=0, keepdims=True)
+        gbuf[0, 0:1, :] = jnp.where(k == 0, row, gbuf[0, 0:1, :] + row)
         return carry
 
     gbuf[0, 0:1, :] = jnp.zeros((1, model), F32)
-    lax.fori_loop(0, 4, step, 0)
+    lax.fori_loop(0, RANKS, gain_rows, 0)
     gbuf[0, 0:1, :] = gbuf[0, 0:1, :] / gain[...].reshape(1, model)
     gbuf[0, 1:2, :] = gain2[...]
 
@@ -1031,7 +1044,7 @@
         c.wait()
 
 
-def input_back_kernel(dp, grad_q, grad_k, grad_v, a1_all, w_query, w_key, w_value, tokens, grad_hidden, attended_own, gain, gain_two):
+def input_back_kernel(dp, grad_q, grad_k, grad_v, a1_all, grad_one, tokens, grad_hidden, attended_own, gain, gain_two):
     rows, model = tokens.shape
     length, width = grad_q.shape
     share = model // dp
@@ -1041,12 +1054,12 @@
     splits = [w // 256 * 128 for w in wide]
     return pl.pallas_call(
         functools.partial(input_back_body, dp),
-        in_specs=[ANY] * 10 + [VM, VM],
+        in_specs=[ANY] * 8 + [VM, VM],
         out_specs=[ANY] * 4,
         out_shape=[jax.ShapeDtypeStruct((rows, model), BF), jax.ShapeDtypeStruct((2, model), F32),
                    jax.ShapeDtypeStruct((share, wide[0]), F32), jax.ShapeDtypeStruct((share, width), F32)],
         scratch_shapes=[
-            pltpu.VMEM((3, length, width), BF), pltpu.VMEM((length, model), BF), pltpu.VMEM((3, model, width), BF),
+            pltpu.VMEM((3, length, width), BF), pltpu.VMEM((length, model), BF),
             pltpu.VMEM((rows, model), BF), pltpu.VMEM((rows, model), F32), pltpu.VMEM((rows, model), BF), pltpu.VMEM((RANKS, rows, width), BF),
             pltpu.VMEM(shard, BF), pltpu.VMEM(shard, BF),
             pltpu.VMEM((dp, share, wide[0]), BF), pltpu.VMEM((dp, share, wide[1]), BF),
@@ -1060,7 +1073,7 @@
         ],
         compiler_params=pltpu.CompilerParams(collective_id=5, has_side_effects=True, vmem_limit_bytes=63 << 20),
         name="input_back",
-    )(grad_q, grad_k, grad_v, a1_all.reshape(length, model), w_query, w_key, w_value, tokens, grad_hidden, attended_own, gain, gain_two)
+    )(grad_q, grad_k, grad_v, a1_all.reshape(length, model), grad_one, tokens, grad_hidden, attended_own, gain, gain_two)
 
 
 def finish_body(output, dx, gains, mixed, out_t, ff,
@@ -1136,11 +1149,11 @@
     grads_ff, down_parts, grad_hidden, gain_two = mlp_kernel(
         dp, rows_two, grad_rows, w_gate, w_up, w_down, hidden_own, cot_own, granularity, norm2_gain
     )
-    output, grad_q, grad_k, grad_v, own_ff = attention_back_kernel(
-        dp, grad_hidden, w_out_all, down_parts, grads_ff, query_rot, key_rot, value_low, probs_low, hidden_own, cosine, sine
+    output, grad_q, grad_k, grad_v, own_ff, grad_one = attention_back_kernel(
+        dp, grad_hidden, w_out_all, down_parts, grads_ff, query_rot, key_rot, value_low, probs_low, hidden_own, w_query, w_key, w_value, cosine, sine
     )
     grad_tokens, gains, own_qkv, own_out = input_back_kernel(
-        dp, grad_q, grad_k, grad_v, a1_all, w_query, w_key, w_value, tokens, grad_hidden, attended_own, norm1_gain, gain_two
+        dp, grad_q, grad_k, grad_v, a1_all, grad_one, tokens, grad_hidden, attended_own, norm1_gain, gain_two
     )
     outs = finish_kernel(output, grad_tokens, gains, own_qkv, own_out, own_ff)
     return tuple(o.T if i in (7, 10) else o for i, o in enumerate(outs))

time: 367 us -> 362 us (0.986)
  Pallas kernels: 365 us -> 360 us
where the time goes in v7:
time: 362 us
  Pallas kernels  360 us (99%)
    pallas_call x1, Pallas kernels, forward_kernel(): pl.pallas_call(functools.partial(forward_body, dp), in_specs=[ANY, ANY, V...  141 us
    pallas_call x1, Pallas kernels, mlp_kernel(): pl.pallas_call(mlp_body, in_specs=[ANY] * 7 + [pl.BlockSpec(memory_space=...  76 us
    pallas_call x1, Pallas kernels, attention_back_kernel(): pl.pallas_call(functools.partial(attention_back_body, dp), in_specs=[ANY]...  72.3 us
    pallas_call x1, Pallas kernels, input_back_kernel(): pl.pallas_call(functools.partial(input_back_body, dp), in_specs=[ANY] * 8...  66.3 us

profile of v7, /device:TPU:0, one launch (start us, length us, event | category | flops | bytes accessed | tf_op | source)
XLA Modules:
  0.0 361.7 jit_solution(6491592339499788764)
XLA Ops:
  1.3 141.4 %forward_gather.1 = (bf16[4,256,1536]{2,1,0:T(8,128)(2,1)}, bf16[1024,384]{1,0:T(8,128)(2,1)}, bf16[1024,384]{1,0:T(8,128)(2,1)}, bf16[1024,384]{1,0:T(8,128)(2,...) custom-call(bf16[256,1536]{1,0:T(8,128)(2,1)} %tok.3, ...), custom_call_target="tpu_custom_call" | custom-call | tf_op jit(solution)/shard_map/forward_gather/pallas_call | solution.py:495
  142.7 76.0 %mlp_scatter.1 = (bf16[3,8,192,1536]{3,2,1,0:T(8,128)(2,1)}, bf16[4,256,1536]{2,1,0:T(8,128)(2,1)}, f32[256,1536]{1,0:T(8,128)}, f32[1,1536]{1,0:T(1,128)}) custom-call(bf16[1024,1536]{1,0:T(8,128)(2,1)} %bitcast.9, bf16[4,256,1536]{2,1,0:T(8,128)(2,1)} %get-tuple-element.48.dy, bf16[1536,1536]{1,0:T(8,128)(2,1)} %wg.1, bf16[1536,1536]{1,0:T(8,128)(2,1)} %wu.1, ...), custom_call_target="tpu_custom_call" | custom-call | tf_op jit(solution)/shard_map/mlp_scatter/pallas_call | solution.py:737
  218.7 72.3 %attention_back.1 = (bf16[256,1536]{1,0:T(8,128)(2,1)}, bf16[1024,384]{1,0:T(8,128)(2,1)}, bf16[1024,384]{1,0:T(8,128)(2,1)}, bf16[1024,384]{1,0:T(8,128)(2,1)},...) custom-call(f32[256,1536]{1,0:T(8,128)} %get-tuple-element.51.dh, bf16[4,384,1536]{2,1,0:T(8,128)(2,1)} %bitcast.8, ...), custom_call_target="tpu_custom_call" | custom-call | tf_op jit(solution)/shard_map/attention_back/pallas_call | solution.py:893
  291.1 66.3 %input_back.1 = (bf16[256,1536]{1,0:T(8,128)(2,1)}, f32[2,1536]{1,0:T(2,128)}, f32[192,1152]{1,0:T(8,128)}, f32[192,384]{1,0:T(8,128)}) custom-call(bf16[1024,384]{1,0:T(8,128)(2,1)} %get-tuple-element.60.dq, bf16[1024,384]{1,0:T(8,128)(2,1)} %get-tuple-element.61.dk, bf16[1024,384]{1,0:T(8,128)(2,1)} %get-tuple-element.62.dv, bf16[1024,1536]{1,0:T(8,128)(2,1)} %bitcast.10, ...), custom_call_target="tpu_custom_call" | custom-call | tf_op jit(solution)/shard_map/input_back/pallas_call | solution.py:1055
  357.4 4.1 %finish.1 = (bf16[256,1536]{1,0:T(8,128)(2,1)}, bf16[256,1536]{1,0:T(8,128)(2,1)}, f32[1536]{0:T(1024)}, f32[1536]{0:T(1024)}, f32[192,384]{1,0:T(8,128)}, /*ind...) custom-call(bf16[256,1536]{1,0:T(8,128)(2,1)} %get-tuple-element.59., ...), custom_call_target="tpu_custom_call" | custom-call | tf_op jit(solution)/shard_map/finish/pallas_call | solution.py:1126

commit v8 on v7

--- a/solution.py
+++ b/solution.py
@@ -159,19 +159,20 @@
         for piece in pieces or range(self.pieces):
             self.copy(1, 1, 1, piece).start()
 
-    def total(self, target):
+    def total(self, target, then=None):
         for piece in range(self.pieces):
             where = self.where(piece)
             self.copy(1, 1, 1, piece).wait_recv()
             self.copy(2, 2, 2, piece).wait_recv()
             target[where] = (self.parts[0, where].astype(F32) + self.inbox[1, where].astype(F32)) + self.inbox[2, where].astype(F32)
 
-        @pl.when(self.inner)
-        def _():
-            for piece in range(self.pieces):
-                where = self.where(piece)
+            @pl.when(self.inner)
+            def _():
                 self.copy(3, 3, 3, piece).wait_recv()
                 target[where] += self.inbox[3, where].astype(F32)
+
+            if then is not None:
+                then(piece, where)
 
     def finish(self):
         for piece in range(self.pieces):
@@ -317,7 +318,6 @@
     weights = [local(w, ws.at[i], l_sem.at[3 + i]) for i, w in enumerate((wq, wk, wv))]
     for c in first + weights:
         c.start()
-    column_of(seg[...], segs)
     greet(line_peers(rank) + [{"dp": partner}] + [{"dp": base + mate(s)} for s in range(1, mates)])
     out_gather = LineGather(rank, lambda s, p: wos.at[s, member], 1, z_ss, z_rs)
     gather = LineGather(rank, lambda s, p: xs.at[s, pl.ds(p * half_rows, half_rows)], 2, x_ss, x_rs)
@@ -335,6 +335,7 @@
     gather.start(0)
     gather.start(1)
     first[2].wait()
+    column_of(seg[...], segs)
     real = segs[pl.ds(pl.multiple_of(rank * rows, rows), rows), :1] >= 0.0
     dys[rank] = jnp.where(real, dys[rank], jnp.zeros((rows, model), BF))
     near(1, rank).start()
@@ -430,7 +431,13 @@
             weight = wos[source].reshape(width, model)
             part = dot(obs[source, pl.ds(pl.multiple_of(b * rows, rows), rows), :], weight)
             total = part + (xs[b].astype(F32) if first else hs[b])
-            hs[b] = total
+            if last:
+                @pl.when(b == rank)
+                def _():
+                    hs[b] = total
+
+            else:
+                hs[b] = total
             if last:
                 xs[b] = (total * norm_factor(total) * gain2[...].reshape(1, model)).astype(BF)
                 local(xs.at[b], a2_out.at[b], b_sem.at[b]).start()
@@ -526,7 +533,7 @@
 
 def mlp_body(a2, dy, wg, wu, wd, hid, cot, gran, gain,
              g_out, down_out, dh_out, gain_out,
-             lefts, acts, ws, parts, inbox, stage, downs, hs, cots, total, gains, r_ss, r_rs, y_ss, y_rs, l_sem, s_sem):
+             lefts, acts, ws, parts, inbox, stage, downs, hs, cots, total, gains, r_ss, r_rs, y_ss, y_rs, l_sem, s_sem, d_sem):
     rank = lax.axis_index("tensor")
     rows, model = cot.shape
     width = wg.shape[1]
@@ -705,13 +712,20 @@
     keep.start()
     for c in late:
         c.wait()
-    scatter.total(total)
-    values, gradient = hs[...], total[...]
-    factor = norm_factor(values)
-    back_rows, gain_rows = norm_back(values, factor, gain[...].reshape(1, model), gradient)
-    total[...] = cots[...].astype(F32) + back_rows
-    gains[...] = gain_rows.reshape(1, model)
-    last = [local(total, dh_out, l_sem.at[1]), local(gains, gain_out, l_sem.at[2])]
+
+    def dh_copy(piece, where):
+        return local(total.at[where], dh_out.at[where], d_sem.at[piece])
+
+    def finish_rows(piece, where):
+        values, gradient = hs[where], total[where]
+        back_rows, row = norm_back(values, norm_factor(values), gain[...].reshape(1, model), gradient)
+        total[where] = cots[where].astype(F32) + back_rows
+        row = row.reshape(1, model)
+        gains[...] = row if piece == 0 else gains[...] + row
+        dh_copy(piece, where).start()
+
+    scatter.total(total, finish_rows)
+    last = [local(gains, gain_out, l_sem.at[2])]
     for c in last:
         c.start()
     scatter.finish()
@@ -727,6 +741,8 @@
     put(3 * blocks - 1, 1).wait()
     for c in last + [keep]:
         c.wait()
+    for piece in range(4):
+        dh_copy(piece, scatter.where(piece)).wait()
 
 
 def mlp_kernel(dp, a2, dy, w_gate, w_up, w_down, hidden_own, cot_own, granularity, gain):
@@ -744,7 +760,7 @@
             pltpu.VMEM((2, RANKS * rows, model), BF), pltpu.VMEM((3, RANKS * rows, width), BF), pltpu.VMEM((3, model, width), BF),
             pltpu.VMEM(shard, BF), pltpu.VMEM(shard, BF), pltpu.VMEM((2, WB // share, share, width), BF), pltpu.VMEM(shard, BF),
             pltpu.VMEM((rows, model), F32), pltpu.VMEM((rows, model), BF), pltpu.VMEM((rows, model), F32), pltpu.VMEM((1, model), F32),
-            *LineScatter.sems(4), DMA((3, 2)), DMA((3, 2)), DMA((9,)), DMA((2,)),
+            *LineScatter.sems(4), DMA((3, 2)), DMA((3, 2)), DMA((9,)), DMA((2,)), DMA((4,)),
         ],
         compiler_params=pltpu.CompilerParams(collective_id=3, has_side_effects=True, vmem_limit_bytes=63 << 20),
         name="mlp_scatter",
@@ -869,8 +885,11 @@
     for w in range(count):
         reduce.add(reduce.bits - 1, w, finals.at[w])
         put(w).start()
-    scatter.total(dhs)
-    outs[...] = (hs[...] + dhs[...]).astype(BF)
+
+    def out_rows(piece, where):
+        outs[where] = (hs[where] + dhs[where]).astype(BF)
+
+    scatter.total(dhs, out_rows)
     last = local(outs, out_out, l_sem.at[3])
     last.start()
     scatter.finish()

time: 362 us -> 360 us (level)
  no operation moved by 1% of the time
where the time goes in v8:
time: 360 us
  Pallas kernels  359 us (100%)
    pallas_call x1, Pallas kernels, forward_kernel(): pl.pallas_call(functools.partial(forward_body, dp), in_specs=[ANY, ANY, V...  142 us
    pallas_call x1, Pallas kernels, mlp_kernel(): pl.pallas_call(mlp_body, in_specs=[ANY] * 7 + [pl.BlockSpec(memory_space=...  74.5 us
    pallas_call x1, Pallas kernels, attention_back_kernel(): pl.pallas_call(functools.partial(attention_back_body, dp), in_specs=[ANY]...  72 us
    pallas_call x1, Pallas kernels, input_back_kernel(): pl.pallas_call(functools.partial(input_back_body, dp), in_specs=[ANY] * 8...  66.3 us

profile of v8, /device:TPU:0, one launch (start us, length us, event | category | flops | bytes accessed | tf_op | source)
XLA Modules:
  0.0 360.0 jit_solution(6243897696330901686)
XLA Ops:
  1.3 141.5 %forward_gather.1 = (bf16[4,256,1536]{2,1,0:T(8,128)(2,1)}, bf16[1024,384]{1,0:T(8,128)(2,1)}, bf16[1024,384]{1,0:T(8,128)(2,1)}, bf16[1024,384]{1,0:T(8,128)(2,...) custom-call(bf16[256,1536]{1,0:T(8,128)(2,1)} %tok.3, ...), custom_call_target="tpu_custom_call" | custom-call | tf_op jit(solution)/shard_map/forward_gather/pallas_call | solution.py:502
  142.8 74.5 %mlp_scatter.1 = (bf16[3,8,192,1536]{3,2,1,0:T(8,128)(2,1)}, bf16[4,256,1536]{2,1,0:T(8,128)(2,1)}, f32[256,1536]{1,0:T(8,128)}, f32[1,1536]{1,0:T(1,128)}) custom-call(bf16[1024,1536]{1,0:T(8,128)(2,1)} %bitcast.9, bf16[4,256,1536]{2,1,0:T(8,128)(2,1)} %get-tuple-element.48.dy, bf16[1536,1536]{1,0:T(8,128)(2,1)} %wg.1, bf16[1536,1536]{1,0:T(8,128)(2,1)} %wu.1, ...), custom_call_target="tpu_custom_call" | custom-call | tf_op jit(solution)/shard_map/mlp_scatter/pallas_call | solution.py:753
  217.4 72.0 %attention_back.1 = (bf16[256,1536]{1,0:T(8,128)(2,1)}, bf16[1024,384]{1,0:T(8,128)(2,1)}, bf16[1024,384]{1,0:T(8,128)(2,1)}, bf16[1024,384]{1,0:T(8,128)(2,1)},...) custom-call(f32[256,1536]{1,0:T(8,128)} %get-tuple-element.51.dh, bf16[4,384,1536]{2,1,0:T(8,128)(2,1)} %bitcast.8, ...), custom_call_target="tpu_custom_call" | custom-call | tf_op jit(solution)/shard_map/attention_back/pallas_call | solution.py:912
  289.4 66.3 %input_back.1 = (bf16[256,1536]{1,0:T(8,128)(2,1)}, f32[2,1536]{1,0:T(2,128)}, f32[192,1152]{1,0:T(8,128)}, f32[192,384]{1,0:T(8,128)}) custom-call(bf16[1024,384]{1,0:T(8,128)(2,1)} %get-tuple-element.60.dq, bf16[1024,384]{1,0:T(8,128)(2,1)} %get-tuple-element.61.dk, bf16[1024,384]{1,0:T(8,128)(2,1)} %get-tuple-element.62.dv, bf16[1024,1536]{1,0:T(8,128)(2,1)} %bitcast.10, ...), custom_call_target="tpu_custom_call" | custom-call | tf_op jit(solution)/shard_map/input_back/pallas_call | solution.py:1074
  355.7 4.1 %finish.1 = (bf16[256,1536]{1,0:T(8,128)(2,1)}, bf16[256,1536]{1,0:T(8,128)(2,1)}, f32[1536]{0:T(1024)}, f32[1536]{0:T(1024)}, f32[192,384]{1,0:T(8,128)}, /*ind...) custom-call(bf16[256,1536]{1,0:T(8,128)(2,1)} %get-tuple-element.59., ...), custom_call_target="tpu_custom_call" | custom-call | tf_op jit(solution)/shard_map/finish/pallas_call | solution.py:1145
